TPU v7x, 32 devices: a whole 2x2x4 slice. The times are simulated.
32 devices in a mesh: dp: 8 (over z, x), fsdp: 4 (over y, core).
Axes of the slice: x: 2, y: 2, z: 4, core: 2. Of those that a mesh axis runs over, the one named last changes fastest.
Arguments:
- tokens: float32 [16, 1024, 512], P('dp', 'fsdp'), may hold values from -12 to 12
- segments: int32 [16, 1024], P('dp', 'fsdp'), may hold values from 0 to 15, never falling along the last dimension, each value on 1 to 512 neighbouring positions
- cotangent: float32 [16, 1024, 512], P('dp', 'fsdp'), may hold values from -6 to 6
- ln1_gain: float32 [512], P('dp'), may hold values from 0.5 to 1.5
- ln1_bias: float32 [512], P('dp'), may hold values from -2.5 to 2.5
- w_qkv: float32 [512, 1536], P('fsdp', 'dp'), may hold values from -0.25 to 0.25
- w_out: float32 [512, 512], P('fsdp', 'dp'), may hold values from -1.5 to 1.5
- ln2_gain: float32 [512], P('dp'), may hold values from 0.5 to 1.5
- ln2_bias: float32 [512], P('dp'), may hold values from -2.5 to 2.5
- w_up: float32 [512, 2048], P('fsdp', 'dp'), may hold values from -0.25 to 0.25
- w_down: float32 [2048, 512], P('fsdp', 'dp'), may hold values from -0.125 to 0.125
Outputs:
- output: float32 [16, 1024, 512], P('dp', 'fsdp')
- grad_tokens: float32 [16, 1024, 512], P('dp', 'fsdp')
- grad_ln1_gain: float32 [512], P('dp')
- grad_ln1_bias: float32 [512], P('dp')
- grad_w_qkv: float32 [512, 1536], P('fsdp', 'dp')
- grad_w_out: float32 [512, 512], P('fsdp', 'dp')
- grad_ln2_gain: float32 [512], P('dp')
- grad_ln2_bias: float32 [512], P('dp')
- grad_w_up: float32 [512, 2048], P('fsdp', 'dp')
- grad_w_down: float32 [2048, 512], P('fsdp', 'dp')
Inputs may be any that keep to these rules, and one draw needn't show every extreme that they name: `segments`: in each sequence the numbers never fall; each document runs for 1 to 512 tokens, and one runs for exactly 512.
All inputs are finite; a program needn't handle non-finite values.
Results may differ from a plain program's by a relative error of at most 0.0003.
Values sent between devices are 32-bit elements; how exact they have to be, the bound alone decides.
No kernel may reach another device: no remote copies, remote signals or barrier semaphores. Data moves between devices by JAX's collectives and lax.ppermute only.
A program may use at most 256 MiB of HBM per device.

v0:
```python
import jax
import jax.numpy as jnp
import numpy as np
from jax import lax
from jax.experimental import pallas as pl
from jax.experimental.pallas import tpu as pltpu
from jax.sharding import PartitionSpec as P

HEADS = 8
NR = 16
LEVELS = 6
EPSILON = 1e-05
MASKED = -1e30
F32 = jnp.float32
BF16 = jnp.bfloat16
LN_ROWS = 16
TILE = 128
SCALE = 0.05


def split(x):
    high = x.astype(BF16)
    return high, (x - high.astype(F32)).astype(BF16)


def mm(a, b, ca, cb):
    return lax.dot_general(a, b, (((ca,), (cb,)), ((), ())), preferred_element_type=F32)


def mm3(a, b, ca, cb):
    return mm(a[0], b[0], ca, cb) + mm(a[0], b[1], ca, cb) + mm(a[1], b[0], ca, cb)


def mm2(a, b, ca, cb):
    return mm(a, b[0], ca, cb) + mm(a, b[1], ca, cb)


def level_layout(length):
    rows, start = [], 0
    for level in range(1, LEVELS):
        count = length >> level
        rows.append((level, start, count))
        start += count
    return rows, start


def pooling(length):
    spread = np.zeros((length, length), np.float32)
    pool = np.zeros((length, length), np.float32)
    same = np.zeros((length, length), np.float32)
    layout, _ = level_layout(length)
    bounds = [first for _, first, _ in layout] + [length]
    for index, (level, first, count) in enumerate(layout):
        token = np.arange(length)
        spread[token, first + (token >> level)] = 1.0
        pool[first + (token >> level), token] = 0.5**level
        same[bounds[index] : bounds[index + 1], bounds[index] : bounds[index + 1]] = 1.0
    return spread, pool, same


def score_bias(seg, near, far_a, far_b):
    count, length = seg.shape
    token = np.arange(length)
    near_pair = (token[:TILE, None] >> 5) == (token[None, :TILE] >> 5)
    tiles = seg.reshape(count, length // TILE, TILE)
    ok = near_pair & (tiles[:, :, :, None] == tiles[:, :, None, :])
    inner = jnp.where(ok, 0.0, MASKED).astype(F32).reshape(count, length, TILE)
    parts = []
    for level in range(1, LEVELS):
        ratio = 1 << level

        def ends(values):
            grouped = values.reshape(count, length // ratio, ratio)
            return grouped[:, :, 0], grouped[:, :, -1]

        low_q, high_q = ends(seg)
        low_q = jnp.repeat(low_q, ratio, axis=1)
        high_q = jnp.repeat(high_q, ratio, axis=1)
        if 2 * NR * ratio <= length:
            low_k, high_k = ends(seg)
            block_q = (token >> level) >> 4
            block_k = np.arange(length >> level) >> 4
            where = (block_q[:, None] ^ 1) == block_k[None, :]
        else:
            if NR * ratio <= length:
                low_k, high_k = ends(near)
            else:
                pieces = [ends(far_a), ends(far_b)]
                low_k = jnp.concatenate([pieces[0][0], pieces[1][0]], axis=1)
                high_k = jnp.concatenate([pieces[0][1], pieces[1][1]], axis=1)
            where = np.ones((length, low_k.shape[1]), bool)
        ok = (
            where[None]
            & (low_q[:, :, None] <= high_k[:, None, :])
            & (low_k[:, None, :] <= high_q[:, :, None])
        )
        parts.append(jnp.where(ok, np.float32(level * np.log(2.0)), MASKED))
    return inner, jnp.concatenate(parts, axis=2).astype(F32)


class Plan:
    def __init__(self, dp, fsdp):
        self.dp, self.fsdp = dp, fsdp
        self.dims = {}
        names = ["x", "z", "w"]
        bit = 1
        while bit < dp:
            name = names[len(self.dims)] if len(self.dims) < 3 else "d%d" % bit
            self.dims[name] = ("dp", bit)
            bit *= 2
        self.extra = list(self.dims)[3:]
        self.dims["y"] = ("fsdp", 2)
        self.dims["c"] = ("fsdp", 1)

    def corner(self, group, v):
        return tuple(name for i, name in enumerate(group) if (v >> i) & 1)

    def mask(self, names):
        d = f = 0
        for name in names:
            axis, bit = self.dims[name]
            if axis == "dp":
                d |= bit
            else:
                f |= bit
        return d, f

    def send(self, x, names):
        d, f = self.mask(names)
        if not f:
            return lax.ppermute(x, "dp", [(i, i ^ d) for i in range(self.dp)])
        if not d:
            return lax.ppermute(x, "fsdp", [(i, i ^ f) for i in range(self.fsdp)])
        n = self.fsdp
        pairs = [(i, ((i // n) ^ d) * n + ((i % n) ^ f)) for i in range(self.dp * n)]
        return lax.ppermute(x, ("dp", "fsdp"), pairs)

    def position(self, stages, d, f):
        pos = 0
        for group in stages:
            for name in reversed(group):
                axis, bit = self.dims[name]
                value = d if axis == "dp" else f
                pos = pos * 2 + ((value // bit) & 1)
        return pos


class Part:
    def __init__(self, start, held, names):
        self.start, self.held, self.names, self.got = start, held, names, []


class Gather:
    def __init__(self, plan, piece):
        self.plan, self.parts = plan, [Part(0, piece[None], [()])]
        self.arrays, self.slots = [], []

    def cut(self, row):
        (part,) = self.parts
        self.parts = [
            Part(0, part.held[:, :row], part.names),
            Part(row, part.held[:, row:], part.names),
        ]

    def send(self, groups, *earlier):
        for part, group in zip(self.parts, groups):
            if earlier:
                part.held = after(part.held, *earlier)
            for v in range(1, 1 << len(group)):
                names = self.plan.corner(group, v)
                part.got.append((self.plan.send(part.held, names), names))

    def came(self):
        return [value for part in self.parts for value, _ in part.got]

    def join(self):
        for part in self.parts:
            names = list(part.names)
            for _, corner in part.got:
                names += [n + corner for n in part.names]
            part.held = jnp.concatenate([part.held] + [v for v, _ in part.got], axis=0)
            part.names, part.got = names, []

    def stage(self, groups, *earlier):
        self.join()
        self.send(groups, *earlier)

    def share(self, held, *earlier):
        sent = []
        for part in self.parts:
            for value, corner in [(part.held, ())] if held else part.got:
                if earlier:
                    value = after(value, *earlier)
                other = self.plan.send(value, ("c",))
                sent.append(other)
                for array, core in ((value, ()), (other, ("c",))):
                    self.arrays.append(array)
                    slots = [self.plan.mask(n + corner + core) for n in part.names]
                    self.slots.append((slots, part.start))
        return sent


def assemble(scratch, refs, gathered, me_d, me_f, rows, lanes, segments):
    for ref, (slots, start) in zip(refs, gathered.slots):
        for slot, (d, f) in enumerate(slots):
            row0 = (me_d ^ d) * rows
            col0 = (me_f ^ f) * lanes
            for source, size, to_lane in segments:
                low, high = max(source, start), min(source + size, start + ref.shape[1])
                if low < high:
                    row = pl.multiple_of(row0 + (low - source), 8)
                    col = pl.multiple_of(col0 + to_lane, 128)
                    scratch[pl.ds(row, high - low), pl.ds(col, 128)] = ref[
                        slot, low - start : high - start, :
                    ]


def norm_rows(refs, gathered):
    total = None
    for ref, (slots, start) in zip(refs, gathered.slots):
        for slot, (d, f) in enumerate(slots):
            if f == 0 and start == 0:
                value = ref[slot, :LN_ROWS, :]
                total = value if total is None else total + value
    return jnp.concatenate([total[4 * i : 4 * i + 4] for i in range(4)], axis=1)


class Stream:
    def __init__(self, plan, rows, stages):
        self.plan, self.rows, self.stages = plan, rows, stages
        self.slots = plan.dp * plan.fsdp // 2

    def shape(self):
        return (self.slots, self.rows, 128)

    def put(self, out, d, f, row, value):
        size = value.shape[0]
        out[self.plan.position(self.stages, d, f), row : row + size, :] = value


class Reduce:
    def __init__(self, plan, stages):
        self.plan, self.stages = plan, list(stages)
        self.kept, self.came, self.last = [], [], []

    def begin(self, part, *earlier):
        part = after(part, *earlier) if earlier else part
        self.last = [self.plan.send(part, ("c",))]
        self.came.append(self.last[0])
        return self.last

    def keep(self, part):
        self.kept.append(part)

    def send(self, *earlier, rider=None):
        if self.kept:
            self.terms = [self.kept, self.came]
            self.slots, self.kept = self.kept[0].shape[0], []
        if earlier:
            self.terms[-1] = after(self.terms[-1], *earlier)
        group = self.stages.pop(0)
        self.slots >>= len(group)
        n = self.slots
        count = range(len(self.terms[0]))
        sizes = [part.shape[1] for part in self.terms[0]]
        cuts = np.cumsum([0] + sizes)
        out = []
        for v in range(1, 1 << len(group)):
            parts = [sum(term[i][v * n : (v + 1) * n] for term in self.terms) for i in count]
            if rider is not None:
                parts.append(jnp.broadcast_to(rider[None], (n,) + rider.shape))
            out.append(parts[0] if len(parts) == 1 else jnp.concatenate(parts, axis=1))
        self.last, self.rode = [], rider
        for v, value in enumerate(out):
            got = self.plan.send(value, self.plan.corner(group, v + 1))
            self.last.append(got)
            self.terms.append([got[:, a:b] for a, b in zip(cuts[:-1], cuts[1:])])
            if rider is not None:
                self.rode = self.rode + got[0, cuts[-1] :]
        return out

    def total(self, *earlier):
        count = range(len(self.terms[0]))
        return [sum(term[i][0] for term in self.terms) for i in count]


def after(value, *earlier):
    return lax.optimization_barrier((value, earlier))[0]


def whole(shape=None):
    return pl.BlockSpec(memory_space=pltpu.VMEM)


SMEM = pl.BlockSpec(memory_space=pltpu.SMEM)


def cost(micros):
    return pl.CostEstimate(
        flops=int(micros * SCALE * 9e8), bytes_accessed=int(micros * SCALE * 2.5e6), transcendentals=0
    )


def call(body, outs, scratch=(), **kw):
    return pl.pallas_call(
        body,
        out_shape=[jax.ShapeDtypeStruct(s, t) for s, t in outs],
        scratch_shapes=list(scratch),
        **kw,
    )


def qkv_stage(me, tokens, gathered, plan, pool, seqs):
    rows_all, width = tokens.shape
    length = rows_all // seqs
    n4, n5 = length >> 4, length >> 5
    slots = gathered.arrays
    triple = 3 * width
    rows = triple // plan.dp
    lanes = width // plan.fsdp

    def body(me_ref, tok, pool_ref, *rest):
        refs = rest[: len(slots)]
        packed, wh, wl, xhat, inv, ln, s4, s5, full, nh, nl = rest[len(slots) :]
        step = pl.program_id(0)

        @pl.when(step == 0)
        def _():
            assemble(full, refs, gathered, me_ref[0], me_ref[1], rows, lanes, [(LN_ROWS, rows, 0)])
            params = norm_rows(refs, gathered)
            ln[0:4, :] = params
            x = tok[...]
            centre = x - jnp.mean(x, axis=1, keepdims=True)
            scale = lax.rsqrt(jnp.mean(centre * centre, axis=1, keepdims=True) + EPSILON)
            xh = centre * scale
            xhat[...] = xh
            inv[...] = jnp.broadcast_to(scale, inv.shape)
            n = split(xh * params[0:1, :] + params[1:2, :])
            nh[...] = n[0]
            nl[...] = n[1]

        w = split(full[pl.ds(pl.multiple_of(step * width, width), width), :])
        wh[...] = w[0]
        wl[...] = w[1]
        packed[...] = mm3((nh[...], nl[...]), w, 1, 1)

        @pl.when(step > 0)
        def _():
            for s in range(seqs):
                means = mm2(pool_ref[...], split(packed[s * length : (s + 1) * length, :]), 1, 0)
                s4[s, 0] = means[:n4]
                s5[s, 0] = means[n4 : n4 + n5]

    fixed = lambda shape: pl.BlockSpec(shape, lambda i: (0,) * len(shape))
    later = lambda n: pl.BlockSpec((seqs, 1, n, width), lambda i: (0, jnp.maximum(i - 1, 0), 0, 0))
    outs = [
        ((rows_all, triple), F32, pl.BlockSpec((rows_all, width), lambda i: (0, i))),
        ((triple, width), BF16, pl.BlockSpec((width, width), lambda i: (i, 0))),
        ((triple, width), BF16, pl.BlockSpec((width, width), lambda i: (i, 0))),
        ((rows_all, width), F32, fixed((rows_all, width))),
        ((rows_all, 128), F32, fixed((rows_all, 128))),
        ((8, width), F32, fixed((8, width))),
        ((seqs, 2, n4, width), F32, later(n4)),
        ((seqs, 2, n5, width), F32, later(n5)),
    ]
    return pl.pallas_call(
        body,
        cost_estimate=cost(7.4),
        grid=(3,),
        out_shape=[jax.ShapeDtypeStruct(shape, kind) for shape, kind, _ in outs],
        in_specs=[SMEM, fixed((rows_all, width)), fixed(pool.shape)]
        + [fixed(x.shape) for x in slots],
        out_specs=[spec for _, _, spec in outs],
        scratch_shapes=[
            pltpu.VMEM((triple, width), F32),
            pltpu.VMEM((rows_all, width), BF16),
            pltpu.VMEM((rows_all, width), BF16),
        ],
    )(me, tokens, pool, *slots)


def lanes2(pair):
    return jnp.concatenate(pair, axis=1)


def fold(r):
    return r[:, :128] + r[:, 128:]


def wide_nt(a, b):
    first = mm(lanes2(a), lanes2((b[0], b[0])), 1, 1)
    return first + mm(a[0], b[1], 1, 1)


def wide_nn(a, b):
    return fold(mm(a[0], lanes2(b), 1, 0)) + mm(a[1], b[0], 1, 0)


def wide_tn(a, b):
    return fold(mm(a[0], lanes2(b), 0, 0)) + mm(a[1], b[0], 0, 0)


def tile_tn(a, b):
    left = jnp.concatenate(a, axis=0)
    right = jnp.concatenate([lanes2(b), lanes2((b[0], jnp.zeros_like(b[0])))], axis=0)
    return fold(mm(left, right, 0, 0))


def rows(pair, t):
    return tuple(x[t * TILE : (t + 1) * TILE] for x in pair)


class Heads:
    def __init__(self, q, k, v, fk, fv, pool, local):
        length = q.shape[0]
        self.tiles = range(length // TILE)
        self.lane = lax.broadcasted_iota(jnp.int32, (length, 128), 1) < 64
        qs, ks, vs = split(q), split(k), split(v)
        pooled = mm(pool, jnp.concatenate([qs[0], ks[0], vs[0], qs[1], ks[1], vs[1]], axis=1), 1, 0)
        pooled = pooled[:, :384] + pooled[:, 384:]
        kc = jnp.concatenate([pooled[:local, 128:256], fk], axis=0)
        vc = jnp.concatenate([pooled[:local, 256:], fv], axis=0)
        self.q, self.qc = qs, split(pooled[:, :128])
        self.k2 = [self.two(rows(ks, t)) for t in self.tiles]
        self.v2 = [self.two(rows(vs, t)) for t in self.tiles]
        self.kc2, self.vc2 = self.two(split(kc)), self.two(split(vc))

    def two(self, pair):
        out = []
        for x in pair:
            lane = self.lane[: x.shape[0]]
            zero = jnp.zeros_like(x)
            both = [jnp.where(lane, x, zero), jnp.where(lane, zero, x)]
            out.append(jnp.concatenate(both, axis=0))
        return tuple(out)

    def one(self, x):
        half = x.shape[0] // 2
        return jnp.where(self.lane[:half], x[:half], x[half:])

    def inner(self, left, right):
        return jnp.concatenate([wide_nt(rows(left, t), right[t]) for t in self.tiles], axis=0)

    def scores(self, spread, same, inner_bias, outer_bias):
        s0 = self.inner(self.q, self.k2) + lanes2((inner_bias, inner_bias))
        high, low = split(wide_nt(self.qc, self.kc2) * lanes2((same, same)))
        st = mm(spread, high, 1, 0) + mm(spread, low, 1, 0)
        return s0, st + lanes2((outer_bias, outer_bias))


def head_columns(x):
    half = x.shape[1] // 2
    return x[:, :half], x[:, half:]


def attention_specs(length, width, first=0, pair=0):
    pairs = width // 128
    block = lambda off: pl.BlockSpec((length, 128), lambda s, h: (first + s, off * pairs + pair + h))
    far = lambda j: pl.BlockSpec((1, 1, 32, 128), lambda s, h: (first + s, j, 0, pair + h))
    fixed = pl.BlockSpec((length, length), lambda s, h: (0, 0))
    bias = lambda n: pl.BlockSpec((1, length, n), lambda s, h: (first + s, 0, 0))
    return block, far, fixed, [bias(TILE), bias(length), fixed, fixed, fixed]


def attention_forward(packed, far, bias, spread, pool, same, seqs, local, which, before):
    rows_all, triple = packed.shape
    width = triple // 3
    length = rows_all // seqs
    first, count, pair, pairs = which
    block, far_spec, fixed, common = attention_specs(length, width, first, pair)
    carried = len(before)

    def body(q, k, v, fk, fv, inner_bias, outer_bias, spread_ref, pool_ref, same_ref, *rest):
        out, lse = rest[carried:]
        heads = Heads(q[...] * 0.125, k[...], v[...], fk[0, 0], fv[0, 0], pool_ref[...], local)
        s0, st = heads.scores(spread_ref[...], same_ref[...], inner_bias[0], outer_bias[0])
        p0, pc, peaks, sums = [], [], [], []
        for a, b in zip(head_columns(s0), head_columns(st)):
            peak = jnp.maximum(jnp.max(a, axis=1, keepdims=True), jnp.max(b, axis=1, keepdims=True))
            a, b = jnp.exp(a - peak), jnp.exp(b - peak)
            p0.append(a)
            pc.append(b)
            peaks.append(peak)
            sums.append(jnp.sum(a, axis=1, keepdims=True) + jnp.sum(b, axis=1, keepdims=True))
        p0, pc = split(lanes2(p0)), split(lanes2(pc))
        mixed = [wide_nn(rows(p0, t), heads.v2[t]) for t in heads.tiles]
        mixed = jnp.concatenate(mixed, axis=0) + wide_nn(pc, heads.vc2)
        total = jnp.where(heads.lane, sums[0], sums[1])
        out[...] = mixed / total
        lse[...] = jnp.where(heads.lane, peaks[0], peaks[1]) + jnp.log(total)

    return pl.pallas_call(
        body,
        cost_estimate=cost(9.5),
        grid=(count, pairs),
        out_shape=[jax.ShapeDtypeStruct((rows_all, width), F32)] * 2,
        in_specs=[block(0), block(1), block(2), far_spec(0), far_spec(1)]
        + common
        + [pl.BlockSpec(memory_space=pl.ANY)] * carried,
        out_specs=[block(0), block(0)],
        input_output_aliases={10 + i: i for i in range(carried)},
    )(packed, packed, packed, far, far, *bias, spread, pool, same, *before)


def attention_backward(
    packed, far, bias, spread, pool, same, attended, lse, grad, seqs, local, which, before
):
    rows_all, triple = packed.shape
    width = triple // 3
    length = rows_all // seqs
    first, count, pair, pairs = which
    block, far_spec, fixed, common = attention_specs(length, width, first, pair)
    n4, n5 = length >> 4, length >> 5
    carried = len(before)

    def body(q, k, v, fk, fv, inner_bias, outer_bias, spread_ref, pool_ref, same_ref, *rest):
        o_ref, lse_ref, g_ref = rest[:3]
        dq_ref, dk_ref, dv_ref, f4, f5a, f5b = rest[3 + carried :]
        spread_m, pool_m, same_m = spread_ref[...], pool_ref[...], same_ref[...]
        heads = Heads(q[...] * 0.125, k[...], v[...], fk[0, 0], fv[0, 0], pool_m, local)
        lane = heads.lane
        s0, st = heads.scores(spread_m, same_m, inner_bias[0], outer_bias[0])
        logs = lse_ref[...]
        logs = (logs[:, 0:1], logs[:, 64:65])
        p0 = lanes2([jnp.exp(a - x) for a, x in zip(head_columns(s0), logs)])
        pc = lanes2([jnp.exp(a - x) for a, x in zip(head_columns(st), logs)])
        grad_rows = g_ref[...]
        g = split(grad_rows)
        product = grad_rows * o_ref[...]
        zero = jnp.zeros_like(product)
        deltas = [
            jnp.sum(jnp.where(lane, product, zero), axis=1, keepdims=True),
            jnp.sum(jnp.where(lane, zero, product), axis=1, keepdims=True),
        ]
        d0 = heads.inner(g, heads.v2)
        d0 = split(p0 * lanes2([a - x for a, x in zip(head_columns(d0), deltas)]))
        dt = wide_nt(g, heads.vc2)
        dt = split(pc * lanes2([a - x for a, x in zip(head_columns(dt), deltas)]))
        p0, pc = split(p0), split(pc)
        dv = [heads.one(tile_tn(rows(p0, t), rows(g, t))) for t in heads.tiles]
        dk = [heads.one(tile_tn(rows(d0, t), rows(heads.q, t))) for t in heads.tiles]
        dq = [wide_nn(rows(d0, t), heads.k2[t]) for t in heads.tiles]
        dvc = heads.one(wide_tn(pc, g))
        dsc = mm(spread_m, dt[0], 0, 0) + mm(spread_m, dt[1], 0, 0)
        dsc = split(dsc * lanes2((same_m, same_m)))
        dqc = wide_nn(dsc, heads.kc2)
        dkc = heads.one(wide_tn(dsc, heads.qc))
        near = lax.broadcasted_iota(jnp.int32, (length, 128), 0) < local
        high, low = split(
            jnp.concatenate([dqc, jnp.where(near, dkc, zero), jnp.where(near, dvc, zero)], axis=1)
        )
        back = mm(pool_m, lanes2((high, low)), 0, 0)
        back = back[:, :384] + back[:, 384:]
        dq_ref[...] = (jnp.concatenate(dq, axis=0) + back[:, :128]) * 0.125
        dk_ref[...] = jnp.concatenate(dk, axis=0) + back[:, 128:256]
        dv_ref[...] = jnp.concatenate(dv, axis=0) + back[:, 256:]
        for j, value in ((0, dkc), (1, dvc)):
            f4[0, j] = value[local : local + n4]
            f5a[0, j] = value[local + n4 : local + n4 + n5]
            f5b[0, j] = value[local + n4 + n5 :]

    far_out = lambda n: pl.BlockSpec((1, 2, n, 128), lambda s, h: (first + s, 0, 0, pair + h))
    return pl.pallas_call(
        body,
        cost_estimate=cost(8),
        grid=(count, pairs),
        out_shape=[jax.ShapeDtypeStruct((rows_all, width), F32)] * 3
        + [jax.ShapeDtypeStruct((seqs, 2, n, width), F32) for n in (n4, n5, n5)],
        in_specs=[block(0), block(1), block(2), far_spec(0), far_spec(1)]
        + common
        + [block(0)] * 3
        + [pl.BlockSpec(memory_space=pl.ANY)] * carried,
        out_specs=[block(0)] * 3 + [far_out(n4), far_out(n5), far_out(n5)],
        input_output_aliases={13 + i: i for i in range(carried)},
    )(packed, packed, packed, far, far, *bias, spread, pool, same, attended, lse, grad, *before)


def middle_stage(tokens, attended, wh, wl):
    rows_all, width = tokens.shape

    def body(tok, att, wh_ref, wl_ref, middle, xhat, inv):
        x = tok[...] + mm3(split(att[...]), (wh_ref[...], wl_ref[...]), 1, 1)
        middle[...] = x
        centre = x - jnp.mean(x, axis=1, keepdims=True)
        scale = lax.rsqrt(jnp.mean(centre * centre, axis=1, keepdims=True) + EPSILON)
        xhat[...] = centre * scale
        inv[...] = jnp.broadcast_to(scale, inv.shape)

    return call(
        body,
        [((rows_all, width), F32), ((rows_all, width), F32), ((rows_all, 128), F32)],
        cost_estimate=cost(4.3),
        in_specs=[whole()] * 4,
        out_specs=[whole()] * 3,
    )(tokens, attended, wh, wl)


def projection_stage(me, gathered, plan, width, hidden_width):
    rows, lanes = width // plan.dp, hidden_width // plan.fsdp
    out_lanes = width // plan.fsdp
    slots = gathered.arrays
    chunks = lanes // 128
    down_parts = [(k * rows, rows, 128 * k) for k in range(chunks)]
    out_parts = [(chunks * rows, rows, 0)]
    chunk = 512

    def body(me_ref, *rest):
        refs = rest[: len(slots)]
        dh, dl, oh, ol, full, full_out = rest[len(slots) :]
        me_d, me_f = me_ref[0], me_ref[1]
        step = pl.program_id(0)

        @pl.when(step == 0)
        def _():
            assemble(full_out, refs, gathered, me_d, me_f, rows, out_lanes, out_parts)
            w = split(full_out[...])
            oh[...] = w[0]
            ol[...] = w[1]
            assemble(full, refs, gathered, me_d, me_f, rows, lanes, down_parts)

        w = split(full[:, pl.ds(pl.multiple_of(step * chunk, chunk), chunk)])
        dh[...] = w[0]
        dl[...] = w[1]

    fixed = lambda shape: pl.BlockSpec(shape, lambda i: (0,) * len(shape))
    cols = pl.BlockSpec((width, chunk), lambda i: (0, i))
    return pl.pallas_call(
        body,
        cost_estimate=cost(5),
        grid=(hidden_width // chunk,),
        out_shape=[jax.ShapeDtypeStruct((width, hidden_width), BF16)] * 2
        + [jax.ShapeDtypeStruct((width, width), BF16)] * 2,
        in_specs=[SMEM] + [fixed(x.shape) for x in slots],
        out_specs=[cols, cols, fixed((width, width)), fixed((width, width))],
        scratch_shapes=[pltpu.VMEM((width, hidden_width), F32), pltpu.VMEM((width, width), F32)],
    )(me, *slots)


def hidden_stage(me, xhat, ln, cot, dh, dl, gathered, plan):
    rows_all, width = xhat.shape
    hidden_width = dh.shape[1]
    rows, lanes = hidden_width // plan.dp, width // plan.fsdp
    slots = gathered.arrays
    chunk = 512
    steps = hidden_width // chunk
    root = float(np.sqrt(2.0 / np.pi))
    cubic = 0.044715 * root

    def body(me_ref, xhat_ref, ln_ref, cot_ref, d0, d1, *rest):
        refs = rest[: len(slots)]
        hh, hl, ph, plo, wh, wl, full, nh, nl, ch, cl = rest[len(slots) :]
        step = pl.program_id(0)

        @pl.when(step == 0)
        def _():
            assemble(full, refs, gathered, me_ref[0], me_ref[1], rows, lanes, [(0, rows, 0)])
            n = split(xhat_ref[...] * ln_ref[2:3, :] + ln_ref[3:4, :])
            nh[...] = n[0]
            nl[...] = n[1]
            c = split(cot_ref[...])
            ch[...] = c[0]
            cl[...] = c[1]

        w = split(full[pl.ds(pl.multiple_of(step * chunk, chunk), chunk), :])
        wh[...] = w[0]
        wl[...] = w[1]
        v = mm3((nh[...], nl[...]), w, 1, 1)
        square = v * v
        half = 0.5 + 0.5 * jnp.tanh(v * (root + cubic * square))
        h = split(v * half)
        hh[...] = h[0]
        hl[...] = h[1]
        slope = half + (half - half * half) * (v * (2.0 * root + 6.0 * cubic * square))
        g = split(mm3((ch[...], cl[...]), (d0[...], d1[...]), 1, 0) * slope)
        ph[...] = g[0]
        plo[...] = g[1]

    fixed = lambda shape: pl.BlockSpec(shape, lambda i: (0,) * len(shape))
    cols = pl.BlockSpec((rows_all, chunk), lambda i: (0, i))
    down = pl.BlockSpec((width, chunk), lambda i: (0, i))
    act = fixed((rows_all, width))
    return pl.pallas_call(
        body,
        cost_estimate=cost(15),
        grid=(steps,),
        out_shape=[jax.ShapeDtypeStruct((rows_all, hidden_width), BF16)] * 4
        + [jax.ShapeDtypeStruct((hidden_width, width), BF16)] * 2,
        in_specs=[SMEM, act, fixed((8, width)), act, down, down]
        + [fixed(x.shape) for x in slots],
        out_specs=[cols] * 4 + [pl.BlockSpec((chunk, width), lambda i: (i, 0))] * 2,
        scratch_shapes=[pltpu.VMEM((hidden_width, width), F32)]
        + [pltpu.VMEM((rows_all, width), BF16)] * 4,
    )(me, xhat, ln, cot, dh, dl, *slots)


def grad_down_stage(me, cot, hh, hl, plan, stream, core):
    rows_all, width = cot.shape
    hidden_width = hh.shape[1]
    rows, lanes = width // plan.dp, hidden_width // plan.fsdp

    def body(me_ref, cot_ref, hh_ref, hl_ref, out):
        jf = core + 2 * pl.program_id(0)
        res = mm3(split(cot_ref[...]), (hh_ref[...], hl_ref[...]), 0, 0)
        for d in range(plan.dp):
            jd = me_ref[0] ^ d
            for k in range(lanes // 128):
                value = res[d * rows : (d + 1) * rows, 128 * k : 128 * (k + 1)]
                stream.put(out, jd, jf, k * rows, value)

    cols = pl.BlockSpec((rows_all, lanes), lambda i, m: (0, m[1] ^ (core + 2 * i)))
    grid_spec = pltpu.PrefetchScalarGridSpec(
        num_scalar_prefetch=1,
        grid=(plan.fsdp // 2,),
        in_specs=[pl.BlockSpec((rows_all, width), lambda i, m: (0, 0)), cols, cols],
        out_specs=pl.BlockSpec(stream.shape(), lambda i, m: (0, 0, 0)),
    )
    return pl.pallas_call(
        body,
        cost_estimate=cost(5.5),
        grid_spec=grid_spec,
        out_shape=jax.ShapeDtypeStruct(stream.shape(), F32),
    )(me, cot, hh, hl)


def half_lanes(ref, me_f, core, lanes):
    parts = []
    for y in range(2):
        start = pl.multiple_of((me_f ^ (core + 2 * y)) * lanes, 128)
        parts.append(ref[:, pl.ds(start, lanes)])
    return jnp.concatenate(parts, axis=1)


def grad_up_stage(me, xhat, ln, ph, plo, plan, stream, core):
    rows_all, width = xhat.shape
    hidden_width = ph.shape[1]
    rows, lanes = hidden_width // plan.dp, width // plan.fsdp
    chunk = 512
    steps = hidden_width // chunk
    per = chunk // rows

    def body(me_ref, xhat_ref, ln_ref, ph_ref, pl_ref, out, full, nh, nl):
        step = pl.program_id(0)

        @pl.when(step == 0)
        def _():
            full[...] = xhat_ref[...] * ln_ref[2:3, :] + ln_ref[3:4, :]
            n = split(half_lanes(full, me_ref[1], core, lanes))
            nh[...] = n[0]
            nl[...] = n[1]

        res = mm3((ph_ref[...], pl_ref[...]), (nh[...], nl[...]), 0, 0)
        for i in range(per):
            jd = (step * per + i) ^ me_ref[0]
            for y in range(2):
                value = res[i * rows : (i + 1) * rows, y * lanes : (y + 1) * lanes]
                stream.put(out, jd, core + 2 * y, 0, value)

    fixed = lambda shape: pl.BlockSpec(shape, lambda i: (0,) * len(shape))
    cols = pl.BlockSpec((rows_all, chunk), lambda i: (0, i))
    return pl.pallas_call(
        body,
        cost_estimate=cost(6.4),
        grid=(steps,),
        out_shape=jax.ShapeDtypeStruct(stream.shape(), F32),
        in_specs=[SMEM, fixed((rows_all, width)), fixed((8, width)), cols, cols],
        out_specs=fixed(stream.shape()),
        scratch_shapes=[pltpu.VMEM((rows_all, width), F32)]
        + [pltpu.VMEM((rows_all, 2 * lanes), BF16)] * 2,
    )(me, xhat, ln, ph, plo)


def norm_back(e, gain, xhat, inv):
    u = e * gain
    mean_u = jnp.mean(u, axis=1, keepdims=True)
    mean_ux = jnp.mean(u * xhat, axis=1, keepdims=True)
    return inv * (u - mean_u - xhat * mean_ux)


def output_stage(middle, hh, hl, dh, dl):
    rows_all, width = middle.shape
    chunk = 512
    steps = hh.shape[1] // chunk

    def body(mid, h0, h1, d0, d1, out):
        @pl.when(pl.program_id(0) == 0)
        def _():
            out[...] = mid[...]

        out[...] += mm3((h0[...], h1[...]), (d0[...], d1[...]), 1, 1)

    cols = pl.BlockSpec((rows_all, chunk), lambda i: (0, i))
    act = pl.BlockSpec((rows_all, width), lambda i: (0, 0))
    return pl.pallas_call(
        body,
        cost_estimate=cost(8),
        grid=(steps,),
        out_shape=jax.ShapeDtypeStruct((rows_all, width), F32),
        in_specs=[act, cols, cols] + [pl.BlockSpec((width, chunk), lambda i: (0, i))] * 2,
        out_specs=act,
    )(middle, hh, hl, dh, dl)


def middle_grad_stage(cot, xhat, inv, ln, ph, plo, uh, ul):
    rows_all, width = cot.shape
    chunk = 512
    steps = ph.shape[1] // chunk

    def body(cot_ref, xhat_ref, inv_ref, ln_ref, p0, p1, u0, u1, gm, gln, acc):
        step = pl.program_id(0)

        @pl.when(step == 0)
        def _():
            acc[...] = jnp.zeros_like(acc)

        acc[...] += mm3((p0[...], p1[...]), (u0[...], u1[...]), 1, 0)

        @pl.when(step == steps - 1)
        def _():
            e = acc[...]
            xh = xhat_ref[...]
            gm[...] = cot_ref[...] + norm_back(e, ln_ref[2:3, :], xh, inv_ref[:, 0:1])
            gln[0:1, :] = jnp.sum(e * xh, axis=0, keepdims=True)
            gln[1:2, :] = jnp.sum(e, axis=0, keepdims=True)

    fixed = lambda shape: pl.BlockSpec(shape, lambda i: (0,) * len(shape))
    cols = pl.BlockSpec((rows_all, chunk), lambda i: (0, i))
    act = fixed((rows_all, width))
    return pl.pallas_call(
        body,
        cost_estimate=cost(8.5),
        grid=(steps,),
        out_shape=[
            jax.ShapeDtypeStruct((rows_all, width), F32),
            jax.ShapeDtypeStruct((8, width), F32),
        ],
        in_specs=[act, act, fixed((rows_all, 128)), fixed((8, width)), cols, cols]
        + [pl.BlockSpec((chunk, width), lambda i: (i, 0))] * 2,
        out_specs=[act, fixed((8, width))],
        scratch_shapes=[pltpu.VMEM((rows_all, width), F32)],
    )(cot, xhat, inv, ln, ph, plo, uh, ul)


def mixture_grad_stage(me, gm, attended, oh, ol, plan, stream):
    rows_all, width = gm.shape
    rows, lanes = width // plan.dp, width // plan.fsdp

    def body(me_ref, gm_ref, att, oh_ref, ol_ref, gmix, away, keep, full):
        g = split(gm_ref[...])
        gmix[...] = mm3(g, (oh_ref[...], ol_ref[...]), 1, 0)
        full[...] = att[...]
        for core in range(2):
            res = mm3(g, split(half_lanes(full, me_ref[1], core, lanes)), 0, 0)
            mine = away if core else keep
            for d in range(plan.dp):
                for y in range(2):
                    value = res[d * rows : (d + 1) * rows, y * lanes : (y + 1) * lanes]
                    stream.put(mine, d ^ me_ref[0], core + 2 * y, 0, value)

    return call(
        body,
        [((rows_all, width), F32), (stream.shape(), F32), (stream.shape(), F32)],
        [pltpu.VMEM((rows_all, width), F32)],
        cost_estimate=cost(5),
        in_specs=[SMEM] + [whole()] * 4,
        out_specs=[whole()] * 3,
    )(me, gm, attended, oh, ol)


def packed_grad_stage(dq, dk, dv, g4, g5a, g5b, pool, seqs):
    rows_all, width = dq.shape
    length = rows_all // seqs

    def body(dq_r, dk_r, dv_r, g4_r, g5a_r, g5b_r, pool_r, gph, gpl, column):
        for j, ref in enumerate((dq_r, dk_r, dv_r)):
            total = None
            for s in range(seqs):
                rs = slice(s * length, (s + 1) * length)
                value = ref[rs, :]
                if j:
                    groups = jnp.concatenate(
                        [g4_r[s, j - 1], g5a_r[s, j - 1] + g5b_r[s, j - 1]], axis=0
                    )
                    value = value + mm2(pool_r[...], split(groups), 0, 0)
                part = jnp.sum(value, axis=0, keepdims=True)
                total = part if total is None else total + part
                h = split(value)
                gph[rs, j * width : (j + 1) * width] = h[0]
                gpl[rs, j * width : (j + 1) * width] = h[1]
            column[j * width : (j + 1) * width, :] = jnp.transpose(
                jnp.broadcast_to(total, (128, width))
            )

    return call(
        body,
        [((rows_all, 3 * width), BF16)] * 2 + [((3 * width, 128), F32)],
        cost_estimate=cost(4.5),
        in_specs=[whole()] * 7,
        out_specs=[whole()] * 3,
    )(dq, dk, dv, g4, g5a, g5b, pool)


def input_grad_stage(gph, gpl, wqh, wql, xhat, inv, ln, gm):
    rows_all, width = gm.shape

    def body(gph_r, gpl_r, wh, wl, xhat_r, inv_r, ln_r, gm_r, gtok):
        e = mm3((gph_r[...], gpl_r[...]), (wh[...], wl[...]), 1, 0)
        gtok[...] = gm_r[...] + norm_back(e, ln_r[0:1, :], xhat_r[...], inv_r[:, 0:1])

    return call(
        body,
        [((rows_all, width), F32)],
        cost_estimate=cost(7.4),
        in_specs=[whole()] * 8,
        out_specs=[whole()],
    )(gph, gpl, wqh, wql, xhat, inv, ln, gm)[0]


def grad_qkv_stage(me, gph, gpl, column, xhat, ln, wh, wl, plan, stream, core):
    rows_all, triple = gph.shape
    width = triple // 3
    rows, lanes = triple // plan.dp, width // plan.fsdp
    steps = 2
    block = triple // steps

    def body(me_ref, gph_r, gpl_r, col_r, xhat_r, ln_r, wh_r, wl_r, out, sums, nh, nl):
        me_f = me_ref[1]
        step = pl.program_id(0)
        pick = lambda ref: half_lanes(ref, me_f, core, lanes)

        @pl.when(step == 0)
        def _():
            n = split(pick(xhat_r))
            nh[...] = n[0]
            nl[...] = n[1]
            sums[...] = jnp.zeros_like(sums)

        params = pick(ln_r)
        res = mm3((gph_r[...], gpl_r[...]), (nh[...], nl[...]), 0, 0)
        w = pick(wh_r).astype(F32) + pick(wl_r).astype(F32)
        col = col_r[:, 0:1]
        parts = [jnp.sum(res * w, axis=0, keepdims=True), jnp.sum(w * col, axis=0, keepdims=True)]
        for y in range(2):
            at = pl.ds(pl.multiple_of((me_f ^ (core + 2 * y)) * lanes, 128), lanes)
            for i in range(2):
                sums[i : i + 1, at] += parts[i][:, y * lanes : (y + 1) * lanes]
        res = res * params[0:1, :] + col * params[1:2, :]
        for i in range(block // rows):
            jd = me_ref[0] ^ (step * (block // rows) + i)
            for y in range(2):
                value = res[i * rows : (i + 1) * rows, y * lanes : (y + 1) * lanes]
                stream.put(out, jd, core + 2 * y, 0, value)

    fixed = lambda shape: pl.BlockSpec(shape, lambda i: (0,) * len(shape))
    cols = pl.BlockSpec((rows_all, block), lambda i: (0, i))
    down = lambda n: pl.BlockSpec((block, n), lambda i: (i, 0))
    return pl.pallas_call(
        body,
        cost_estimate=cost(0.25),
        grid=(steps,),
        out_shape=[
            jax.ShapeDtypeStruct(stream.shape(), F32),
            jax.ShapeDtypeStruct((8, width), F32),
        ],
        in_specs=[SMEM, cols, cols, down(128), fixed((rows_all, width)), fixed((8, width))]
        + [down(width)] * 2,
        out_specs=[fixed(stream.shape()), fixed((8, width))],
        scratch_shapes=[pltpu.VMEM((rows_all, 2 * lanes), BF16)] * 2,
    )(me, gph, gpl, column, xhat, ln, wh, wl)


def swap(x, mask, axis="fsdp"):
    size = lax.axis_size(axis)
    return lax.ppermute(x, axis, [(i, i ^ mask) for i in range(size)])


def local(
    tokens, segments, cotangent, ln1_gain, ln1_bias, w_qkv, w_out, ln2_gain, ln2_bias, w_up, w_down
):
    seqs, length, width = tokens.shape
    dp, fsdp = lax.axis_size("dp"), lax.axis_size("fsdp")
    plan = Plan(dp, fsdp)
    me_d = lax.axis_index("dp")
    me = jnp.stack([me_d, lax.axis_index("fsdp")]).astype(jnp.int32)
    rows_all = seqs * length
    hidden_width = w_down.shape[0] * fsdp

    spread, pool, same = pooling(length)
    layout, _ = level_layout(length)
    local_rows = [first for level, first, _ in layout if 2 * NR * (1 << level) > length][0]
    spread_c = jnp.asarray(spread, BF16)
    pool_c = jnp.asarray(pool, BF16)
    same_c = jnp.asarray(same, F32)
    far_pool = jnp.asarray(pool[local_rows : local_rows + (length >> 4) + (length >> 5)], BF16)

    share = width // dp
    norms = jnp.stack([ln1_gain, ln1_bias, ln2_gain, ln2_bias])
    placed = lax.dynamic_update_slice(jnp.zeros((4, width), F32), norms, (0, me_d * share))
    placed = placed.reshape(4, 4, 128).transpose(1, 0, 2).reshape(LN_ROWS, 128)
    rows_qkv, rows_d, rows_up = 3 * share, share, hidden_width // dp
    chunks = hidden_width // fsdp // 128
    down_piece = w_down.T.reshape(rows_d, chunks, 128).transpose(1, 0, 2).reshape(-1, 128)
    down_piece = jnp.concatenate([down_piece, w_out.T], axis=0)
    extra = [(name,) for name in plan.extra]
    qkv_piece = jnp.concatenate([placed, w_qkv.T], axis=0)
    up_piece = w_up.T
    qkv_in, down_in, up_in = (Gather(plan, p) for p in (qkv_piece, down_piece, up_piece))
    tok = tokens.reshape(rows_all, width)
    cot = cotangent.reshape(rows_all, width)
    attend = (spread_c, pool_c, same_c)

    near = swap(segments, 1)
    qkv_in.send([("z", "w")])
    for group in extra:
        qkv_in.stage([group])
    gate = qkv_in.came()
    qkv_in.join()
    qkv_in.cut(LN_ROWS + rows_qkv // 16 * 8)
    qkv_in.send([("x",), ("y",)], gate)
    down_in.send([("w",)], gate)
    for group in extra:
        down_in.stage([group])
    far_segments = swap(jnp.stack([segments, after(near, gate)]), 2)
    bias = score_bias(segments, near, far_segments[0], far_segments[1])
    gate = (qkv_in.came(), down_in.came(), far_segments)
    qkv_in.stage([("y",), ("x",)], gate)
    down_in.stage([("z",)], gate)
    up_in.send([("w",)], gate)
    for group in extra:
        up_in.stage([group])
    gate = (qkv_in.came(), down_in.came(), up_in.came(), bias)
    cores = qkv_in.share(True, gate) + qkv_in.share(False, gate)
    down_in.join()
    down_in.cut(down_piece.shape[0] // 16 * 8)
    down_in.send([("x",), ("y",)], cores)
    up_in.stage([("z",)], cores)
    packed, wqh, wql, xhat1, inv1, ln, s4, s5 = qkv_stage(
        me, after(tok, cores, bias), qkv_in, plan, far_pool, seqs
    )
    gate = (packed, down_in.came(), up_in.came())
    s4, s5 = after((s4, s5), gate)
    got = [swap(s4, 1), swap(s5, 2), swap(s5, 3)]
    far = jnp.concatenate(got, axis=2)
    down_in.stage([("y",), ("x",)], gate)
    cores = down_in.share(True, far)
    calls = [(s, 1, 0, width // 128) for s in range(seqs)]
    before = ()
    gate = far
    for index, which in enumerate(calls):
        packed_in = after(packed, gate, before)
        before = attention_forward(packed_in, far, bias, *attend, seqs, local_rows, which, before)
        if index == 0:
            gate = (before, down_in.came(), cores)
            cores = down_in.share(False, gate)
            up_in.join()
            up_in.cut(rows_up // 2 // 8 * 8)
            up_in.send([("x",), ("y",)], gate)
    attended, lse = before
    gate = (attended, up_in.came(), cores)
    up_in.stage([("y",), ("x",)], gate)
    dh, dl, oh, ol = projection_stage(after(me, gate), down_in, plan, width, hidden_width)
    cores = up_in.share(True, gate)
    middle, xhat2, inv2 = middle_stage(tok, attended, oh, ol)
    gate = (middle, up_in.came(), cores)
    cores = up_in.share(False, gate)
    hh, hl, ph, plo, uh, ul = hidden_stage(
        me, after(xhat2, cores), ln, cot, dh, dl, up_in, plan
    )

    single = [("x", "y"), ("z",), ("w",)] + extra
    double = [("x", "y"), ("z", "w")] + extra
    down = Stream(plan, chunks * rows_d, single)
    up = Stream(plan, rows_up, single)
    out = Stream(plan, rows_d, single)
    qkv = Stream(plan, rows_qkv, double)
    down_sum, up_sum, qkv_sum = Reduce(plan, single), Reduce(plan, single), Reduce(plan, double)

    away = grad_down_stage(me, cot, hh, hl, plan, down, 1)
    down_core = down_sum.begin(away)
    away = grad_up_stage(me, after(xhat2, away), ln, ph, plo, plan, up, 1)
    up_core = up_sum.begin(away)
    keep = grad_down_stage(me, after(cot, away), hh, hl, plan, down, 0)
    down_sum.keep(keep)
    sent = down_sum.send(keep, down_core)
    keep = grad_up_stage(me, after(xhat2, sent), ln, ph, plo, plan, up, 0)
    up_sum.keep(keep)
    gm, gln = middle_grad_stage(after(cot, keep, up_core), xhat2, inv2, ln, ph, plo, uh, ul)
    gmix, away, keep = mixture_grad_stage(me, gm, attended, oh, ol, plan, out)
    got = up_sum.begin(away, down_sum.last)
    up_sum.keep(keep)
    sent = (down_sum.send(), up_sum.send(got))
    before = ()
    calls = [(s, 1, 0, width // 128) for s in range(seqs)]
    for index, which in enumerate(calls):
        grad = after(gmix, sent, before)
        before = attention_backward(
            packed, far, bias, *attend, attended, lse, grad, seqs, local_rows, which, before
        )
        if down_sum.stages:
            sent = down_sum.send(before, down_sum.last)
        else:
            sent = down_sum.last
    gate = (before, up_sum.last)
    dq, dk, dv, f4, f5a, f5b = before
    f4, f5a, f5b = after((f4, f5a, f5b), gate)
    g4, g5a, g5b = swap(f4, 1), swap(f5a, 2), swap(f5b, 3)
    gph, gpl, column = packed_grad_stage(dq, dk, dv, g4, g5a, g5b, far_pool, seqs)
    away, sums_away = grad_qkv_stage(
        me, gph, gpl, column, xhat1, ln, wqh, wql, plan, qkv, 1
    )
    got = qkv_sum.begin(away)
    keep, sums_keep = grad_qkv_stage(
        me, gph, gpl, column, after(xhat1, away), ln, wqh, wql, plan, qkv, 0
    )
    qkv_sum.keep(keep)
    sums = jnp.concatenate([(sums_away + sums_keep)[0:2], gln[0:2]], axis=0)
    sent = qkv_sum.send(got, rider=sums.reshape(-1, 128))
    up_sum.send(sent)
    gtok = input_grad_stage(gph, gpl, wqh, wql, after(xhat1, sent), inv1, ln, gm)
    output = output_stage(after(middle, gtok), hh, hl, dh, dl)
    rode = qkv_sum.rode
    sent = qkv_sum.send(qkv_sum.last, up_sum.last, output, rider=rode)
    while qkv_sum.stages:
        sent = qkv_sum.send(qkv_sum.last, rider=qkv_sum.rode)
    while up_sum.stages:
        up_sum.send(sent)
    for total in (down_sum, up_sum):
        total.terms[0] = after(total.terms[0], sent)
    sums = qkv_sum.rode
    sums = (sums + plan.send(sums, ("c",))).reshape(4, width)
    (g_down,), (g_up, g_out), (g_qkv,) = (t.total() for t in (down_sum, up_sum, qkv_sum))
    mine = lax.dynamic_slice(sums, (0, me_d * share), (4, share))
    g_down = g_down.reshape(chunks, rows_d, 128).transpose(0, 2, 1).reshape(-1, rows_d)
    shape = tokens.shape
    return (
        output.reshape(shape),
        gtok.reshape(shape),
        mine[0],
        mine[1],
        g_qkv.T,
        g_out.T,
        mine[2],
        mine[3],
        g_up.T,
        g_down,
    )


def solution(mesh):
    weight = P("fsdp", "dp")
    rows = P("dp", "fsdp", None)
    vector = P("dp")
    return jax.shard_map(
        local,
        mesh=mesh,
        in_specs=(rows, P("dp", "fsdp"), rows, vector, vector, weight, weight, vector, vector, weight, weight),
        out_specs=(rows, rows, vector, vector, weight, weight, vector, vector, weight, weight),
        check_vma=False,
    )
```

profile of v0, /device:TPU:0, one launch (start us, length us, event | category | flops | bytes accessed | tf_op | source)
XLA Modules:
  0.0 289.3 jit_solution(7777545155725539255)
XLA Ops:
  2.6 3.0 %collective-permute-start = (f32[1,208,128]{2,1,0:T(8,128)S(1)}, f32[1,208,128]{2,1,0:T(8,128)S(1)}, u32[]{:S(2)}, u32[]{:S(2)}) collective-permute-start(f32[1,208,128]{2,1,0:T(8,128)S(1)} %maximum_bitcast_fusion.1), channel_id=1, source_target_pairs={{0,8},{4,12},{8,0},{12,4},{16,24},{20,28},{24,16},{28,20},{1,9},{5... | collective-permute-start | bytes 319496 | tf_op jit(solution)/shard_map/ppermute | solution.py:131
  5.6 2.6 collective-permute-start.1
  17.3 2.0 collective-permute-start.5
  19.4 1.7 collective-permute-start.3
  25.3 3.8 %collective-permute-done.4 = f32[4,96,128]{2,1,0:T(8,128)S(1)} collective-permute-done((f32[4,96,128]{2,1,0:T(8,128)S(1)}, f32[4,96,128]{2,1,0:T(8,128)S(1)}, u32[]{:S(2)}, u32[]{:S(2)}) %collective-permute-start.4) | collective-permute-done | bytes 196640 | tf_op jit(solution)/shard_map/ppermute | solution.py:133
  30.3 1.6 collective-permute-start.9
  34.0 2.1 collective-permute-start.11
  37.4 5.3 %collective-permute-done.11 = f32[1,256,128]{2,1,0:T(8,128)} collective-permute-done((f32[1,256,128]{2,1,0:T(8,128)S(1)}, f32[1,256,128]{2,1,0:T(8,128)}, u32[]{:S(2)}, u32[]{:S(2)}) %collective-permute-start.11) | collective-permute-done | bytes 131104 | tf_op jit(solution)/shard_map/ppermute | solution.py:131
  42.7 1.9 collective-permute-done.10
  50.6 1.5 collective-permute-start.18
  52.8 8.8 %shard_map.276 = (f32[512,1536]{1,0:T(8,128)}, bf16[1536,512]{1,0:T(8,128)(2,1)}, bf16[1536,512]{1,0:T(8,128)(2,1)}, f32[512,512]{1,0:T(8,128)}, f32[512,128]{1,...) custom-call(s32[2]{0:T(128)} %pad_add_fusion.3.me_ref, f32[512,512]{1,0:T(8,128)} %bitcast.115, ...), custom_call_target="tpu_custom_call" | custom-call | flops 333000000 | bytes 925000 | tf_op jit(solution)/shard_map/pallas_call | solution.py:366
  61.6 1.6 collective-permute-start.20
  64.9 1.7 collective-permute-start.23
  67.6 1.6 collective-permute-start.22
  70.8 7.5 %shard_map.277 = (f32[512,512]{1,0:T(8,128)}, f32[512,512]{1,0:T(8,128)}) custom-call(f32[512,1536]{1,0:T(8,128)} %get-tuple-element.148.q.k.v, f32[512,1536]{1,0:T(8,128)} %get-tuple-element.148.q.k.v, f32[512,1536]{1,0:T(8,128)} %get-tuple-element.148.q.k.v, f32[2,2,32,512]{3,2,1,0:T(8,128)} %copy-done.2, f32[2,2,32,512]{3,2,1,0:T(8,128)} %copy-done.2, ...), custom_call_target="tpu_custom_call" | custom-call | flops 427500000 | bytes 1187500 | tf_op jit(solution)/shard_map/pallas_call | solution.py:492
  78.3 3.3 %collective-permute-done.23.rest_6_ = f32[8,160,128]{2,1,0:T(8,128)S(1)} collective-permute-done((f32[8,160,128]{2,1,0:T(8,128)S(1)}, f32[8,160,128]{2,1,0:T(8,128)S(1)}, u32[]{:S(2)}, u32[]{:S(2)}) %collective-permute-start.23) | collective-permute-done | bytes 655392 | tf_op jit(solution)/shard_map/ppermute | solution.py:131
  81.6 2.5 collective-permute-done.22.rest_4_
  86.7 7.5 %shard_map.278 = (f32[512,512]{1,0:T(8,128)}, f32[512,512]{1,0:T(8,128)}) custom-call(f32[512,1536]{1,0:T(8,128)} %get-tuple-element.148.q.k.v, f32[512,1536]{1,0:T(8,128)} %get-tuple-element.148.q.k.v, f32[512,1536]{1,0:T(8,128)} %get-tuple-element.148.q.k.v, f32[2,2,32,512]{3,2,1,0:T(8,128)} %copy-done.2, ...), custom_call_target="tpu_custom_call", output_to_operand_aliasing={{0}: (10, {}), {1}: (11, {})} | custom-call | flops 427500000 | bytes 1187500 | tf_op jit(solution)/shard_map/pallas_call | solution.py:492
  94.9 1.6 collective-permute-start.31
  97.0 6.1 %shard_map.279 = (bf16[512,2048]{1,0:T(8,128)(2,1)}, bf16[512,2048]{1,0:T(8,128)(2,1)}, bf16[512,512]{1,0:T(8,128)(2,1)}, bf16[512,512]{1,0:T(8,128)(2,1)}) custom-call(s32[2]{0:T(128)} %pad_add_fusion.3.me_ref, f32[8,160,128]{2,1,0:T(8,128)} %copy-done.5, f32[8,160,128]{2,1,0:T(8,128)} %collective-permute-done.24.rest_1_, f32[8,160,128]{2,1,0:T(8,128)} %copy-done.4, ...), custom_call_target="tpu_custom_call" | custom-call | flops 225000000 | bytes 625000 | tf_op jit(solution)/shard_map/pallas_call | solution.py:627
  103.1 4.3 %shard_map.280 = (f32[512,512]{1,0:T(8,128)}, f32[512,512]{1,0:T(8,128)}, f32[512,128]{1,0:T(8,128)}) custom-call(f32[512,512]{1,0:T(8,128)} %bitcast.116, f32[512,512]{1,0:T(8,128)} %get-tuple-element.149.att.rest_0_, bf16[512,512]{1,0:T(8,128)(2,1)} %get-tuple-element.155.wh_ref.oh_ref, bf16[512,512]{1,0:T(8,128)(2,1)} %get-tuple-element.156.wl_ref.ol_ref), custom_call_target="tpu_custom_call" | custom-call | flops 193500000 | bytes 537500 | tf_op jit(solution)/shard_map/pallas_call | solution.py:589
  111.5 14.5 %shard_map.281 = (bf16[512,2048]{1,0:T(8,128)(2,1)}, bf16[512,2048]{1,0:T(8,128)(2,1)}, bf16[512,2048]{1,0:T(8,128)(2,1)}, bf16[512,2048]{1,0:T(8,128)(2,1)}, bf...) custom-call(s32[2]{0:T(128)} %pad_add_fusion.3.me_ref, f32[512,512]{1,0:T(8,128)} %get-tuple-element.177.xhat_ref, ...), custom_call_target="tpu_custom_call" | custom-call | flops 675000000 | bytes 1875000 | tf_op jit(solution)/shard_map/pallas_call | solution.py:682
  126.0 5.7 %shard_map.282 = f32[16,256,128]{2,1,0:T(8,128)} custom-call(s32[2]{0:T(128)} %pad_add_fusion.3.me_ref, f32[512,512]{1,0:T(8,128)} %bitcast.112, bf16[512,2048]{1,0:T(8,128)(2,1)} %get-tuple-element.170.hh_ref.h0, bf16[512,2048]{1,0:T(8,128)(2,1)} %get-tuple-element.171.hl_ref.h1), custom_call_target="tpu_custom_call" | custom-call | flops 247500000 | bytes 687500 | tf_op jit(solution)/shard_map/pallas_call | solution.py:717
  131.8 6.4 %shard_map.283 = f32[16,256,128]{2,1,0:T(8,128)} custom-call(s32[2]{0:T(128)} %pad_add_fusion.3.me_ref, f32[512,512]{1,0:T(8,128)} %get-tuple-element.177.xhat_ref, f32[8,512]{1,0:T(8,128)} %get-tuple-element.167.ln_ref.ln_r, bf16[512,2048]{1,0:T(8,128)(2,1)} %get-tuple-element.173.ph_ref.p0, bf16[512,2048]{1,0:T(8,128)(2,1)} %get-tuple-element.174.pl_ref.p1), custom_call_target="tpu_custom_call" | custom-call | flops 288000000 | bytes 800000 | tf_op jit(solution)/shard_map/pallas_call | solution.py:760
  138.6 5.6 %shard_map.284 = f32[16,256,128]{2,1,0:T(8,128)} custom-call(s32[2]{0:T(128)} %pad_add_fusion.3.me_ref, f32[512,512]{1,0:T(8,128)} %bitcast.113, bf16[512,2048]{1,0:T(8,128)(2,1)} %get-tuple-element.170.hh_ref.h0, bf16[512,2048]{1,0:T(8,128)(2,1)} %get-tuple-element.171.hl_ref.h1), custom_call_target="tpu_custom_call" | custom-call | flops 247500000 | bytes 687500 | tf_op jit(solution)/shard_map/pallas_call | solution.py:717
  144.2 2.8 slice_add_fusion.3
  147.0 2.5 collective-permute-start.40
  150.5 6.5 %shard_map.285 = f32[16,256,128]{2,1,0:T(8,128)} custom-call(s32[2]{0:T(128)} %pad_add_fusion.3.me_ref, f32[512,512]{1,0:T(8,128)} %get-tuple-element.177.xhat_ref, f32[8,512]{1,0:T(8,128)} %get-tuple-element.167.ln_ref.ln_r, bf16[512,2048]{1,0:T(8,128)(2,1)} %get-tuple-element.173.ph_ref.p0, bf16[512,2048]{1,0:T(8,128)(2,1)} %get-tuple-element.174.pl_ref.p1), custom_call_target="tpu_custom_call" | custom-call | flops 288000000 | bytes 800000 | tf_op jit(solution)/shard_map/pallas_call | solution.py:760
  158.3 8.7 %shard_map.286 = (f32[512,512]{1,0:T(8,128)}, f32[8,512]{1,0:T(8,128)}) custom-call(f32[512,512]{1,0:T(8,128)} %bitcast.114, f32[512,512]{1,0:T(8,128)} %get-tuple-element.177.xhat_ref, f32[512,128]{1,0:T(8,128)} %get-tuple-element.179.inv_ref, f32[8,512]{1,0:T(8,128)} %get-tuple-element.167.ln_ref.ln_r, bf16[512,2048]{1,0:T(8,128)(2,1)} %get-tuple-element.173.ph_ref.p0, ...), custom_call_target="tpu_custom_call" | custom-call | flops 382500000 | bytes 1062500 | tf_op jit(solution)/shard_map/pallas_call | solution.py:828
  166.9 5.2 %shard_map.287 = (f32[512,512]{1,0:T(8,128)}, f32[16,64,128]{2,1,0:T(8,128)}, f32[16,64,128]{2,1,0:T(8,128)}) custom-call(s32[2]{0:T(128)} %pad_add_fusion.3.me_ref, f32[512,512]{1,0:T(8,128)} %get-tuple-element.182.gm_ref.gm_r, f32[512,512]{1,0:T(8,128)} %get-tuple-element.149.att.rest_0_, bf16[512,512]{1,0:T(8,128)(2,1)} %get-tuple-element.155.wh_ref.oh_ref, ...), custom_call_target="tpu_custom_call" | custom-call | flops 225000000 | bytes 625000 | tf_op jit(solution)/shard_map/pallas_call | solution.py:859
  173.5 2.1 collective-permute-done.42
  175.6 1.7 slice_add_fusion
  178.3 1.6 collective-permute-start.43
  185.4 11.9 %shard_map.288 = (f32[512,512]{1,0:T(8,128)}, f32[512,512]{1,0:T(8,128)}, f32[512,512]{1,0:T(8,128)}, f32[2,2,16,512]{3,2,1,0:T(8,128)}, f32[2,2,8,512]{3,2,1,0:T(8,128)}, /*index=5*/f32[2,2,8,512]{3,2,1,0:T(8,128)}) custom-call(f32[512,1536]{1,0:T(8,128)} %get-tuple-element.148.q.k.v, f32[512,1536]{1,0:T(8,128)} %get-tuple-element.148.q.k.v, ...), custom_call_target="tpu_custom_call" | custom-call | flops 360000000 | bytes 1000000 | tf_op jit(solution)/shard_map/pallas_call | solution.py:563
  197.3 1.9 fusion.10
  199.3 11.7 %shard_map.289 = (f32[512,512]{1,0:T(8,128)}, f32[512,512]{1,0:T(8,128)}, f32[512,512]{1,0:T(8,128)}, f32[2,2,16,512]{3,2,1,0:T(8,128)}, f32[2,2,8,512]{3,2,1,0:T(8,128)}, /*index=5*/f32[2,2,8,512]{3,2,1,0:T(8,128)}) custom-call(f32[512,1536]{1,0:T(8,128)} %get-tuple-element.148.q.k.v,, ...), custom_call_target="tpu_custom_call", output_to_operand_aliasing={{0}: (13, {}), {1}: (14, {}), {2}: (15, {}), {3}: (16, {}),... | custom-call | flops 360000000 | bytes 1000000 | tf_op jit(solution)/shard_map/pallas_call | solution.py:563
  213.5 3.2 %collective-permute-done.47.g5a_r = f32[2,2,8,512]{3,2,1,0:T(8,128)S(1)} collective-permute-done((f32[2,2,8,512]{3,2,1,0:T(8,128)}, f32[2,2,8,512]{3,2,1,0:T(8,128)S(1)}, u32[]{:S(2)}, u32[]{:S(2)}) %collective-permute-start.47) | collective-permute-done | bytes 65568 | tf_op jit(solution)/shard_map/ppermute | solution.py:973
  218.6 4.9 %shard_map.290 = (bf16[512,1536]{1,0:T(8,128)(2,1)}, bf16[512,1536]{1,0:T(8,128)(2,1)}, f32[1536,128]{1,0:T(8,128)}) custom-call(f32[512,512]{1,0:T(8,128)} %get-tuple-element.198.dq_r, f32[512,512]{1,0:T(8,128)} %get-tuple-element.199.dk_r, f32[512,512]{1,0:T(8,128)} %get-tuple-element.200.dv_r, f32[2,2,16,512]{3,2,1,0:T(8,128)} %copy-done.34, ...), custom_call_target="tpu_custom_call" | custom-call | flops 202500000 | bytes 562500 | tf_op jit(solution)/shard_map/pallas_call | solution.py:893
  223.5 5.9 %shard_map.291 = (f32[16,192,128]{2,1,0:T(8,128)}, f32[8,512]{1,0:T(8,128)}) custom-call(s32[2]{0:T(128)} %pad_add_fusion.3.me_ref, bf16[512,1536]{1,0:T(8,128)(2,1)} %get-tuple-element.207.gph_r, bf16[512,1536]{1,0:T(8,128)(2,1)} %get-tuple-element.208.gpl_r, f32[1536,128]{1,0:T(8,128)} %get-tuple-element.212.col_r, f32[512,512]{1,0:T(8,128)} %get-tuple-element.219.xhat_r, ...), custom_call_target="tpu_custom_call" | custom-call | flops 11250000 | bytes 31250 | tf_op jit(solution)/shard_map/pallas_call | solution.py:956
  230.3 5.9 %shard_map.292 = (f32[16,192,128]{2,1,0:T(8,128)}, f32[8,512]{1,0:T(8,128)}) custom-call(s32[2]{0:T(128)} %pad_add_fusion.3.me_ref, bf16[512,1536]{1,0:T(8,128)(2,1)} %get-tuple-element.207.gph_r, bf16[512,1536]{1,0:T(8,128)(2,1)} %get-tuple-element.208.gpl_r, f32[1536,128]{1,0:T(8,128)} %get-tuple-element.212.col_r, f32[512,512]{1,0:T(8,128)} %get-tuple-element.219.xhat_r, ...), custom_call_target="tpu_custom_call" | custom-call | flops 11250000 | bytes 31250 | tf_op jit(solution)/shard_map/pallas_call | solution.py:956
  237.0 1.7 slice_add_fusion.6
  246.5 1.7 collective-permute-start.59
  248.3 7.2 %shard_map.293 = f32[512,512]{1,0:T(8,128)} custom-call(bf16[512,1536]{1,0:T(8,128)(2,1)} %get-tuple-element.207.gph_r, bf16[512,1536]{1,0:T(8,128)(2,1)} %get-tuple-element.208.gpl_r, bf16[1536,512]{1,0:T(8,128)(2,1)} %get-tuple-element.209.wh_r.wh, bf16[1536,512]{1,0:T(8,128)(2,1)} %get-tuple-element.210.wl_r.wl, f32[512,512]{1,0:T(8,128)} %get-tuple-element.219.xhat_r, ...), custom_call_target="tpu_custom_call" | custom-call | flops 333000000 | bytes 925000 | tf_op jit(solution)/shard_map/pallas_call | solution.py:909
  255.5 7.8 %shard_map.294 = f32[512,512]{1,0:T(8,128)} custom-call(f32[512,512]{1,0:T(8,128)} %get-tuple-element.221.mid, bf16[512,2048]{1,0:T(8,128)(2,1)} %get-tuple-element.170.hh_ref.h0, bf16[512,2048]{1,0:T(8,128)(2,1)} %get-tuple-element.171.hl_ref.h1, bf16[512,2048]{1,0:T(8,128)(2,1)} %get-tuple-element.168.d0, bf16[512,2048]{1,0:T(8,128)(2,1)} %get-tuple-element.169.d1), custom_call_target="tpu_custom_call" | custom-call | flops 360000000 | bytes 1000000 | tf_op jit(solution)/shard_map/pallas_call | solution.py:793
  266.7 1.7 collective-permute-start.56
  269.4 1.7 collective-permute-start.54
  275.4 7.3 %collective-permute-done.55 = f32[1,208,128]{2,1,0:T(8,128)S(1)} collective-permute-done((f32[1,208,128]{2,1,0:T(8,128)S(1)}, f32[1,208,128]{2,1,0:T(8,128)S(1)}, u32[]{:S(2)}, u32[]{:S(2)}) %collective-permute-start.55) | collective-permute-done | bytes 106528 | tf_op jit(solution)/shard_map/ppermute | solution.py:131
  283.6 1.7 fusion.11
  (302 shorter events, 76.2 us)
Async XLA Ops:
  2.6 14.7 %collective-permute-start = (f32[1,208,128]{2,1,0:T(8,128)S(1)}, f32[1,208,128]{2,1,0:T(8,128)S(1)}, u32[]{:S(2)}, u32[]{:S(2)}) collective-permute-start(f32[1,208,128]{2,1,0:T(8,128)S(1)} %maximum_bitcast_fusion.1), channel_id=1, source_target_pairs={{0,8},{4,12},{8,0},{12,4},{16,24},{20,28},{24,16},{28,20},{1,9},{5... | collective-permute-start | bytes 319496 | tf_op jit(solution)/shard_map/ppermute | solution.py:131
  5.6 11.7 %collective-permute-start.1 = (f32[1,208,128]{2,1,0:T(8,128)S(1)}, f32[1,208,128]{2,1,0:T(8,128)S(1)}, u32[]{:S(2)}, u32[]{:S(2)}) collective-permute-start(f32[1,208,128]{2,1,0:T(8,128)S(1)} %maximum_bitcast_fusion.1), channel_id=1, source_target_pairs={{0,16},{4,20},{8,24},{12,28},{16,0},{20,4},{24,8},{28,12},{1,17},{... | collective-permute-start | bytes 319496 | tf_op jit(solution)/shard_map/ppermute | solution.py:131
  8.2 9.1 %collective-permute-start.2 = (f32[1,208,128]{2,1,0:T(8,128)S(1)}, f32[1,208,128]{2,1,0:T(8,128)S(1)}, u32[]{:S(2)}, u32[]{:S(2)}) collective-permute-start(f32[1,208,128]{2,1,0:T(8,128)S(1)} %maximum_bitcast_fusion.1), channel_id=1, source_target_pairs={{0,24},{4,28},{8,16},{12,20},{16,8},{20,12},{24,0},{28,4},{1,25},{... | collective-permute-start | bytes 319496 | tf_op jit(solution)/shard_map/ppermute | solution.py:131
  8.2 8.6 %collective-permute-start.6 = (s32[2,256]{1,0:T(2,128)}, s32[2,256]{1,0:T(2,128)S(1)}, u32[]{:S(2)}, u32[]{:S(2)}) collective-permute-start(s32[2,256]{1,0:T(2,128)} %param.22), channel_id=1, source_target_pairs={{0,1},{1,0},{2,3},{3,2},{4,5},{5,4},{6,7},{7,6},{8,9},{9,8},{10,11... | collective-permute-start | bytes 6152 | tf_op jit(solution)/shard_map/ppermute | solution.py:973
  17.3 11.9 %collective-permute-start.5 = (f32[1,320,128]{2,1,0:T(8,128)S(1)}, f32[1,320,128]{2,1,0:T(8,128)}, u32[]{:S(2)}, u32[]{:S(2)}) collective-permute-start(f32[1,320,128]{2,1,0:T(8,128)S(1)} %maximum_bitcast_fusion), channel_id=1, source_target_pairs={{0,16},{4,20},{8,24},{12,28},{16,0},{20,4},{24,8},{28,12},{1,17},{... | collective-permute-start | bytes 491528 | tf_op jit(solution)/shard_map/ppermute | solution.py:131
  19.4 9.7 %collective-permute-start.3 = (f32[4,112,128]{2,1,0:T(8,128)S(1)}, f32[4,112,128]{2,1,0:T(8,128)S(1)}, u32[]{:S(2)}, u32[]{:S(2)}) collective-permute-start(f32[4,112,128]{2,1,0:T(8,128)S(1)} %slice.596), channel_id=1, source_target_pairs={{0,4},{4,0},{8,12},{12,8},{16,20},{20,16},{24,28},{28,24},{1,5},{5... | collective-permute-start | bytes 688136 | tf_op jit(solution)/shard_map/ppermute | solution.py:131
  22.6 6.5 %collective-permute-start.4 = (f32[4,96,128]{2,1,0:T(8,128)S(1)}, f32[4,96,128]{2,1,0:T(8,128)S(1)}, u32[]{:S(2)}, u32[]{:S(2)}) collective-permute-start(f32[4,96,128]{2,1,0:T(8,128)S(1)} %pad_maximum_fusion.16), channel_id=1, source_target_pairs={{0,2},{1,3},{2,0},{3,1},{4,6},{5,7},{6,4},{7,5},{8,10},{9,11},{10,... | collective-permute-start | bytes 589832 | tf_op jit(solution)/shard_map/ppermute | solution.py:133
  29.2 15.4 %collective-permute-start.8 = (f32[8,112,128]{2,1,0:T(8,128)S(1)}, f32[8,112,128]{2,1,0:T(8,128)S(1)}, u32[]{:S(2)}, u32[]{:S(2)}) collective-permute-start(f32[8,112,128]{2,1,0:T(8,128)S(1)} %pad_maximum_fusion.10.rest_0_), channel_id=1, source_target_pairs={{0,2},{1,3},{2,0},{3,1},{4,6},{5,7},{6,4},{7,5},{8,10},{9,11},{10,... | collective-permute-start | bytes 1376264 | tf_op jit(solution)/shard_map/ppermute | solution.py:133
  30.3 14.3 %collective-permute-start.9 = (f32[8,96,128]{2,1,0:T(8,128)S(1)}, f32[8,96,128]{2,1,0:T(8,128)S(1)}, u32[]{:S(2)}, u32[]{:S(2)}) collective-permute-start(f32[8,96,128]{2,1,0:T(8,128)S(1)} %pad_maximum_fusion.12.rest_2_), channel_id=1, source_target_pairs={{0,4},{4,0},{8,12},{12,8},{16,20},{20,16},{24,28},{28,24},{1,5},{5... | collective-permute-start | bytes 1179656 | tf_op jit(solution)/shard_map/ppermute | solution.py:131
  32.8 11.8 %collective-permute-start.10 = (f32[2,320,128]{2,1,0:T(8,128)S(1)}, f32[2,320,128]{2,1,0:T(8,128)}, u32[]{:S(2)}, u32[]{:S(2)}) collective-permute-start(f32[2,320,128]{2,1,0:T(8,128)S(1)} %pad_maximum_fusion.13), channel_id=1, source_target_pairs={{0,8},{4,12},{8,0},{12,4},{16,24},{20,28},{24,16},{28,20},{1,9},{5... | collective-permute-start | bytes 983048 | tf_op jit(solution)/shard_map/ppermute | solution.py:131
  34.0 8.7 %collective-permute-start.11 = (f32[1,256,128]{2,1,0:T(8,128)S(1)}, f32[1,256,128]{2,1,0:T(8,128)}, u32[]{:S(2)}, u32[]{:S(2)}) collective-permute-start(f32[1,256,128]{2,1,0:T(8,128)S(1)} %bitcast.120), channel_id=1, source_target_pairs={{0,16},{4,20},{8,24},{12,28},{16,0},{20,4},{24,8},{28,12},{1,17},{... | collective-permute-start | bytes 393224 | tf_op jit(solution)/shard_map/ppermute | solution.py:131
  48.4 13.2 %collective-permute-start.17 = (f32[4,160,128]{2,1,0:T(8,128)S(1)}, f32[4,160,128]{2,1,0:T(8,128)S(1)}, u32[]{:S(2)}, u32[]{:S(2)}) collective-permute-start(f32[4,160,128]{2,1,0:T(8,128)S(1)} %get-tuple-element.137), channel_id=1, source_target_pairs={{0,2},{1,3},{2,0},{3,1},{4,6},{5,7},{6,4},{7,5},{8,10},{9,11},{10,... | collective-permute-start | bytes 983048 | tf_op jit(solution)/shard_map/ppermute | solution.py:133
  49.0 12.7 %collective-permute-start.16 = (f32[4,160,128]{2,1,0:T(8,128)S(1)}, f32[4,160,128]{2,1,0:T(8,128)S(1)}, u32[]{:S(2)}, u32[]{:S(2)}) collective-permute-start(f32[4,160,128]{2,1,0:T(8,128)S(1)} %get-tuple-element.136), channel_id=1, source_target_pairs={{0,4},{4,0},{8,12},{12,8},{16,20},{20,16},{24,28},{28,24},{1,5},{5... | collective-permute-start | bytes 983048 | tf_op jit(solution)/shard_map/ppermute | solution.py:131
  50.6 11.0 %collective-permute-start.18 = (f32[2,256,128]{2,1,0:T(8,128)S(1)}, f32[2,256,128]{2,1,0:T(8,128)}, u32[]{:S(2)}, u32[]{:S(2)}) collective-permute-start(f32[2,256,128]{2,1,0:T(8,128)S(1)} %pad_maximum_fusion.15), channel_id=1, source_target_pairs={{0,8},{4,12},{8,0},{12,4},{16,24},{20,28},{24,16},{28,20},{1,9},{5... | collective-permute-start | bytes 786440 | tf_op jit(solution)/shard_map/ppermute | solution.py:131
  61.6 7.5 %collective-permute-start.20 = (f32[2,2,8,512]{3,2,1,0:T(8,128)}, f32[2,2,8,512]{3,2,1,0:T(8,128)S(1)}, u32[]{:S(2)}, u32[]{:S(2)}) collective-permute-start(f32[2,2,8,512]{3,2,1,0:T(8,128)} %get-tuple-element.140), channel_id=1, source_target_pairs={{0,2},{1,3},{2,0},{3,1},{4,6},{5,7},{6,4},{7,5},{8,10},{9,11},{10,... | collective-permute-start | bytes 196616 | tf_op jit(solution)/shard_map/ppermute | solution.py:973
  63.2 6.0 %collective-permute-start.21 = (f32[2,2,8,512]{3,2,1,0:T(8,128)}, f32[2,2,8,512]{3,2,1,0:T(8,128)S(1)}, u32[]{:S(2)}, u32[]{:S(2)}) collective-permute-start(f32[2,2,8,512]{3,2,1,0:T(8,128)} %get-tuple-element.140), channel_id=1, source_target_pairs={{0,3},{1,2},{2,1},{3,0},{4,7},{5,6},{6,5},{7,4},{8,11},{9,10},{10,... | collective-permute-start | bytes 196616 | tf_op jit(solution)/shard_map/ppermute | solution.py:973
  63.2 5.9 %collective-permute-start.19 = (f32[2,2,16,512]{3,2,1,0:T(8,128)}, f32[2,2,16,512]{3,2,1,0:T(8,128)S(1)}, u32[]{:S(2)}, u32[]{:S(2)}) collective-permute-start(f32[2,2,16,512]{3,2,1,0:T(8,128)} %get-tuple-element.139), channel_id=1, source_target_pairs={{0,1},{1,0},{2,3},{3,2},{4,5},{5,4},{6,7},{7,6},{8,9},{9,8},{10,11... | collective-permute-start | bytes 393224 | tf_op jit(solution)/shard_map/ppermute | solution.py:973
  64.9 16.7 %collective-permute-start.23 = (f32[8,160,128]{2,1,0:T(8,128)S(1)}, f32[8,160,128]{2,1,0:T(8,128)S(1)}, u32[]{:S(2)}, u32[]{:S(2)}) collective-permute-start(f32[8,160,128]{2,1,0:T(8,128)S(1)} %pad_maximum_fusion.4.rest_2_), channel_id=1, source_target_pairs={{0,4},{4,0},{8,12},{12,8},{16,20},{20,16},{24,28},{28,24},{1,5},{5... | collective-permute-start | bytes 1966088 | tf_op jit(solution)/shard_map/ppermute | solution.py:131
  67.6 16.5 %collective-permute-start.22 = (f32[8,160,128]{2,1,0:T(8,128)S(1)}, f32[8,160,128]{2,1,0:T(8,128)}, u32[]{:S(2)}, u32[]{:S(2)}) collective-permute-start(f32[8,160,128]{2,1,0:T(8,128)S(1)} %pad_maximum_fusion.3.rest_0_), channel_id=1, source_target_pairs={{0,2},{1,3},{2,0},{3,1},{4,6},{5,7},{6,4},{7,5},{8,10},{9,11},{10,... | collective-permute-start | bytes 1966088 | tf_op jit(solution)/shard_map/ppermute | solution.py:133
  69.2 14.9 %collective-permute-start.24 = (f32[8,160,128]{2,1,0:T(8,128)S(1)}, f32[8,160,128]{2,1,0:T(8,128)}, u32[]{:S(2)}, u32[]{:S(2)}) collective-permute-start(f32[8,160,128]{2,1,0:T(8,128)S(1)} %pad_maximum_fusion.3.rest_0_), channel_id=1, source_target_pairs={{0,1},{1,0},{2,3},{3,2},{4,5},{5,4},{6,7},{7,6},{8,9},{9,8},{10,11... | collective-permute-start | bytes 1966088 | tf_op jit(solution)/shard_map/ppermute | solution.py:133
  69.3 14.8 %collective-permute-start.25 = (f32[8,160,128]{2,1,0:T(8,128)S(1)}, f32[8,160,128]{2,1,0:T(8,128)}, u32[]{:S(2)}, u32[]{:S(2)}) collective-permute-start(f32[8,160,128]{2,1,0:T(8,128)S(1)} %pad_maximum_fusion.4.rest_2_), channel_id=1, source_target_pairs={{0,1},{1,0},{2,3},{3,2},{4,5},{5,4},{6,7},{7,6},{8,9},{9,8},{10,11... | collective-permute-start | bytes 1966088 | tf_op jit(solution)/shard_map/ppermute | solution.py:133
  84.1 10.2 %collective-permute-start.28 = (f32[8,160,128]{2,1,0:T(8,128)}, f32[8,160,128]{2,1,0:T(8,128)}, u32[]{:S(2)}, u32[]{:S(2)}) collective-permute-start(f32[8,160,128]{2,1,0:T(8,128)} %collective-permute-done.22.rest_4_), channel_id=1, source_target_pairs={{0,1},{1,0},{2,3},{3,2},{4,5},{5,4},{6,7},{7,6},{8,9},{9,8},{10,11... | collective-permute-start | bytes 1966088 | tf_op jit(solution)/shard_map/ppermute | solution.py:133
  84.1 10.2 %collective-permute-start.29 = (f32[8,160,128]{2,1,0:T(8,128)S(1)}, f32[8,160,128]{2,1,0:T(8,128)}, u32[]{:S(2)}, u32[]{:S(2)}) collective-permute-start(f32[8,160,128]{2,1,0:T(8,128)S(1)} %collective-permute-done.23.rest_6_), channel_id=1, source_target_pairs={{0,1},{1,0},{2,3},{3,2},{4,5},{5,4},{6,7},{7,6},{8,9},{9,8},{10,11... | collective-permute-start | bytes 1966088 | tf_op jit(solution)/shard_map/ppermute | solution.py:133
  84.7 9.5 %collective-permute-start.26 = (f32[4,128,128]{2,1,0:T(8,128)S(1)}, f32[4,128,128]{2,1,0:T(8,128)S(1)}, u32[]{:S(2)}, u32[]{:S(2)}) collective-permute-start(f32[4,128,128]{2,1,0:T(8,128)S(1)} %get-tuple-element.150), channel_id=1, source_target_pairs={{0,4},{4,0},{8,12},{12,8},{16,20},{20,16},{24,28},{28,24},{1,5},{5... | collective-permute-start | bytes 786440 | tf_op jit(solution)/shard_map/ppermute | solution.py:131
  85.2 9.0 %collective-permute-start.27 = (f32[4,128,128]{2,1,0:T(8,128)S(1)}, f32[4,128,128]{2,1,0:T(8,128)S(1)}, u32[]{:S(2)}, u32[]{:S(2)}) collective-permute-start(f32[4,128,128]{2,1,0:T(8,128)S(1)} %get-tuple-element.151), channel_id=1, source_target_pairs={{0,2},{1,3},{2,0},{3,1},{4,6},{5,7},{6,4},{7,5},{8,10},{9,11},{10,... | collective-permute-start | bytes 786440 | tf_op jit(solution)/shard_map/ppermute | solution.py:133
  94.3 13.4 %collective-permute-start.30 = (f32[8,128,128]{2,1,0:T(8,128)S(1)}, f32[8,128,128]{2,1,0:T(8,128)S(1)}, u32[]{:S(2)}, u32[]{:S(2)}) collective-permute-start(f32[8,128,128]{2,1,0:T(8,128)S(1)} %pad_maximum_fusion.8.rest_0_), channel_id=1, source_target_pairs={{0,2},{1,3},{2,0},{3,1},{4,6},{5,7},{6,4},{7,5},{8,10},{9,11},{10,... | collective-permute-start | bytes 1572872 | tf_op jit(solution)/shard_map/ppermute | solution.py:133
  94.9 13.1 %collective-permute-start.31 = (f32[8,128,128]{2,1,0:T(8,128)S(1)}, f32[8,128,128]{2,1,0:T(8,128)S(1)}, u32[]{:S(2)}, u32[]{:S(2)}) collective-permute-start(f32[8,128,128]{2,1,0:T(8,128)S(1)} %pad_maximum_fusion.9.rest_2_), channel_id=1, source_target_pairs={{0,4},{4,0},{8,12},{12,8},{16,20},{20,16},{24,28},{28,24},{1,5},{5... | collective-permute-start | bytes 1572872 | tf_op jit(solution)/shard_map/ppermute | solution.py:131
  96.5 11.5 %collective-permute-start.32 = (f32[8,128,128]{2,1,0:T(8,128)S(1)}, f32[8,128,128]{2,1,0:T(8,128)S(1)}, u32[]{:S(2)}, u32[]{:S(2)}) collective-permute-start(f32[8,128,128]{2,1,0:T(8,128)S(1)} %pad_maximum_fusion.8.rest_0_), channel_id=1, source_target_pairs={{0,1},{1,0},{2,3},{3,2},{4,5},{5,4},{6,7},{7,6},{8,9},{9,8},{10,11... | collective-permute-start | bytes 1572872 | tf_op jit(solution)/shard_map/ppermute | solution.py:133
  96.5 11.5 %collective-permute-start.33 = (f32[8,128,128]{2,1,0:T(8,128)S(1)}, f32[8,128,128]{2,1,0:T(8,128)S(1)}, u32[]{:S(2)}, u32[]{:S(2)}) collective-permute-start(f32[8,128,128]{2,1,0:T(8,128)S(1)} %pad_maximum_fusion.9.rest_2_), channel_id=1, source_target_pairs={{0,1},{1,0},{2,3},{3,2},{4,5},{5,4},{6,7},{7,6},{8,9},{9,8},{10,11... | collective-permute-start | bytes 1572872 | tf_op jit(solution)/shard_map/ppermute | solution.py:133
  131.7 12.5 %collective-permute-start.36 = (f32[16,256,128]{2,1,0:T(8,128)}, f32[16,256,128]{2,1,0:T(8,128)}, u32[]{:S(2)}, u32[]{:S(2)}) collective-permute-start(f32[16,256,128]{2,1,0:T(8,128)} %shard_map.282), channel_id=1, source_target_pairs={{0,1},{1,0},{2,3},{3,2},{4,5},{5,4},{6,7},{7,6},{8,9},{9,8},{10,11... | collective-permute-start | bytes 6291464 | tf_op jit(solution)/shard_map/ppermute | solution.py:133
  138.2 18.8 %collective-permute-start.37 = (f32[16,256,128]{2,1,0:T(8,128)}, f32[16,256,128]{2,1,0:T(8,128)S(1)}, u32[]{:S(2)}, u32[]{:S(2)}) collective-permute-start(f32[16,256,128]{2,1,0:T(8,128)} %shard_map.283), channel_id=1, source_target_pairs={{0,1},{1,0},{2,3},{3,2},{4,5},{5,4},{6,7},{7,6},{8,9},{9,8},{10,11... | collective-permute-start | bytes 6291464 | tf_op jit(solution)/shard_map/ppermute | solution.py:133
  147.0 25.1 %collective-permute-start.40 = (f32[4,256,128]{2,1,0:T(8,128)}, f32[4,256,128]{2,1,0:T(8,128)}, u32[]{:S(2)}, u32[]{:S(2)}) collective-permute-start(f32[4,256,128]{2,1,0:T(8,128)} %get-tuple-element.272), channel_id=1, source_target_pairs={{0,6},{1,7},{2,4},{3,5},{4,2},{5,3},{6,0},{7,1},{8,14},{9,15},{10,... | collective-permute-start | bytes 1572872 | tf_op jit(solution)/shard_map/ppermute | solution.py:136
  149.5 23.9 %collective-permute-start.39 = (f32[4,256,128]{2,1,0:T(8,128)S(1)}, f32[4,256,128]{2,1,0:T(8,128)}, u32[]{:S(2)}, u32[]{:S(2)}) collective-permute-start(f32[4,256,128]{2,1,0:T(8,128)S(1)} %get-tuple-element.273), channel_id=1, source_target_pairs={{0,2},{1,3},{2,0},{3,1},{4,6},{5,7},{6,4},{7,5},{8,10},{9,11},{10,... | collective-permute-start | bytes 1572872 | tf_op jit(solution)/shard_map/ppermute | solution.py:133
  150.0 23.5 %collective-permute-start.38 = (f32[4,256,128]{2,1,0:T(8,128)S(1)}, f32[4,256,128]{2,1,0:T(8,128)}, u32[]{:S(2)}, u32[]{:S(2)}) collective-permute-start(f32[4,256,128]{2,1,0:T(8,128)S(1)} %get-tuple-element.274), channel_id=1, source_target_pairs={{0,4},{4,0},{8,12},{12,8},{16,20},{20,16},{24,28},{28,24},{1,5},{5... | collective-permute-start | bytes 1572872 | tf_op jit(solution)/shard_map/ppermute | solution.py:131
  178.3 32.7 %collective-permute-start.43 = (f32[4,320,128]{2,1,0:T(8,128)}, f32[4,320,128]{2,1,0:T(8,128)}, u32[]{:S(2)}, u32[]{:S(2)}) collective-permute-start(f32[4,320,128]{2,1,0:T(8,128)} %pad_maximum_fusion.5), channel_id=1, source_target_pairs={{0,4},{4,0},{8,12},{12,8},{16,20},{20,16},{24,28},{28,24},{1,5},{5... | collective-permute-start | bytes 1966088 | tf_op jit(solution)/shard_map/ppermute | solution.py:131
  180.7 30.9 %collective-permute-start.44 = (f32[4,320,128]{2,1,0:T(8,128)}, f32[4,320,128]{2,1,0:T(8,128)}, u32[]{:S(2)}, u32[]{:S(2)}) collective-permute-start(f32[4,320,128]{2,1,0:T(8,128)} %pad_maximum_fusion.6), channel_id=1, source_target_pairs={{0,2},{1,3},{2,0},{3,1},{4,6},{5,7},{6,4},{7,5},{8,10},{9,11},{10,... | collective-permute-start | bytes 1966088 | tf_op jit(solution)/shard_map/ppermute | solution.py:133
  182.2 29.4 %collective-permute-start.45 = (f32[4,320,128]{2,1,0:T(8,128)}, f32[4,320,128]{2,1,0:T(8,128)S(1)}, u32[]{:S(2)}, u32[]{:S(2)}) collective-permute-start(f32[4,320,128]{2,1,0:T(8,128)} %pad_maximum_fusion.7), channel_id=1, source_target_pairs={{0,6},{1,7},{2,4},{3,5},{4,2},{5,3},{6,0},{7,1},{8,14},{9,15},{10,... | collective-permute-start | bytes 1966088 | tf_op jit(solution)/shard_map/ppermute | solution.py:136
  184.9 12.4 %collective-permute-start.41 = (f32[2,256,128]{2,1,0:T(8,128)S(1)}, f32[2,256,128]{2,1,0:T(8,128)S(1)}, u32[]{:S(2)}, u32[]{:S(2)}) collective-permute-start(f32[2,256,128]{2,1,0:T(8,128)S(1)} %slice_add_fusion.12), channel_id=1, source_target_pairs={{0,8},{4,12},{8,0},{12,4},{16,24},{20,28},{24,16},{28,20},{1,9},{5... | collective-permute-start | bytes 786440 | tf_op jit(solution)/shard_map/ppermute | solution.py:131
  229.4 7.6 %collective-permute-start.49 = (f32[16,192,128]{2,1,0:T(8,128)}, f32[16,192,128]{2,1,0:T(8,128)}, u32[]{:S(2)}, u32[]{:S(2)}) collective-permute-start(f32[16,192,128]{2,1,0:T(8,128)} %get-tuple-element.213), channel_id=1, source_target_pairs={{0,1},{1,0},{2,3},{3,2},{4,5},{5,4},{6,7},{7,6},{8,9},{9,8},{10,11... | collective-permute-start | bytes 4718600 | tf_op jit(solution)/shard_map/ppermute | solution.py:133
  239.8 23.6 %collective-permute-start.52 = (f32[4,208,128]{2,1,0:T(8,128)}, f32[4,208,128]{2,1,0:T(8,128)}, u32[]{:S(2)}, u32[]{:S(2)}) collective-permute-start(f32[4,208,128]{2,1,0:T(8,128)} %get-tuple-element.285), channel_id=1, source_target_pairs={{0,6},{1,7},{2,4},{3,5},{4,2},{5,3},{6,0},{7,1},{8,14},{9,15},{10,... | collective-permute-start | bytes 1277960 | tf_op jit(solution)/shard_map/ppermute | solution.py:136
  241.1 23.3 %collective-permute-start.51 = (f32[4,208,128]{2,1,0:T(8,128)}, f32[4,208,128]{2,1,0:T(8,128)}, u32[]{:S(2)}, u32[]{:S(2)}) collective-permute-start(f32[4,208,128]{2,1,0:T(8,128)} %get-tuple-element.286), channel_id=1, source_target_pairs={{0,2},{1,3},{2,0},{3,1},{4,6},{5,7},{6,4},{7,5},{8,10},{9,11},{10,... | collective-permute-start | bytes 1277960 | tf_op jit(solution)/shard_map/ppermute | solution.py:133
  242.1 22.3 %collective-permute-start.50 = (f32[4,208,128]{2,1,0:T(8,128)}, f32[4,208,128]{2,1,0:T(8,128)}, u32[]{:S(2)}, u32[]{:S(2)}) collective-permute-start(f32[4,208,128]{2,1,0:T(8,128)} %get-tuple-element.287), channel_id=1, source_target_pairs={{0,4},{4,0},{8,12},{12,8},{16,20},{20,16},{24,28},{28,24},{1,5},{5... | collective-permute-start | bytes 1277960 | tf_op jit(solution)/shard_map/ppermute | solution.py:131
  245.5 17.9 %collective-permute-start.53 = (f32[2,320,128]{2,1,0:T(8,128)S(1)}, f32[2,320,128]{2,1,0:T(8,128)S(1)}, u32[]{:S(2)}, u32[]{:S(2)}) collective-permute-start(f32[2,320,128]{2,1,0:T(8,128)S(1)} %pad_maximum_fusion.14), channel_id=1, source_target_pairs={{0,8},{4,12},{8,0},{12,4},{16,24},{20,28},{24,16},{28,20},{1,9},{5... | collective-permute-start | bytes 983048 | tf_op jit(solution)/shard_map/ppermute | solution.py:131
  246.5 26.9 %collective-permute-start.59 = (f32[1,256,128]{2,1,0:T(8,128)}, f32[1,256,128]{2,1,0:T(8,128)}, u32[]{:S(2)}, u32[]{:S(2)}) collective-permute-start(f32[1,256,128]{2,1,0:T(8,128)} %fusion.10), channel_id=1, source_target_pairs={{0,16},{4,20},{8,24},{12,28},{16,0},{20,4},{24,8},{28,12},{1,17},{... | collective-permute-start | bytes 393224 | tf_op jit(solution)/shard_map/ppermute | solution.py:131
  266.7 8.7 %collective-permute-start.56 = (f32[1,208,128]{2,1,0:T(8,128)S(1)}, f32[1,208,128]{2,1,0:T(8,128)S(1)}, u32[]{:S(2)}, u32[]{:S(2)}) collective-permute-start(f32[1,208,128]{2,1,0:T(8,128)S(1)} %get-tuple-element.294), channel_id=1, source_target_pairs={{0,24},{4,28},{8,16},{12,20},{16,8},{20,12},{24,0},{28,4},{1,25},{... | collective-permute-start | bytes 319496 | tf_op jit(solution)/shard_map/ppermute | solution.py:131
  268.4 14.4 %collective-permute-start.55 = (f32[1,208,128]{2,1,0:T(8,128)S(1)}, f32[1,208,128]{2,1,0:T(8,128)S(1)}, u32[]{:S(2)}, u32[]{:S(2)}) collective-permute-start(f32[1,208,128]{2,1,0:T(8,128)S(1)} %get-tuple-element.293), channel_id=1, source_target_pairs={{0,16},{4,20},{8,24},{12,28},{16,0},{20,4},{24,8},{28,12},{1,17},{... | collective-permute-start | bytes 319496 | tf_op jit(solution)/shard_map/ppermute | solution.py:131
  269.4 13.4 %collective-permute-start.54 = (f32[1,208,128]{2,1,0:T(8,128)S(1)}, f32[1,208,128]{2,1,0:T(8,128)S(1)}, u32[]{:S(2)}, u32[]{:S(2)}) collective-permute-start(f32[1,208,128]{2,1,0:T(8,128)S(1)} %get-tuple-element.292), channel_id=1, source_target_pairs={{0,8},{4,12},{8,0},{12,4},{16,24},{20,28},{24,16},{28,20},{1,9},{5... | collective-permute-start | bytes 319496 | tf_op jit(solution)/shard_map/ppermute | solution.py:131
  273.1 12.8 %collective-permute-start.58 = (f32[1,320,128]{2,1,0:T(8,128)S(1)}, f32[1,320,128]{2,1,0:T(8,128)}, u32[]{:S(2)}, u32[]{:S(2)}) collective-permute-start(f32[1,320,128]{2,1,0:T(8,128)S(1)} %pad_maximum_fusion.20), channel_id=1, source_target_pairs={{0,16},{4,20},{8,24},{12,28},{16,0},{20,4},{24,8},{28,12},{1,17},{... | collective-permute-start | bytes 491528 | tf_op jit(solution)/shard_map/ppermute | solution.py:131
  (54 other events, 359.0 us)
where the time goes:
time: 291 us; the launch traced here: 289 us
  Pallas kernels  142 us (49%)
  starting transfers between devices  53.7 us (18%)
  waiting for transfers between devices  37.8 us (13%)
  other arithmetic  34.9 us (12%)
  local copies, waits for them, and re-layouts  19.3 us (7%)
    ppermute x23, starting transfers between devices, send(): return lax.ppermute(x, 'dp', [(i, i ^ d) for i in range(self.dp)])  31.5 us
    pallas_call x2, Pallas kernels, attention_backward(): pl.pallas_call(body, cost_estimate=cost(8), grid=(count, pairs), out_shap...  23.5 us
    ppermute x23, waiting for transfers between devices, send(): return lax.ppermute(x, 'dp', [(i, i ^ d) for i in range(self.dp)])  18.2 us
    add x11, other arithmetic, send(): sum((term[i][v * n:(v + 1) * n] for term in self.terms))  15 us
    pallas_call x2, Pallas kernels, attention_forward(): pl.pallas_call(body, cost_estimate=cost(9.5), grid=(count, pairs), out_sh...  14.9 us
    pallas_call x1, Pallas kernels, hidden_stage(): pl.pallas_call(body, cost_estimate=cost(15), grid=(steps,), out_shape=[ja...  14.5 us
    ppermute x26, waiting for transfers between devices, send(): return lax.ppermute(x, 'fsdp', [(i, i ^ f) for i in range(self.fsdp)])  14.2 us
    pallas_call x2, Pallas kernels, grad_up_stage(): pl.pallas_call(body, cost_estimate=cost(6.4), grid=(steps,), out_shape=ja...  12.9 us
  transfers between devices with their start and end apart: 60, of which 19 were waited for; matrix products, arithmetic and copies ran while one was open for 14% of the time, Pallas kernels for 38%

commit v1 on v0

--- a/solution.py
+++ b/solution.py
@@ -15,6 +15,7 @@
 BF16 = jnp.bfloat16
 LN_ROWS = 16
 TILE = 128
+ROOM = pltpu.CompilerParams(vmem_limit_bytes=23 << 20)
 SCALE = 0.05
 
 
@@ -365,6 +366,7 @@
     ]
     return pl.pallas_call(
         body,
+        compiler_params=ROOM,
         cost_estimate=cost(7.4),
         grid=(3,),
         out_shape=[jax.ShapeDtypeStruct(shape, kind) for shape, kind, _ in outs],
@@ -491,6 +493,7 @@
 
     return pl.pallas_call(
         body,
+        compiler_params=ROOM,
         cost_estimate=cost(9.5),
         grid=(count, pairs),
         out_shape=[jax.ShapeDtypeStruct((rows_all, width), F32)] * 2,
@@ -562,6 +565,7 @@
     far_out = lambda n: pl.BlockSpec((1, 2, n, 128), lambda s, h: (first + s, 0, 0, pair + h))
     return pl.pallas_call(
         body,
+        compiler_params=ROOM,
         cost_estimate=cost(8),
         grid=(count, pairs),
         out_shape=[jax.ShapeDtypeStruct((rows_all, width), F32)] * 3
@@ -589,6 +593,7 @@
     return call(
         body,
         [((rows_all, width), F32), ((rows_all, width), F32), ((rows_all, 128), F32)],
+        compiler_params=ROOM,
         cost_estimate=cost(4.3),
         in_specs=[whole()] * 4,
         out_specs=[whole()] * 3,
@@ -626,6 +631,7 @@
     cols = pl.BlockSpec((width, chunk), lambda i: (0, i))
     return pl.pallas_call(
         body,
+        compiler_params=ROOM,
         cost_estimate=cost(5),
         grid=(hidden_width // chunk,),
         out_shape=[jax.ShapeDtypeStruct((width, hidden_width), BF16)] * 2
@@ -648,18 +654,23 @@
 
     def body(me_ref, xhat_ref, ln_ref, cot_ref, d0, d1, *rest):
         refs = rest[: len(slots)]
-        hh, hl, ph, plo, wh, wl, full, nh, nl, ch, cl = rest[len(slots) :]
+        hh, hl, ph, plo, wh, wl, nth, ntl, cth, ctl, full, nh, nl, ch, cl = rest[len(slots) :]
         step = pl.program_id(0)
 
         @pl.when(step == 0)
         def _():
             assemble(full, refs, gathered, me_ref[0], me_ref[1], rows, lanes, [(0, rows, 0)])
-            n = split(xhat_ref[...] * ln_ref[2:3, :] + ln_ref[3:4, :])
-            nh[...] = n[0]
-            nl[...] = n[1]
-            c = split(cot_ref[...])
-            ch[...] = c[0]
-            cl[...] = c[1]
+            n = xhat_ref[...] * ln_ref[2:3, :] + ln_ref[3:4, :]
+            c = cot_ref[...]
+            for value, high, low in (
+                (n, nh, nl),
+                (c, ch, cl),
+                (jnp.transpose(n), nth, ntl),
+                (jnp.transpose(c), cth, ctl),
+            ):
+                halves = split(value)
+                high[...] = halves[0]
+                low[...] = halves[1]
 
         w = split(full[pl.ds(pl.multiple_of(step * chunk, chunk), chunk), :])
         wh[...] = w[0]
@@ -681,26 +692,30 @@
     act = fixed((rows_all, width))
     return pl.pallas_call(
         body,
+        compiler_params=ROOM,
         cost_estimate=cost(15),
         grid=(steps,),
         out_shape=[jax.ShapeDtypeStruct((rows_all, hidden_width), BF16)] * 4
-        + [jax.ShapeDtypeStruct((hidden_width, width), BF16)] * 2,
+        + [jax.ShapeDtypeStruct((hidden_width, width), BF16)] * 2
+        + [jax.ShapeDtypeStruct((width, rows_all), BF16)] * 4,
         in_specs=[SMEM, act, fixed((8, width)), act, down, down]
         + [fixed(x.shape) for x in slots],
-        out_specs=[cols] * 4 + [pl.BlockSpec((chunk, width), lambda i: (i, 0))] * 2,
+        out_specs=[cols] * 4
+        + [pl.BlockSpec((chunk, width), lambda i: (i, 0))] * 2
+        + [fixed((width, rows_all))] * 4,
         scratch_shapes=[pltpu.VMEM((hidden_width, width), F32)]
         + [pltpu.VMEM((rows_all, width), BF16)] * 4,
     )(me, xhat, ln, cot, dh, dl, *slots)
 
 
-def grad_down_stage(me, cot, hh, hl, plan, stream, core):
-    rows_all, width = cot.shape
+def grad_down_stage(me, cth, ctl, hh, hl, plan, stream, core):
+    width, rows_all = cth.shape
     hidden_width = hh.shape[1]
     rows, lanes = width // plan.dp, hidden_width // plan.fsdp
 
-    def body(me_ref, cot_ref, hh_ref, hl_ref, out):
+    def body(me_ref, c0, c1, h0, h1, out):
         jf = core + 2 * pl.program_id(0)
-        res = mm3(split(cot_ref[...]), (hh_ref[...], hl_ref[...]), 0, 0)
+        res = mm3((c0[...], c1[...]), (h0[...], h1[...]), 1, 0)
         for d in range(plan.dp):
             jd = me_ref[0] ^ d
             for k in range(lanes // 128):
@@ -711,15 +726,16 @@
     grid_spec = pltpu.PrefetchScalarGridSpec(
         num_scalar_prefetch=1,
         grid=(plan.fsdp // 2,),
-        in_specs=[pl.BlockSpec((rows_all, width), lambda i, m: (0, 0)), cols, cols],
+        in_specs=[pl.BlockSpec((width, rows_all), lambda i, m: (0, 0))] * 2 + [cols, cols],
         out_specs=pl.BlockSpec(stream.shape(), lambda i, m: (0, 0, 0)),
     )
     return pl.pallas_call(
         body,
-        cost_estimate=cost(5.5),
+        compiler_params=ROOM,
+        cost_estimate=cost(0.27),
         grid_spec=grid_spec,
         out_shape=jax.ShapeDtypeStruct(stream.shape(), F32),
-    )(me, cot, hh, hl)
+    )(me, cth, ctl, hh, hl)
 
 
 def half_lanes(ref, me_f, core, lanes):
@@ -730,43 +746,51 @@
     return jnp.concatenate(parts, axis=1)
 
 
-def grad_up_stage(me, xhat, ln, ph, plo, plan, stream, core):
-    rows_all, width = xhat.shape
+def half_rows(ref, me_f, core, count):
+    parts = []
+    for y in range(2):
+        start = pl.multiple_of((me_f ^ (core + 2 * y)) * count, 128)
+        parts.append(ref[pl.ds(start, count), :])
+    return jnp.concatenate(parts, axis=0)
+
+
+def grad_up_stage(me, nth, ntl, ph, plo, plan, stream, core):
+    width, rows_all = nth.shape
     hidden_width = ph.shape[1]
     rows, lanes = hidden_width // plan.dp, width // plan.fsdp
     chunk = 512
     steps = hidden_width // chunk
     per = chunk // rows
-
-    def body(me_ref, xhat_ref, ln_ref, ph_ref, pl_ref, out, full, nh, nl):
+    natural = rows % 128 == 0
+
+    def body(me_ref, n0, n1, p0, p1, out):
         step = pl.program_id(0)
-
-        @pl.when(step == 0)
-        def _():
-            full[...] = xhat_ref[...] * ln_ref[2:3, :] + ln_ref[3:4, :]
-            n = split(half_lanes(full, me_ref[1], core, lanes))
-            nh[...] = n[0]
-            nl[...] = n[1]
-
-        res = mm3((ph_ref[...], pl_ref[...]), (nh[...], nl[...]), 0, 0)
+        n = (half_rows(n0, me_ref[1], core, lanes), half_rows(n1, me_ref[1], core, lanes))
+        p = (p0[...], p1[...])
+        res = mm3(n, p, 1, 0) if natural else mm3(p, n, 0, 1)
         for i in range(per):
             jd = (step * per + i) ^ me_ref[0]
             for y in range(2):
-                value = res[i * rows : (i + 1) * rows, y * lanes : (y + 1) * lanes]
-                stream.put(out, jd, core + 2 * y, 0, value)
+                if natural:
+                    for k in range(rows // 128):
+                        at = i * rows + 128 * k
+                        value = res[y * lanes : (y + 1) * lanes, at : at + 128]
+                        stream.put(out, jd, core + 2 * y, k * lanes, value)
+                else:
+                    value = res[i * rows : (i + 1) * rows, y * lanes : (y + 1) * lanes]
+                    stream.put(out, jd, core + 2 * y, 0, value)
 
     fixed = lambda shape: pl.BlockSpec(shape, lambda i: (0,) * len(shape))
     cols = pl.BlockSpec((rows_all, chunk), lambda i: (0, i))
     return pl.pallas_call(
         body,
-        cost_estimate=cost(6.4),
+        compiler_params=ROOM,
+        cost_estimate=cost(0.32),
         grid=(steps,),
         out_shape=jax.ShapeDtypeStruct(stream.shape(), F32),
-        in_specs=[SMEM, fixed((rows_all, width)), fixed((8, width)), cols, cols],
+        in_specs=[SMEM] + [fixed((width, rows_all))] * 2 + [cols, cols],
         out_specs=fixed(stream.shape()),
-        scratch_shapes=[pltpu.VMEM((rows_all, width), F32)]
-        + [pltpu.VMEM((rows_all, 2 * lanes), BF16)] * 2,
-    )(me, xhat, ln, ph, plo)
+    )(me, nth, ntl, ph, plo)
 
 
 def norm_back(e, gain, xhat, inv):
@@ -792,6 +816,7 @@
     act = pl.BlockSpec((rows_all, width), lambda i: (0, 0))
     return pl.pallas_call(
         body,
+        compiler_params=ROOM,
         cost_estimate=cost(8),
         grid=(steps,),
         out_shape=jax.ShapeDtypeStruct((rows_all, width), F32),
@@ -827,6 +852,7 @@
     act = fixed((rows_all, width))
     return pl.pallas_call(
         body,
+        compiler_params=ROOM,
         cost_estimate=cost(8.5),
         grid=(steps,),
         out_shape=[
@@ -860,6 +886,7 @@
         body,
         [((rows_all, width), F32), (stream.shape(), F32), (stream.shape(), F32)],
         [pltpu.VMEM((rows_all, width), F32)],
+        compiler_params=ROOM,
         cost_estimate=cost(5),
         in_specs=[SMEM] + [whole()] * 4,
         out_specs=[whole()] * 3,
@@ -893,6 +920,7 @@
     return call(
         body,
         [((rows_all, 3 * width), BF16)] * 2 + [((3 * width, 128), F32)],
+        compiler_params=ROOM,
         cost_estimate=cost(4.5),
         in_specs=[whole()] * 7,
         out_specs=[whole()] * 3,
@@ -909,6 +937,7 @@
     return call(
         body,
         [((rows_all, width), F32)],
+        compiler_params=ROOM,
         cost_estimate=cost(7.4),
         in_specs=[whole()] * 8,
         out_specs=[whole()],
@@ -955,6 +984,7 @@
     down = lambda n: pl.BlockSpec((block, n), lambda i: (i, 0))
     return pl.pallas_call(
         body,
+        compiler_params=ROOM,
         cost_estimate=cost(0.25),
         grid=(steps,),
         out_shape=[
@@ -1003,6 +1033,7 @@
     extra = [(name,) for name in plan.extra]
     qkv_piece = jnp.concatenate([placed, w_qkv.T], axis=0)
     up_piece = w_up.T
+    qkv_piece = after(qkv_piece, me)
     qkv_in, down_in, up_in = (Gather(plan, p) for p in (qkv_piece, down_piece, up_piece))
     tok = tokens.reshape(rows_all, width)
     cot = cotangent.reshape(rows_all, width)
@@ -1021,8 +1052,8 @@
         down_in.stage([group])
     far_segments = swap(jnp.stack([segments, after(near, gate)]), 2)
     bias = score_bias(segments, near, far_segments[0], far_segments[1])
-    gate = (qkv_in.came(), down_in.came(), far_segments)
-    qkv_in.stage([("y",), ("x",)], gate)
+    qkv_in.stage([("y",), ("x",)], qkv_in.came())
+    gate = (down_in.came(), far_segments)
     down_in.stage([("z",)], gate)
     up_in.send([("w",)], gate)
     for group in extra:
@@ -1062,7 +1093,7 @@
     middle, xhat2, inv2 = middle_stage(tok, attended, oh, ol)
     gate = (middle, up_in.came(), cores)
     cores = up_in.share(False, gate)
-    hh, hl, ph, plo, uh, ul = hidden_stage(
+    hh, hl, ph, plo, uh, ul, nth, ntl, cth, ctl = hidden_stage(
         me, after(xhat2, cores), ln, cot, dh, dl, up_in, plan
     )
 
@@ -1074,14 +1105,14 @@
     qkv = Stream(plan, rows_qkv, double)
     down_sum, up_sum, qkv_sum = Reduce(plan, single), Reduce(plan, single), Reduce(plan, double)
 
-    away = grad_down_stage(me, cot, hh, hl, plan, down, 1)
+    away = grad_down_stage(me, cth, ctl, hh, hl, plan, down, 1)
     down_core = down_sum.begin(away)
-    away = grad_up_stage(me, after(xhat2, away), ln, ph, plo, plan, up, 1)
+    away = grad_up_stage(me, after(nth, away), ntl, ph, plo, plan, up, 1)
     up_core = up_sum.begin(away)
-    keep = grad_down_stage(me, after(cot, away), hh, hl, plan, down, 0)
+    keep = grad_down_stage(me, after(cth, away), ctl, hh, hl, plan, down, 0)
     down_sum.keep(keep)
     sent = down_sum.send(keep, down_core)
-    keep = grad_up_stage(me, after(xhat2, sent), ln, ph, plo, plan, up, 0)
+    keep = grad_up_stage(me, after(nth, sent), ntl, ph, plo, plan, up, 0)
     up_sum.keep(keep)
     gm, gln = middle_grad_stage(after(cot, keep, up_core), xhat2, inv2, ln, ph, plo, uh, ul)
     gmix, away, keep = mixture_grad_stage(me, gm, attended, oh, ol, plan, out)
@@ -1129,6 +1160,10 @@
     sums = (sums + plan.send(sums, ("c",))).reshape(4, width)
     (g_down,), (g_up, g_out), (g_qkv,) = (t.total() for t in (down_sum, up_sum, qkv_sum))
     mine = lax.dynamic_slice(sums, (0, me_d * share), (4, share))
+    if rows_up % 128 == 0:
+        g_up = g_up.reshape(-1, width // fsdp, 128).transpose(1, 0, 2).reshape(-1, rows_up)
+    else:
+        g_up = g_up.T
     g_down = g_down.reshape(chunks, rows_d, 128).transpose(0, 2, 1).reshape(-1, rows_d)
     shape = tokens.shape
     return (
@@ -1140,7 +1175,7 @@
         g_out.T,
         mine[2],
         mine[3],
-        g_up.T,
+        g_up,
         g_down,
     )
 

time: 291 us -> 262 us (0.900)
  Pallas kernels: 142 us -> 88.3 us
  waiting for transfers between devices: 37.8 us -> 63.8 us
  local copies, waits for them, and re-layouts: 19.3 us -> 30.3 us
  other arithmetic: 34.9 us -> 26.1 us
    pallas_call x16, Pallas kernels: 127 us -> 83.5 us  [the longest x2 19.6 us: attention_backward(): pl.pallas_call(body, compiler_params=ROOM, cost_estimate=cost(8), grid=(c...]
    ppermute x26, waiting for transfers between devices: 14.2 us -> 33.1 us  [send(): return lax.ppermute(x, 'fsdp', [(i, i ^ f) for i in range(self.fsdp)])]
    unnamed x100 -> x133, local copies, waits for them, and re-layouts: 5.93 us -> 14.6 us
    ppermute x23, waiting for transfers between devices: 18.2 us -> 24.2 us  [send(): return lax.ppermute(x, 'dp', [(i, i ^ d) for i in range(self.dp)])]
    add x11, other arithmetic: 15 us -> 9.53 us  [send(): sum((term[i][v * n:(v + 1) * n] for term in self.terms))]
    pallas_call x1, Pallas kernels: 4.9 us -> 1.22 us  [packed_grad_stage(): call(body, [((rows_all, 3 * width), BF16)] * 2 + [((3 * width, 128), F32)...]
    select_n x5, other arithmetic: 1.02 us -> 4.57 us  [score_bias(): parts.append(jnp.where(ok, np.float32(level * np.log(2.0)), MASKED))]
    pallas_call x1, Pallas kernels: 4.3 us -> 1.22 us  [middle_stage(): call(body, [((rows_all, width), F32), ((rows_all, width), F32), ((rows_al...]
  transfers between devices with their start and end apart: 60 -> 60, of which waited for: 19 -> 24; matrix products, arithmetic and copies ran while one was open for 14% -> 14% of each run, Pallas kernels for 38% -> 26%
where the time goes in v1:
time: 262 us; the launch traced here: 261 us
  Pallas kernels  88.3 us (34%)
  waiting for transfers between devices  63.8 us (24%)
  starting transfers between devices  50.9 us (19%)
  local copies, waits for them, and re-layouts  30.3 us (12%)
  other arithmetic  26.1 us (10%)
    ppermute x26, waiting for transfers between devices, send(): return lax.ppermute(x, 'fsdp', [(i, i ^ f) for i in range(self.fsdp)])  33.1 us
    ppermute x23, starting transfers between devices, send(): return lax.ppermute(x, 'dp', [(i, i ^ d) for i in range(self.dp)])  29.5 us
    ppermute x23, waiting for transfers between devices, send(): return lax.ppermute(x, 'dp', [(i, i ^ d) for i in range(self.dp)])  24.2 us
    pallas_call x2, Pallas kernels, attention_backward(): pl.pallas_call(body, compiler_params=ROOM, cost_estimate=cost(8), grid=(c...  19.6 us
    unnamed x133, local copies, waits for them, and re-layouts  14.6 us
    pallas_call x1, Pallas kernels, hidden_stage(): pl.pallas_call(body, compiler_params=ROOM, cost_estimate=cost(15), grid=(...  11.6 us
    pallas_call x2, Pallas kernels, attention_forward(): pl.pallas_call(body, compiler_params=ROOM, cost_estimate=cost(9.5), grid=...  11.3 us
    ppermute x26, starting transfers between devices, send(): return lax.ppermute(x, 'fsdp', [(i, i ^ f) for i in range(self.fsdp)])  11 us
  transfers between devices with their start and end apart: 60, of which 24 were waited for; matrix products, arithmetic and copies ran while one was open for 14% of the time, Pallas kernels for 26%

profile of v1, /device:TPU:0, one launch (start us, length us, event | category | flops | bytes accessed | tf_op | source)
XLA Modules:
  0.0 261.1 jit_solution(4182234786946180165)
XLA Ops:
  2.7 3.0 %collective-permute-start = (f32[1,208,128]{2,1,0:T(8,128)S(1)}, f32[1,208,128]{2,1,0:T(8,128)S(1)}, u32[]{:S(2)}, u32[]{:S(2)}) collective-permute-start(f32[1,208,128]{2,1,0:T(8,128)S(1)} %bitcast.119), channel_id=1, source_target_pairs={{0,8},{4,12},{8,0},{12,4},{16,24},{20,28},{24,16},{28,20},{1,9},{5... | collective-permute-start | bytes 319496 | tf_op jit(solution)/shard_map/ppermute | solution.py:132
  5.7 2.6 collective-permute-start.1
  19.5 2.0 collective-permute-start.7
  21.5 1.5 collective-permute-start.9
  23.1 1.7 collective-permute-start.3
  26.0 5.3 %collective-permute-done.4 = f32[4,96,128]{2,1,0:T(8,128)S(1)} collective-permute-done((f32[4,96,128]{2,1,0:T(8,128)S(1)}, f32[4,96,128]{2,1,0:T(8,128)S(1)}, u32[]{:S(2)}, u32[]{:S(2)}) %collective-permute-start.4) | collective-permute-done | bytes 196640 | tf_op jit(solution)/shard_map/ppermute | solution.py:134
  33.5 2.5 collective-permute-start.10
  37.3 1.7 concatenate.95.outer_bias
  39.0 5.7 %collective-permute-done.11 = f32[1,256,128]{2,1,0:T(8,128)S(1)} collective-permute-done((f32[1,256,128]{2,1,0:T(8,128)S(1)}, f32[1,256,128]{2,1,0:T(8,128)S(1)}, u32[]{:S(2)}, u32[]{:S(2)}) %collective-permute-start.11) | collective-permute-done | bytes 131104 | tf_op jit(solution)/shard_map/ppermute | solution.py:132
  49.1 1.5 collective-permute-start.17
  52.5 6.0 %shard_map.276 = (f32[512,1536]{1,0:T(8,128)S(1)}, bf16[1536,512]{1,0:T(8,128)(2,1)S(1)}, bf16[1536,512]{1,0:T(8,128)(2,1)S(1)}, f32[512,512]{1,0:T(8,128)S(1)},...) custom-call(s32[2]{0:T(128)S(1)} %pad_add_fusion.3.me_ref, ...), custom_call_target="tpu_custom_call" | custom-call | flops 333000000 | bytes 925000 | tf_op jit(solution)/shard_map/pallas_call | solution.py:367
  60.6 1.6 collective-permute-start.19
  65.7 5.7 %shard_map.277 = (f32[512,512]{1,0:T(8,128)S(1)}, f32[512,512]{1,0:T(8,128)S(1)}) custom-call(f32[512,1536]{1,0:T(8,128)S(1)} %get-tuple-element.154.q.k.v, f32[512,1536]{1,0:T(8,128)S(1)} %get-tuple-element.154.q.k.v, f32[512,1536]{1,0:T(8,128)S(1)} %get-tuple-element.154.q.k.v, f32[2,2,32,512]{3,2,1,0:T(8,128)S(1)} %constant_dynamic-update-slice_fusion.2.fk.fv, ...), custom_call_target="tpu_custom_call" | custom-call | flops 427500000 | bytes 1187500 | tf_op jit(solution)/shard_map/pallas_call | solution.py:494
  71.4 7.7 %collective-permute-done.23.rest_6_ = f32[8,160,128]{2,1,0:T(8,128)S(1)} collective-permute-done((f32[8,160,128]{2,1,0:T(8,128)S(1)}, f32[8,160,128]{2,1,0:T(8,128)S(1)}, u32[]{:S(2)}, u32[]{:S(2)}) %collective-permute-start.23) | collective-permute-done | bytes 655392 | tf_op jit(solution)/shard_map/ppermute | solution.py:132
  82.0 5.6 %shard_map.278 = (f32[512,512]{1,0:T(8,128)S(1)}, f32[512,512]{1,0:T(8,128)S(1)}) custom-call(f32[512,1536]{1,0:T(8,128)S(1)} %get-tuple-element.154.q.k.v, f32[512,1536]{1,0:T(8,128)S(1)} %get-tuple-element.154.q.k.v, f32[512,1536]{1,0:T(8,128)S(1)} %get-tuple-element.154.q.k.v, ...), custom_call_target="tpu_custom_call", output_to_operand_aliasing={{0}: (10, {}), {1}: (11, {})} | custom-call | flops 427500000 | bytes 1187500 | tf_op jit(solution)/shard_map/pallas_call | solution.py:494
  91.6 2.4 shard_map.279
  96.4 6.0 %collective-permute-done.30.rest_4_ = f32[8,128,128]{2,1,0:T(8,128)S(1)} collective-permute-done((f32[8,128,128]{2,1,0:T(8,128)S(1)}, f32[8,128,128]{2,1,0:T(8,128)S(1)}, u32[]{:S(2)}, u32[]{:S(2)}) %collective-permute-start.30) | collective-permute-done | bytes 524320 | tf_op jit(solution)/shard_map/ppermute | solution.py:134
  105.3 11.6 %shard_map.281 = (bf16[512,2048]{1,0:T(8,128)(2,1)S(1)}, bf16[512,2048]{1,0:T(8,128)(2,1)S(1)}, bf16[512,2048]{1,0:T(8,128)(2,1)S(1)}, bf16[512,2048]{1,0:T(8,12...) custom-call(s32[2]{0:T(128)S(1)} %pad_add_fusion.3.me_ref, ...), custom_call_target="tpu_custom_call" | custom-call | flops 675000000 | bytes 1875000 | tf_op jit(solution)/shard_map/pallas_call | solution.py:693
  116.9 2.7 %shard_map.282 = f32[16,256,128]{2,1,0:T(8,128)S(1)} custom-call(s32[2]{0:T(128)S(1)} %pad_add_fusion.3.me_ref, bf16[512,512]{1,0:T(8,128)(2,1)S(1)} %get-tuple-element.185.c0, bf16[512,512]{1,0:T(8,128)(2,1)S(1)} %get-tuple-element.178.c1, bf16[512,2048]{1,0:T(8,128)(2,1)S(1)} %get-tuple-element.179.h0, bf16[512,2048]{1,0:T(8,128)(2,1)S(1)} %get-tuple-element.180.h1), custom_call_target="tpu_custom_call" | custom-call | flops 12150000 | bytes 33750 | tf_op jit(solution)/shard_map/pallas_call | solution.py:732
  119.9 3.2 %shard_map.283 = f32[16,256,128]{2,1,0:T(8,128)S(1)} custom-call(s32[2]{0:T(128)S(1)} %pad_add_fusion.3.me_ref, bf16[512,512]{1,0:T(8,128)(2,1)S(1)} %get-tuple-element.187.n0, bf16[512,512]{1,0:T(8,128)(2,1)S(1)} %get-tuple-element.182.n1, bf16[512,2048]{1,0:T(8,128)(2,1)S(1)} %get-tuple-element.183.p0, bf16[512,2048]{1,0:T(8,128)(2,1)S(1)} %get-tuple-element.184.p1), custom_call_target="tpu_custom_call" | custom-call | flops 14400000 | bytes 40000 | tf_op jit(solution)/shard_map/pallas_call | solution.py:785
  123.5 2.7 %shard_map.284 = f32[16,256,128]{2,1,0:T(8,128)S(1)} custom-call(s32[2]{0:T(128)S(1)} %pad_add_fusion.3.me_ref, bf16[512,512]{1,0:T(8,128)(2,1)S(1)} %get-tuple-element.185.c0, bf16[512,512]{1,0:T(8,128)(2,1)S(1)} %get-tuple-element.178.c1, bf16[512,2048]{1,0:T(8,128)(2,1)S(1)} %get-tuple-element.179.h0, bf16[512,2048]{1,0:T(8,128)(2,1)S(1)} %get-tuple-element.180.h1), custom_call_target="tpu_custom_call" | custom-call | flops 12150000 | bytes 33750 | tf_op jit(solution)/shard_map/pallas_call | solution.py:732
  127.6 1.9 collective-permute-start.40
  131.1 3.2 %shard_map.285 = f32[16,256,128]{2,1,0:T(8,128)S(1)} custom-call(s32[2]{0:T(128)S(1)} %pad_add_fusion.3.me_ref, bf16[512,512]{1,0:T(8,128)(2,1)S(1)} %get-tuple-element.187.n0, bf16[512,512]{1,0:T(8,128)(2,1)S(1)} %get-tuple-element.182.n1, bf16[512,2048]{1,0:T(8,128)(2,1)S(1)} %get-tuple-element.183.p0, bf16[512,2048]{1,0:T(8,128)(2,1)S(1)} %get-tuple-element.184.p1), custom_call_target="tpu_custom_call" | custom-call | flops 14400000 | bytes 40000 | tf_op jit(solution)/shard_map/pallas_call | solution.py:785
  134.3 5.0 %shard_map.286 = (f32[512,512]{1,0:T(8,128)S(1)}, f32[8,512]{1,0:T(8,128)S(1)}) custom-call(f32[512,512]{1,0:T(8,128)S(1)} %bitcast.116, f32[512,512]{1,0:T(8,128)S(1)} %copy-done.26, f32[512,128]{1,0:T(8,128)S(1)} %get-tuple-element.189.inv_ref, f32[8,512]{1,0:T(8,128)S(1)} %get-tuple-element.173.ln_ref.ln_r, bf16[512,2048]{1,0:T(8,128)(2,1)S(1)} %get-tuple-element.183.p0, ...), custom_call_target="tpu_custom_call" | custom-call | flops 382500000 | bytes 1062500 | tf_op jit(solution)/shard_map/pallas_call | solution.py:853
  139.3 2.4 shard_map.287
  141.8 1.5 collective-permute-done.40
  143.3 10.4 %collective-permute-done.39 = f32[4,256,128]{2,1,0:T(8,128)S(1)} collective-permute-done((f32[4,256,128]{2,1,0:T(8,128)S(1)}, f32[4,256,128]{2,1,0:T(8,128)S(1)}, u32[]{:S(2)}, u32[]{:S(2)}) %collective-permute-start.39) | collective-permute-done | bytes 524320 | tf_op jit(solution)/shard_map/ppermute | solution.py:134
  153.8 1.9 collective-permute-done.42
  162.2 9.8 %shard_map.288 = (f32[512,512]{1,0:T(8,128)S(1)}, f32[512,512]{1,0:T(8,128)S(1)}, f32[512,512]{1,0:T(8,128)S(1)}, f32[2,2,16,512]{3,2,1,0:T(8,128)S(1)}, f32[2,2...) custom-call(f32[512,1536]{1,0:T(8,128)S(1)} %get-tuple-element.154.q.k.v, f32[512,1536]{1,0:T(8,128)S(1)} %get-tuple-element.154.q.k.v, ...), custom_call_target="tpu_custom_call" | custom-call | flops 360000000 | bytes 1000000 | tf_op jit(solution)/shard_map/pallas_call | solution.py:566
  173.1 9.8 %shard_map.289 = (f32[512,512]{1,0:T(8,128)S(1)}, f32[512,512]{1,0:T(8,128)S(1)}, f32[512,512]{1,0:T(8,128)S(1)}, f32[2,2,16,512]{3,2,1,0:T(8,128)S(1)}, f32[2,2...) custom-call(f32[512,1536]{1,0:T(8,128)S(1)} %get-tuple-element.154.q, ...), custom_call_target="tpu_custom_call", output_to_operand_aliasing={{0}: (13, {}), {1}: (14, {}), {2}: (15, {}), {3}: (16, {}),... | custom-call | flops 360000000 | bytes 1000000 | tf_op jit(solution)/shard_map/pallas_call | solution.py:566
  183.0 5.3 %collective-permute-done.44 = f32[4,320,128]{2,1,0:T(8,128)S(1)} collective-permute-done((f32[4,320,128]{2,1,0:T(8,128)S(1)}, f32[4,320,128]{2,1,0:T(8,128)S(1)}, u32[]{:S(2)}, u32[]{:S(2)}) %collective-permute-start.44) | collective-permute-done | bytes 655392 | tf_op jit(solution)/shard_map/ppermute | solution.py:134
  190.1 2.8 %collective-permute-done.47.g5a_r = f32[2,2,8,512]{3,2,1,0:T(8,128)S(1)} collective-permute-done((f32[2,2,8,512]{3,2,1,0:T(8,128)S(1)}, f32[2,2,8,512]{3,2,1,0:T(8,128)S(1)}, u32[]{:S(2)}, u32[]{:S(2)}) %collective-permute-start.47) | collective-permute-done | bytes 65568 | tf_op jit(solution)/shard_map/ppermute | solution.py:1003
  195.2 3.7 %shard_map.291 = (f32[16,192,128]{2,1,0:T(8,128)}, f32[8,512]{1,0:T(8,128)S(1)}) custom-call(s32[2]{0:T(128)S(1)} %pad_add_fusion.3.me_ref, bf16[512,1536]{1,0:T(8,128)(2,1)S(1)} %get-tuple-element.217.gph_r, bf16[512,1536]{1,0:T(8,128)(2,1)S(1)} %get-tuple-element.218.gpl_r, f32[1536,128]{1,0:T(8,128)S(1)} %get-tuple-element.222.col_r, ...), custom_call_target="tpu_custom_call" | custom-call | flops 11250000 | bytes 31250 | tf_op jit(solution)/shard_map/pallas_call | solution.py:985
  199.9 2.6 shard_map.292
  203.7 1.7 slice_add_fusion.6
  206.5 1.7 collective-permute-start.52
  213.7 2.3 collective-permute-start.59
  216.0 1.4 copy-done.5
  217.4 1.4 copy-done.7
  218.8 1.4 copy-done.9
  220.2 1.4 copy-done.11
  223.8 3.8 %shard_map.293 = f32[512,512]{1,0:T(8,128)} custom-call(bf16[512,1536]{1,0:T(8,128)(2,1)S(1)} %copy-done.9, bf16[512,1536]{1,0:T(8,128)(2,1)S(1)} %copy-done.11, bf16[1536,512]{1,0:T(8,128)(2,1)S(1)} %copy-done.5, bf16[1536,512]{1,0:T(8,128)(2,1)S(1)} %copy-done.7, f32[512,512]{1,0:T(8,128)S(1)} %copy-done.13, f32[512,128]{1,0:T(8,128)S(1)} %copy-done.34, ...), custom_call_target="tpu_custom_call" | custom-call | flops 333000000 | bytes 925000 | tf_op jit(solution)/shard_map/pallas_call | solution.py:937
  227.6 5.8 %shard_map.294 = f32[512,512]{1,0:T(8,128)} custom-call(f32[512,512]{1,0:T(8,128)S(1)} %copy-done.31, bf16[512,2048]{1,0:T(8,128)(2,1)S(1)} %get-tuple-element.179.h0, bf16[512,2048]{1,0:T(8,128)(2,1)S(1)} %copy-done.3, bf16[512,2048]{1,0:T(8,128)(2,1)S(1)} %copy-done.15, bf16[512,2048]{1,0:T(8,128)(2,1)S(1)} %copy-done.17), custom_call_target="tpu_custom_call" | custom-call | flops 360000000 | bytes 1000000 | tf_op jit(solution)/shard_map/pallas_call | solution.py:817
  237.2 1.4 fusion.14
  239.9 1.7 collective-permute-start.55
  247.1 7.8 %collective-permute-done.55 = f32[1,208,128]{2,1,0:T(8,128)S(1)} collective-permute-done((f32[1,208,128]{2,1,0:T(8,128)S(1)}, f32[1,208,128]{2,1,0:T(8,128)S(1)}, u32[]{:S(2)}, u32[]{:S(2)}) %collective-permute-start.55) | collective-permute-done | bytes 106528 | tf_op jit(solution)/shard_map/ppermute | solution.py:132
  255.6 1.7 fusion.10
  259.7 1.4 fusion.16
  (336 shorter events, 81.7 us)
Async XLA Ops:
  2.7 16.8 %collective-permute-start = (f32[1,208,128]{2,1,0:T(8,128)S(1)}, f32[1,208,128]{2,1,0:T(8,128)S(1)}, u32[]{:S(2)}, u32[]{:S(2)}) collective-permute-start(f32[1,208,128]{2,1,0:T(8,128)S(1)} %bitcast.119), channel_id=1, source_target_pairs={{0,8},{4,12},{8,0},{12,4},{16,24},{20,28},{24,16},{28,20},{1,9},{5... | collective-permute-start | bytes 319496 | tf_op jit(solution)/shard_map/ppermute | solution.py:132
  5.7 13.8 %collective-permute-start.1 = (f32[1,208,128]{2,1,0:T(8,128)S(1)}, f32[1,208,128]{2,1,0:T(8,128)S(1)}, u32[]{:S(2)}, u32[]{:S(2)}) collective-permute-start(f32[1,208,128]{2,1,0:T(8,128)S(1)} %bitcast.120), channel_id=1, source_target_pairs={{0,16},{4,20},{8,24},{12,28},{16,0},{20,4},{24,8},{28,12},{1,17},{... | collective-permute-start | bytes 319496 | tf_op jit(solution)/shard_map/ppermute | solution.py:132
  8.3 11.2 %collective-permute-start.2 = (f32[1,208,128]{2,1,0:T(8,128)S(1)}, f32[1,208,128]{2,1,0:T(8,128)S(1)}, u32[]{:S(2)}, u32[]{:S(2)}) collective-permute-start(f32[1,208,128]{2,1,0:T(8,128)S(1)} %bitcast.121), channel_id=1, source_target_pairs={{0,24},{4,28},{8,16},{12,20},{16,8},{20,12},{24,0},{28,4},{1,25},{... | collective-permute-start | bytes 319496 | tf_op jit(solution)/shard_map/ppermute | solution.py:132
  8.3 9.9 %collective-permute-start.8 = (s32[2,256]{1,0:T(2,128)}, s32[2,256]{1,0:T(2,128)S(1)}, u32[]{:S(2)}, u32[]{:S(2)}) collective-permute-start(s32[2,256]{1,0:T(2,128)} %param.22), channel_id=1, source_target_pairs={{0,1},{1,0},{2,3},{3,2},{4,5},{5,4},{6,7},{7,6},{8,9},{9,8},{10,11... | collective-permute-start | bytes 6152 | tf_op jit(solution)/shard_map/ppermute | solution.py:1003
  19.5 13.3 %collective-permute-start.7 = (f32[1,320,128]{2,1,0:T(8,128)S(1)}, f32[1,320,128]{2,1,0:T(8,128)S(1)}, u32[]{:S(2)}, u32[]{:S(2)}) collective-permute-start(f32[1,320,128]{2,1,0:T(8,128)S(1)} %maximum_bitcast_fusion), channel_id=1, source_target_pairs={{0,16},{4,20},{8,24},{12,28},{16,0},{20,4},{24,8},{28,12},{1,17},{... | collective-permute-start | bytes 491528 | tf_op jit(solution)/shard_map/ppermute | solution.py:132
  23.1 8.2 %collective-permute-start.3 = (f32[4,112,128]{2,1,0:T(8,128)S(1)}, f32[4,112,128]{2,1,0:T(8,128)S(1)}, u32[]{:S(2)}, u32[]{:S(2)}) collective-permute-start(f32[4,112,128]{2,1,0:T(8,128)S(1)} %slice.596), channel_id=1, source_target_pairs={{0,4},{4,0},{8,12},{12,8},{16,20},{20,16},{24,28},{28,24},{1,5},{5... | collective-permute-start | bytes 688136 | tf_op jit(solution)/shard_map/ppermute | solution.py:132
  24.7 6.5 %collective-permute-start.4 = (f32[4,96,128]{2,1,0:T(8,128)S(1)}, f32[4,96,128]{2,1,0:T(8,128)S(1)}, u32[]{:S(2)}, u32[]{:S(2)}) collective-permute-start(f32[4,96,128]{2,1,0:T(8,128)S(1)} %pad_maximum_fusion.16), channel_id=1, source_target_pairs={{0,2},{1,3},{2,0},{3,1},{4,6},{5,7},{6,4},{7,5},{8,10},{9,11},{10,... | collective-permute-start | bytes 589832 | tf_op jit(solution)/shard_map/ppermute | solution.py:134
  31.3 14.2 %collective-permute-start.5 = (f32[8,112,128]{2,1,0:T(8,128)S(1)}, f32[8,112,128]{2,1,0:T(8,128)S(1)}, u32[]{:S(2)}, u32[]{:S(2)}) collective-permute-start(f32[8,112,128]{2,1,0:T(8,128)S(1)} %pad_maximum_fusion.10.rest_0_), channel_id=1, source_target_pairs={{0,2},{1,3},{2,0},{3,1},{4,6},{5,7},{6,4},{7,5},{8,10},{9,11},{10,... | collective-permute-start | bytes 1376264 | tf_op jit(solution)/shard_map/ppermute | solution.py:134
  31.9 13.6 %collective-permute-start.6 = (f32[8,96,128]{2,1,0:T(8,128)S(1)}, f32[8,96,128]{2,1,0:T(8,128)}, u32[]{:S(2)}, u32[]{:S(2)}) collective-permute-start(f32[8,96,128]{2,1,0:T(8,128)S(1)} %pad_maximum_fusion.12.rest_2_), channel_id=1, source_target_pairs={{0,4},{4,0},{8,12},{12,8},{16,20},{20,16},{24,28},{28,24},{1,5},{5... | collective-permute-start | bytes 1179656 | tf_op jit(solution)/shard_map/ppermute | solution.py:132
  33.5 12.0 %collective-permute-start.10 = (f32[2,320,128]{2,1,0:T(8,128)}, f32[2,320,128]{2,1,0:T(8,128)}, u32[]{:S(2)}, u32[]{:S(2)}) collective-permute-start(f32[2,320,128]{2,1,0:T(8,128)} %pad_maximum_fusion.13), channel_id=1, source_target_pairs={{0,8},{4,12},{8,0},{12,4},{16,24},{20,28},{24,16},{28,20},{1,9},{5... | collective-permute-start | bytes 983048 | tf_op jit(solution)/shard_map/ppermute | solution.py:132
  36.1 8.6 %collective-permute-start.11 = (f32[1,256,128]{2,1,0:T(8,128)S(1)}, f32[1,256,128]{2,1,0:T(8,128)S(1)}, u32[]{:S(2)}, u32[]{:S(2)}) collective-permute-start(f32[1,256,128]{2,1,0:T(8,128)S(1)} %bitcast.125), channel_id=1, source_target_pairs={{0,16},{4,20},{8,24},{12,28},{16,0},{20,4},{24,8},{28,12},{1,17},{... | collective-permute-start | bytes 393224 | tf_op jit(solution)/shard_map/ppermute | solution.py:132
  49.1 10.2 %collective-permute-start.17 = (f32[4,160,128]{2,1,0:T(8,128)S(1)}, f32[4,160,128]{2,1,0:T(8,128)S(1)}, u32[]{:S(2)}, u32[]{:S(2)}) collective-permute-start(f32[4,160,128]{2,1,0:T(8,128)S(1)} %get-tuple-element.143), channel_id=1, source_target_pairs={{0,2},{1,3},{2,0},{3,1},{4,6},{5,7},{6,4},{7,5},{8,10},{9,11},{10,... | collective-permute-start | bytes 983048 | tf_op jit(solution)/shard_map/ppermute | solution.py:134
  50.6 9.5 %collective-permute-start.16 = (f32[4,160,128]{2,1,0:T(8,128)S(1)}, f32[4,160,128]{2,1,0:T(8,128)S(1)}, u32[]{:S(2)}, u32[]{:S(2)}) collective-permute-start(f32[4,160,128]{2,1,0:T(8,128)S(1)} %get-tuple-element.142), channel_id=1, source_target_pairs={{0,4},{4,0},{8,12},{12,8},{16,20},{20,16},{24,28},{28,24},{1,5},{5... | collective-permute-start | bytes 983048 | tf_op jit(solution)/shard_map/ppermute | solution.py:132
  51.5 7.9 %collective-permute-start.18 = (f32[2,256,128]{2,1,0:T(8,128)S(1)}, f32[2,256,128]{2,1,0:T(8,128)S(1)}, u32[]{:S(2)}, u32[]{:S(2)}) collective-permute-start(f32[2,256,128]{2,1,0:T(8,128)S(1)} %pad_maximum_fusion.15), channel_id=1, source_target_pairs={{0,8},{4,12},{8,0},{12,4},{16,24},{20,28},{24,16},{28,20},{1,9},{5... | collective-permute-start | bytes 786440 | tf_op jit(solution)/shard_map/ppermute | solution.py:132
  60.1 4.9 %collective-permute-start.20 = (f32[2,2,8,512]{3,2,1,0:T(8,128)S(1)}, f32[2,2,8,512]{3,2,1,0:T(8,128)S(1)}, u32[]{:S(2)}, u32[]{:S(2)}) collective-permute-start(f32[2,2,8,512]{3,2,1,0:T(8,128)S(1)} %get-tuple-element.146), channel_id=1, source_target_pairs={{0,2},{1,3},{2,0},{3,1},{4,6},{5,7},{6,4},{7,5},{8,10},{9,11},{10,... | collective-permute-start | bytes 196616 | tf_op jit(solution)/shard_map/ppermute | solution.py:1003
  62.3 16.7 %collective-permute-start.23 = (f32[8,160,128]{2,1,0:T(8,128)S(1)}, f32[8,160,128]{2,1,0:T(8,128)S(1)}, u32[]{:S(2)}, u32[]{:S(2)}) collective-permute-start(f32[8,160,128]{2,1,0:T(8,128)S(1)} %pad_maximum_fusion.4.rest_2_), channel_id=1, source_target_pairs={{0,4},{4,0},{8,12},{12,8},{16,20},{20,16},{24,28},{28,24},{1,5},{5... | collective-permute-start | bytes 1966088 | tf_op jit(solution)/shard_map/ppermute | solution.py:132
  63.3 16.5 %collective-permute-start.22 = (f32[8,160,128]{2,1,0:T(8,128)S(1)}, f32[8,160,128]{2,1,0:T(8,128)S(1)}, u32[]{:S(2)}, u32[]{:S(2)}) collective-permute-start(f32[8,160,128]{2,1,0:T(8,128)S(1)} %pad_maximum_fusion.3.rest_0_), channel_id=1, source_target_pairs={{0,2},{1,3},{2,0},{3,1},{4,6},{5,7},{6,4},{7,5},{8,10},{9,11},{10,... | collective-permute-start | bytes 1966088 | tf_op jit(solution)/shard_map/ppermute | solution.py:134
  65.1 14.7 %collective-permute-start.24 = (f32[8,160,128]{2,1,0:T(8,128)S(1)}, f32[8,160,128]{2,1,0:T(8,128)S(1)}, u32[]{:S(2)}, u32[]{:S(2)}) collective-permute-start(f32[8,160,128]{2,1,0:T(8,128)S(1)} %pad_maximum_fusion.3.rest_0_), channel_id=1, source_target_pairs={{0,1},{1,0},{2,3},{3,2},{4,5},{5,4},{6,7},{7,6},{8,9},{9,8},{10,11... | collective-permute-start | bytes 1966088 | tf_op jit(solution)/shard_map/ppermute | solution.py:134
  65.6 14.2 %collective-permute-start.25 = (f32[8,160,128]{2,1,0:T(8,128)S(1)}, f32[8,160,128]{2,1,0:T(8,128)S(1)}, u32[]{:S(2)}, u32[]{:S(2)}) collective-permute-start(f32[8,160,128]{2,1,0:T(8,128)S(1)} %pad_maximum_fusion.4.rest_2_), channel_id=1, source_target_pairs={{0,1},{1,0},{2,3},{3,2},{4,5},{5,4},{6,7},{7,6},{8,9},{9,8},{10,11... | collective-permute-start | bytes 1966088 | tf_op jit(solution)/shard_map/ppermute | solution.py:134
  79.8 9.8 %collective-permute-start.28 = (f32[8,160,128]{2,1,0:T(8,128)S(1)}, f32[8,160,128]{2,1,0:T(8,128)S(1)}, u32[]{:S(2)}, u32[]{:S(2)}) collective-permute-start(f32[8,160,128]{2,1,0:T(8,128)S(1)} %collective-permute-done.22.rest_4_), channel_id=1, source_target_pairs={{0,1},{1,0},{2,3},{3,2},{4,5},{5,4},{6,7},{7,6},{8,9},{9,8},{10,11... | collective-permute-start | bytes 1966088 | tf_op jit(solution)/shard_map/ppermute | solution.py:134
  79.8 9.8 %collective-permute-start.29 = (f32[8,160,128]{2,1,0:T(8,128)S(1)}, f32[8,160,128]{2,1,0:T(8,128)S(1)}, u32[]{:S(2)}, u32[]{:S(2)}) collective-permute-start(f32[8,160,128]{2,1,0:T(8,128)S(1)} %collective-permute-done.23.rest_6_), channel_id=1, source_target_pairs={{0,1},{1,0},{2,3},{3,2},{4,5},{5,4},{6,7},{7,6},{8,9},{9,8},{10,11... | collective-permute-start | bytes 1966088 | tf_op jit(solution)/shard_map/ppermute | solution.py:134
  80.3 8.3 %collective-permute-start.26 = (f32[4,128,128]{2,1,0:T(8,128)S(1)}, f32[4,128,128]{2,1,0:T(8,128)S(1)}, u32[]{:S(2)}, u32[]{:S(2)}) collective-permute-start(f32[4,128,128]{2,1,0:T(8,128)S(1)} %get-tuple-element.156), channel_id=1, source_target_pairs={{0,4},{4,0},{8,12},{12,8},{16,20},{20,16},{24,28},{28,24},{1,5},{5... | collective-permute-start | bytes 786440 | tf_op jit(solution)/shard_map/ppermute | solution.py:132
  81.5 8.0 %collective-permute-start.27 = (f32[4,128,128]{2,1,0:T(8,128)S(1)}, f32[4,128,128]{2,1,0:T(8,128)S(1)}, u32[]{:S(2)}, u32[]{:S(2)}) collective-permute-start(f32[4,128,128]{2,1,0:T(8,128)S(1)} %get-tuple-element.157), channel_id=1, source_target_pairs={{0,2},{1,3},{2,0},{3,1},{4,6},{5,7},{6,4},{7,5},{8,10},{9,11},{10,... | collective-permute-start | bytes 786440 | tf_op jit(solution)/shard_map/ppermute | solution.py:134
  89.6 12.8 %collective-permute-start.30 = (f32[8,128,128]{2,1,0:T(8,128)S(1)}, f32[8,128,128]{2,1,0:T(8,128)S(1)}, u32[]{:S(2)}, u32[]{:S(2)}) collective-permute-start(f32[8,128,128]{2,1,0:T(8,128)S(1)} %pad_maximum_fusion.8.rest_0_), channel_id=1, source_target_pairs={{0,2},{1,3},{2,0},{3,1},{4,6},{5,7},{6,4},{7,5},{8,10},{9,11},{10,... | collective-permute-start | bytes 1572872 | tf_op jit(solution)/shard_map/ppermute | solution.py:134
  90.2 12.5 %collective-permute-start.31 = (f32[8,128,128]{2,1,0:T(8,128)S(1)}, f32[8,128,128]{2,1,0:T(8,128)S(1)}, u32[]{:S(2)}, u32[]{:S(2)}) collective-permute-start(f32[8,128,128]{2,1,0:T(8,128)S(1)} %pad_maximum_fusion.9.rest_2_), channel_id=1, source_target_pairs={{0,4},{4,0},{8,12},{12,8},{16,20},{20,16},{24,28},{28,24},{1,5},{5... | collective-permute-start | bytes 1572872 | tf_op jit(solution)/shard_map/ppermute | solution.py:132
  91.1 11.5 %collective-permute-start.32 = (f32[8,128,128]{2,1,0:T(8,128)S(1)}, f32[8,128,128]{2,1,0:T(8,128)S(1)}, u32[]{:S(2)}, u32[]{:S(2)}) collective-permute-start(f32[8,128,128]{2,1,0:T(8,128)S(1)} %pad_maximum_fusion.8.rest_0_), channel_id=1, source_target_pairs={{0,1},{1,0},{2,3},{3,2},{4,5},{5,4},{6,7},{7,6},{8,9},{9,8},{10,11... | collective-permute-start | bytes 1572872 | tf_op jit(solution)/shard_map/ppermute | solution.py:134
  91.1 11.5 %collective-permute-start.33 = (f32[8,128,128]{2,1,0:T(8,128)S(1)}, f32[8,128,128]{2,1,0:T(8,128)S(1)}, u32[]{:S(2)}, u32[]{:S(2)}) collective-permute-start(f32[8,128,128]{2,1,0:T(8,128)S(1)} %pad_maximum_fusion.9.rest_2_), channel_id=1, source_target_pairs={{0,1},{1,0},{2,3},{3,2},{4,5},{5,4},{6,7},{7,6},{8,9},{9,8},{10,11... | collective-permute-start | bytes 1572872 | tf_op jit(solution)/shard_map/ppermute | solution.py:134
  119.6 6.5 %collective-permute-start.36 = (f32[16,256,128]{2,1,0:T(8,128)S(1)}, f32[16,256,128]{2,1,0:T(8,128)S(1)}, u32[]{:S(2)}, u32[]{:S(2)}) collective-permute-start(f32[16,256,128]{2,1,0:T(8,128)S(1)} %shard_map.282), channel_id=1, source_target_pairs={{0,1},{1,0},{2,3},{3,2},{4,5},{5,4},{6,7},{7,6},{8,9},{9,8},{10,11... | collective-permute-start | bytes 6291464 | tf_op jit(solution)/shard_map/ppermute | solution.py:134
  123.0 11.2 %collective-permute-start.37 = (f32[16,256,128]{2,1,0:T(8,128)S(1)}, f32[16,256,128]{2,1,0:T(8,128)S(1)}, u32[]{:S(2)}, u32[]{:S(2)}) collective-permute-start(f32[16,256,128]{2,1,0:T(8,128)S(1)} %shard_map.283), channel_id=1, source_target_pairs={{0,1},{1,0},{2,3},{3,2},{4,5},{5,4},{6,7},{7,6},{8,9},{9,8},{10,11... | collective-permute-start | bytes 6291464 | tf_op jit(solution)/shard_map/ppermute | solution.py:134
  127.6 15.7 %collective-permute-start.40 = (f32[4,256,128]{2,1,0:T(8,128)S(1)}, f32[4,256,128]{2,1,0:T(8,128)S(1)}, u32[]{:S(2)}, u32[]{:S(2)}) collective-permute-start(f32[4,256,128]{2,1,0:T(8,128)S(1)} %get-tuple-element.252), channel_id=1, source_target_pairs={{0,6},{1,7},{2,4},{3,5},{4,2},{5,3},{6,0},{7,1},{8,14},{9,15},{10,... | collective-permute-start | bytes 1572872 | tf_op jit(solution)/shard_map/ppermute | solution.py:137
  129.5 24.2 %collective-permute-start.39 = (f32[4,256,128]{2,1,0:T(8,128)S(1)}, f32[4,256,128]{2,1,0:T(8,128)S(1)}, u32[]{:S(2)}, u32[]{:S(2)}) collective-permute-start(f32[4,256,128]{2,1,0:T(8,128)S(1)} %get-tuple-element.253), channel_id=1, source_target_pairs={{0,2},{1,3},{2,0},{3,1},{4,6},{5,7},{6,4},{7,5},{8,10},{9,11},{10,... | collective-permute-start | bytes 1572872 | tf_op jit(solution)/shard_map/ppermute | solution.py:134
  130.0 23.8 %collective-permute-start.38 = (f32[4,256,128]{2,1,0:T(8,128)S(1)}, f32[4,256,128]{2,1,0:T(8,128)S(1)}, u32[]{:S(2)}, u32[]{:S(2)}) collective-permute-start(f32[4,256,128]{2,1,0:T(8,128)S(1)} %get-tuple-element.254), channel_id=1, source_target_pairs={{0,4},{4,0},{8,12},{12,8},{16,20},{20,16},{24,28},{28,24},{1,5},{5... | collective-permute-start | bytes 1572872 | tf_op jit(solution)/shard_map/ppermute | solution.py:132
  156.6 26.4 %collective-permute-start.43 = (f32[4,320,128]{2,1,0:T(8,128)S(1)}, f32[4,320,128]{2,1,0:T(8,128)S(1)}, u32[]{:S(2)}, u32[]{:S(2)}) collective-permute-start(f32[4,320,128]{2,1,0:T(8,128)S(1)} %pad_maximum_fusion.5), channel_id=1, source_target_pairs={{0,4},{4,0},{8,12},{12,8},{16,20},{20,16},{24,28},{28,24},{1,5},{5... | collective-permute-start | bytes 1966088 | tf_op jit(solution)/shard_map/ppermute | solution.py:132
  157.7 30.6 %collective-permute-start.44 = (f32[4,320,128]{2,1,0:T(8,128)S(1)}, f32[4,320,128]{2,1,0:T(8,128)S(1)}, u32[]{:S(2)}, u32[]{:S(2)}) collective-permute-start(f32[4,320,128]{2,1,0:T(8,128)S(1)} %pad_maximum_fusion.6), channel_id=1, source_target_pairs={{0,2},{1,3},{2,0},{3,1},{4,6},{5,7},{6,4},{7,5},{8,10},{9,11},{10,... | collective-permute-start | bytes 1966088 | tf_op jit(solution)/shard_map/ppermute | solution.py:134
  159.1 29.2 %collective-permute-start.45 = (f32[4,320,128]{2,1,0:T(8,128)S(1)}, f32[4,320,128]{2,1,0:T(8,128)S(1)}, u32[]{:S(2)}, u32[]{:S(2)}) collective-permute-start(f32[4,320,128]{2,1,0:T(8,128)S(1)} %pad_maximum_fusion.7), channel_id=1, source_target_pairs={{0,6},{1,7},{2,4},{3,5},{4,2},{5,3},{6,0},{7,1},{8,14},{9,15},{10,... | collective-permute-start | bytes 1966088 | tf_op jit(solution)/shard_map/ppermute | solution.py:137
  161.4 10.6 %collective-permute-start.41 = (f32[2,256,128]{2,1,0:T(8,128)S(1)}, f32[2,256,128]{2,1,0:T(8,128)S(1)}, u32[]{:S(2)}, u32[]{:S(2)}) collective-permute-start(f32[2,256,128]{2,1,0:T(8,128)S(1)} %slice_add_fusion.12), channel_id=1, source_target_pairs={{0,8},{4,12},{8,0},{12,4},{16,24},{20,28},{24,16},{28,20},{1,9},{5... | collective-permute-start | bytes 786440 | tf_op jit(solution)/shard_map/ppermute | solution.py:132
  188.3 5.7 %collective-permute-start.46 = (f32[2,2,16,512]{3,2,1,0:T(8,128)S(1)}, f32[2,2,16,512]{3,2,1,0:T(8,128)S(1)}, u32[]{:S(2)}, u32[]{:S(2)}) collective-permute-start(f32[2,2,16,512]{3,2,1,0:T(8,128)S(1)} %get-tuple-element.214), channel_id=1, source_target_pairs={{0,1},{1,0},{2,3},{3,2},{4,5},{5,4},{6,7},{7,6},{8,9},{9,8},{10,11... | collective-permute-start | bytes 393224 | tf_op jit(solution)/shard_map/ppermute | solution.py:1003
  188.3 4.7 %collective-permute-start.47 = (f32[2,2,8,512]{3,2,1,0:T(8,128)S(1)}, f32[2,2,8,512]{3,2,1,0:T(8,128)S(1)}, u32[]{:S(2)}, u32[]{:S(2)}) collective-permute-start(f32[2,2,8,512]{3,2,1,0:T(8,128)S(1)} %get-tuple-element.215), channel_id=1, source_target_pairs={{0,2},{1,3},{2,0},{3,1},{4,6},{5,7},{6,4},{7,5},{8,10},{9,11},{10,... | collective-permute-start | bytes 196616 | tf_op jit(solution)/shard_map/ppermute | solution.py:1003
  198.9 4.8 %collective-permute-start.49 = (f32[16,192,128]{2,1,0:T(8,128)}, f32[16,192,128]{2,1,0:T(8,128)}, u32[]{:S(2)}, u32[]{:S(2)}) collective-permute-start(f32[16,192,128]{2,1,0:T(8,128)} %get-tuple-element.223), channel_id=1, source_target_pairs={{0,1},{1,0},{2,3},{3,2},{4,5},{5,4},{6,7},{7,6},{8,9},{9,8},{10,11... | collective-permute-start | bytes 4718600 | tf_op jit(solution)/shard_map/ppermute | solution.py:134
  206.5 28.8 %collective-permute-start.52 = (f32[4,208,128]{2,1,0:T(8,128)}, f32[4,208,128]{2,1,0:T(8,128)}, u32[]{:S(2)}, u32[]{:S(2)}) collective-permute-start(f32[4,208,128]{2,1,0:T(8,128)} %get-tuple-element.265), channel_id=1, source_target_pairs={{0,6},{1,7},{2,4},{3,5},{4,2},{5,3},{6,0},{7,1},{8,14},{9,15},{10,... | collective-permute-start | bytes 1277960 | tf_op jit(solution)/shard_map/ppermute | solution.py:137
  208.2 28.1 %collective-permute-start.51 = (f32[4,208,128]{2,1,0:T(8,128)}, f32[4,208,128]{2,1,0:T(8,128)}, u32[]{:S(2)}, u32[]{:S(2)}) collective-permute-start(f32[4,208,128]{2,1,0:T(8,128)} %get-tuple-element.266), channel_id=1, source_target_pairs={{0,2},{1,3},{2,0},{3,1},{4,6},{5,7},{6,4},{7,5},{8,10},{9,11},{10,... | collective-permute-start | bytes 1277960 | tf_op jit(solution)/shard_map/ppermute | solution.py:134
  209.0 27.3 %collective-permute-start.50 = (f32[4,208,128]{2,1,0:T(8,128)}, f32[4,208,128]{2,1,0:T(8,128)}, u32[]{:S(2)}, u32[]{:S(2)}) collective-permute-start(f32[4,208,128]{2,1,0:T(8,128)} %get-tuple-element.267), channel_id=1, source_target_pairs={{0,4},{4,0},{8,12},{12,8},{16,20},{20,16},{24,28},{28,24},{1,5},{5... | collective-permute-start | bytes 1277960 | tf_op jit(solution)/shard_map/ppermute | solution.py:132
  212.8 20.5 %collective-permute-start.53 = (f32[2,320,128]{2,1,0:T(8,128)}, f32[2,320,128]{2,1,0:T(8,128)}, u32[]{:S(2)}, u32[]{:S(2)}) collective-permute-start(f32[2,320,128]{2,1,0:T(8,128)} %pad_maximum_fusion.14), channel_id=1, source_target_pairs={{0,8},{4,12},{8,0},{12,4},{16,24},{20,28},{24,16},{28,20},{1,9},{5... | collective-permute-start | bytes 983048 | tf_op jit(solution)/shard_map/ppermute | solution.py:132
  213.7 31.5 %collective-permute-start.59 = (f32[1,256,128]{2,1,0:T(8,128)S(1)}, f32[1,256,128]{2,1,0:T(8,128)}, u32[]{:S(2)}, u32[]{:S(2)}) collective-permute-start(f32[1,256,128]{2,1,0:T(8,128)S(1)} %fusion.9), channel_id=1, source_target_pairs={{0,16},{4,20},{8,24},{12,28},{16,0},{20,4},{24,8},{28,12},{1,17},{... | collective-permute-start | bytes 393224 | tf_op jit(solution)/shard_map/ppermute | solution.py:132
  238.6 8.5 %collective-permute-start.56 = (f32[1,208,128]{2,1,0:T(8,128)S(1)}, f32[1,208,128]{2,1,0:T(8,128)S(1)}, u32[]{:S(2)}, u32[]{:S(2)}) collective-permute-start(f32[1,208,128]{2,1,0:T(8,128)S(1)} %get-tuple-element.274), channel_id=1, source_target_pairs={{0,24},{4,28},{8,16},{12,20},{16,8},{20,12},{24,0},{28,4},{1,25},{... | collective-permute-start | bytes 319496 | tf_op jit(solution)/shard_map/ppermute | solution.py:132
  239.9 14.9 %collective-permute-start.55 = (f32[1,208,128]{2,1,0:T(8,128)S(1)}, f32[1,208,128]{2,1,0:T(8,128)S(1)}, u32[]{:S(2)}, u32[]{:S(2)}) collective-permute-start(f32[1,208,128]{2,1,0:T(8,128)S(1)} %get-tuple-element.273), channel_id=1, source_target_pairs={{0,16},{4,20},{8,24},{12,28},{16,0},{20,4},{24,8},{28,12},{1,17},{... | collective-permute-start | bytes 319496 | tf_op jit(solution)/shard_map/ppermute | solution.py:132
  241.6 13.2 %collective-permute-start.54 = (f32[1,208,128]{2,1,0:T(8,128)S(1)}, f32[1,208,128]{2,1,0:T(8,128)S(1)}, u32[]{:S(2)}, u32[]{:S(2)}) collective-permute-start(f32[1,208,128]{2,1,0:T(8,128)S(1)} %get-tuple-element.272), channel_id=1, source_target_pairs={{0,8},{4,12},{8,0},{12,4},{16,24},{20,28},{24,16},{28,20},{1,9},{5... | collective-permute-start | bytes 319496 | tf_op jit(solution)/shard_map/ppermute | solution.py:132
  244.9 13.1 %collective-permute-start.58 = (f32[1,320,128]{2,1,0:T(8,128)S(1)}, f32[1,320,128]{2,1,0:T(8,128)S(1)}, u32[]{:S(2)}, u32[]{:S(2)}) collective-permute-start(f32[1,320,128]{2,1,0:T(8,128)S(1)} %pad_maximum_fusion.20), channel_id=1, source_target_pairs={{0,16},{4,20},{8,24},{12,28},{16,0},{20,4},{24,8},{28,12},{1,17},{... | collective-permute-start | bytes 491528 | tf_op jit(solution)/shard_map/ppermute | solution.py:132
  (71 other events, 1042.9 us)

commit v2 on v1

--- a/solution.py
+++ b/solution.py
@@ -1099,41 +1099,39 @@
 
     single = [("x", "y"), ("z",), ("w",)] + extra
     double = [("x", "y"), ("z", "w")] + extra
-    down = Stream(plan, chunks * rows_d, single)
+    outer = [("z",), ("x",), ("w",)] + extra + [("y",)]
+    down = Stream(plan, chunks * rows_d, outer)
     up = Stream(plan, rows_up, single)
     out = Stream(plan, rows_d, single)
     qkv = Stream(plan, rows_qkv, double)
-    down_sum, up_sum, qkv_sum = Reduce(plan, single), Reduce(plan, single), Reduce(plan, double)
-
-    away = grad_down_stage(me, cth, ctl, hh, hl, plan, down, 1)
-    down_core = down_sum.begin(away)
+    down_sum, up_sum, qkv_sum = Reduce(plan, outer), Reduce(plan, single), Reduce(plan, double)
+
+    gm, gln = middle_grad_stage(cot, xhat2, inv2, ln, ph, plo, uh, ul)
+    gmix, away_out, keep_out = mixture_grad_stage(me, gm, attended, oh, ol, plan, out)
+    away = grad_down_stage(me, after(cth, away_out), ctl, hh, hl, plan, down, 1)
+    cores = down_sum.begin(away)
     away = grad_up_stage(me, after(nth, away), ntl, ph, plo, plan, up, 1)
-    up_core = up_sum.begin(away)
+    cores += up_sum.begin(away)
+    cores += up_sum.begin(away_out)
     keep = grad_down_stage(me, after(cth, away), ctl, hh, hl, plan, down, 0)
     down_sum.keep(keep)
-    sent = down_sum.send(keep, down_core)
-    keep = grad_up_stage(me, after(nth, sent), ntl, ph, plo, plan, up, 0)
+    keep = grad_up_stage(me, after(nth, keep), ntl, ph, plo, plan, up, 0)
     up_sum.keep(keep)
-    gm, gln = middle_grad_stage(after(cot, keep, up_core), xhat2, inv2, ln, ph, plo, uh, ul)
-    gmix, away, keep = mixture_grad_stage(me, gm, attended, oh, ol, plan, out)
-    got = up_sum.begin(away, down_sum.last)
-    up_sum.keep(keep)
-    sent = (down_sum.send(), up_sum.send(got))
+    up_sum.keep(keep_out)
+    sent = (down_sum.send(keep, cores), up_sum.send(keep, cores))
     before = ()
     calls = [(s, 1, 0, width // 128) for s in range(seqs)]
-    for index, which in enumerate(calls):
+    for which in calls:
         grad = after(gmix, sent, before)
         before = attention_backward(
             packed, far, bias, *attend, attended, lse, grad, seqs, local_rows, which, before
         )
-        if down_sum.stages:
-            sent = down_sum.send(before, down_sum.last)
-        else:
-            sent = down_sum.last
-    gate = (before, up_sum.last)
+    output = output_stage(after(middle, before), hh, hl, dh, dl)
+    gate = (output, down_sum.last, up_sum.last)
     dq, dk, dv, f4, f5a, f5b = before
     f4, f5a, f5b = after((f4, f5a, f5b), gate)
     g4, g5a, g5b = swap(f4, 1), swap(f5a, 2), swap(f5b, 3)
+    down_sum.send(gate)
     gph, gpl, column = packed_grad_stage(dq, dk, dv, g4, g5a, g5b, far_pool, seqs)
     away, sums_away = grad_qkv_stage(
         me, gph, gpl, column, xhat1, ln, wqh, wql, plan, qkv, 1
@@ -1145,17 +1143,17 @@
     qkv_sum.keep(keep)
     sums = jnp.concatenate([(sums_away + sums_keep)[0:2], gln[0:2]], axis=0)
     sent = qkv_sum.send(got, rider=sums.reshape(-1, 128))
+    down_sum.send(sent)
     up_sum.send(sent)
     gtok = input_grad_stage(gph, gpl, wqh, wql, after(xhat1, sent), inv1, ln, gm)
-    output = output_stage(after(middle, gtok), hh, hl, dh, dl)
     rode = qkv_sum.rode
-    sent = qkv_sum.send(qkv_sum.last, up_sum.last, output, rider=rode)
+    gate = (up_sum.last, down_sum.last, gtok)
+    sent = qkv_sum.send(qkv_sum.last, gate, rider=rode)
     while qkv_sum.stages:
         sent = qkv_sum.send(qkv_sum.last, rider=qkv_sum.rode)
-    while up_sum.stages:
-        up_sum.send(sent)
     for total in (down_sum, up_sum):
-        total.terms[0] = after(total.terms[0], sent)
+        while total.stages:
+            total.send(gate, sent)
     sums = qkv_sum.rode
     sums = (sums + plan.send(sums, ("c",))).reshape(4, width)
     (g_down,), (g_up, g_out), (g_qkv,) = (t.total() for t in (down_sum, up_sum, qkv_sum))

time: 262 us -> 251 us (0.958)
  waiting for transfers between devices: 63.8 us -> 46.8 us
  starting transfers between devices: 50.9 us -> 56.2 us
    ppermute x26, waiting for transfers between devices: 33.1 us -> 18.8 us  [send(): return lax.ppermute(x, 'fsdp', [(i, i ^ f) for i in range(self.fsdp)])]
    ppermute x23, starting transfers between devices: 29.5 us -> 33 us  [send(): return lax.ppermute(x, 'dp', [(i, i ^ d) for i in range(self.dp)])]
    ppermute x26, starting transfers between devices: 11 us -> 14.3 us  [send(): return lax.ppermute(x, 'fsdp', [(i, i ^ f) for i in range(self.fsdp)])]
    select_n x5, other arithmetic: 4.57 us -> 1.73 us  [score_bias(): parts.append(jnp.where(ok, np.float32(level * np.log(2.0)), MASKED))]
    unnamed x133 -> x141, local copies, waits for them, and re-layouts: 14.6 us -> 12.7 us
    add x11 -> x12, other arithmetic: 9.53 us -> 11.4 us  [send(): sum((term[i][v * n:(v + 1) * n] for term in self.terms))]
  transfers between devices with their start and end apart: 60 -> 59, of which waited for: 24 -> 22; matrix products, arithmetic and copies ran while one was open for 14% -> 15% of each run, Pallas kernels for 26% -> 23%
where the time goes in v2:
time: 251 us; the launch traced here: 249 us
  Pallas kernels  87.8 us (35%)
  starting transfers between devices  56.2 us (22%)
  waiting for transfers between devices  46.8 us (19%)
  local copies, waits for them, and re-layouts  29.5 us (12%)
  other arithmetic  26.8 us (11%)
    ppermute x23, starting transfers between devices, send(): return lax.ppermute(x, 'dp', [(i, i ^ d) for i in range(self.dp)])  33 us
    ppermute x23, waiting for transfers between devices, send(): return lax.ppermute(x, 'dp', [(i, i ^ d) for i in range(self.dp)])  23.9 us
    pallas_call x2, Pallas kernels, attention_backward(): pl.pallas_call(body, compiler_params=ROOM, cost_estimate=cost(8), grid=(c...  19.7 us
    ppermute x26, waiting for transfers between devices, send(): return lax.ppermute(x, 'fsdp', [(i, i ^ f) for i in range(self.fsdp)])  18.8 us
    ppermute x26, starting transfers between devices, send(): return lax.ppermute(x, 'fsdp', [(i, i ^ f) for i in range(self.fsdp)])  14.3 us
    unnamed x141, local copies, waits for them, and re-layouts  12.7 us
    pallas_call x1, Pallas kernels, hidden_stage(): pl.pallas_call(body, compiler_params=ROOM, cost_estimate=cost(15), grid=(...  11.6 us
    add x12, other arithmetic, send(): sum((term[i][v * n:(v + 1) * n] for term in self.terms))  11.4 us
  transfers between devices with their start and end apart: 59, of which 22 were waited for; matrix products, arithmetic and copies ran while one was open for 15% of the time, Pallas kernels for 23%

profile of v2, /device:TPU:0, one launch (start us, length us, event | category | flops | bytes accessed | tf_op | source)
XLA Modules:
  0.0 249.0 jit_solution(17804395523801823489)
XLA Ops:
  3.2 3.0 %collective-permute-start = (f32[1,208,128]{2,1,0:T(8,128)S(1)}, f32[1,208,128]{2,1,0:T(8,128)S(1)}, u32[]{:S(2)}, u32[]{:S(2)}) collective-permute-start(f32[1,208,128]{2,1,0:T(8,128)S(1)} %bitcast.119), channel_id=1, source_target_pairs={{0,8},{4,12},{8,0},{12,4},{16,24},{20,28},{24,16},{28,20},{1,9},{5... | collective-permute-start | bytes 319496 | tf_op jit(solution)/shard_map/ppermute | solution.py:132
  6.2 2.6 %collective-permute-start.1 = (f32[1,208,128]{2,1,0:T(8,128)S(1)}, f32[1,208,128]{2,1,0:T(8,128)S(1)}, u32[]{:S(2)}, u32[]{:S(2)}) collective-permute-start(f32[1,208,128]{2,1,0:T(8,128)S(1)} %bitcast.120), channel_id=1, source_target_pairs={{0,16},{4,20},{8,24},{12,28},{16,0},{20,4},{24,8},{28,12},{1,17},{... | collective-permute-start | bytes 319496 | tf_op jit(solution)/shard_map/ppermute | solution.py:132
  17.9 1.8 collective-permute-start.9
  20.1 1.9 collective-permute-start.3
  22.0 1.8 collective-permute-start.7
  24.4 2.4 collective-permute-done.4
  27.7 1.7 collective-permute-start.6
  33.5 3.1 %collective-permute-start.11 = (f32[1,256,128]{2,1,0:T(8,128)}, f32[1,256,128]{2,1,0:T(8,128)}, u32[]{:S(2)}, u32[]{:S(2)}) collective-permute-start(f32[1,256,128]{2,1,0:T(8,128)} %bitcast.20), channel_id=1, source_target_pairs={{0,16},{4,20},{8,24},{12,28},{16,0},{20,4},{24,8},{28,12},{1,17},{... | collective-permute-start | bytes 393224 | tf_op jit(solution)/shard_map/ppermute | solution.py:132
  37.5 2.1 concatenate.95.outer_bias
  39.6 3.5 %collective-permute-done.11 = f32[1,256,128]{2,1,0:T(8,128)} collective-permute-done((f32[1,256,128]{2,1,0:T(8,128)}, f32[1,256,128]{2,1,0:T(8,128)}, u32[]{:S(2)}, u32[]{:S(2)}) %collective-permute-start.11) | collective-permute-done | bytes 131104 | tf_op jit(solution)/shard_map/ppermute | solution.py:132
  43.1 1.8 collective-permute-done.10
  48.9 1.7 collective-permute-start.17
  51.6 2.5 collective-permute-start.18
  57.1 5.5 %shard_map.276 = (f32[512,1536]{1,0:T(8,128)S(1)}, bf16[1536,512]{1,0:T(8,128)(2,1)S(1)}, bf16[1536,512]{1,0:T(8,128)(2,1)S(1)}, f32[512,512]{1,0:T(8,128)S(1)},...) custom-call(s32[2]{0:T(128)S(1)} %copy-done.39, ...), custom_call_target="tpu_custom_call" | custom-call | flops 333000000 | bytes 925000 | tf_op jit(solution)/shard_map/pallas_call | solution.py:367
  65.6 1.6 collective-permute-start.23
  69.1 5.6 %shard_map.277 = (f32[512,512]{1,0:T(8,128)S(1)}, f32[512,512]{1,0:T(8,128)S(1)}) custom-call(f32[512,1536]{1,0:T(8,128)S(1)} %get-tuple-element.152.q.k.v, f32[512,1536]{1,0:T(8,128)S(1)} %get-tuple-element.152.q.k.v, f32[512,1536]{1,0:T(8,128)S(1)} %get-tuple-element.152.q.k.v, f32[2,2,32,512]{3,2,1,0:T(8,128)S(1)} %constant_dynamic-update-slice_fusion.2.fk.fv, ...), custom_call_target="tpu_custom_call" | custom-call | flops 427500000 | bytes 1187500 | tf_op jit(solution)/shard_map/pallas_call | solution.py:494
  74.7 7.7 %collective-permute-done.22.rest_4_ = f32[8,160,128]{2,1,0:T(8,128)S(1)} collective-permute-done((f32[8,160,128]{2,1,0:T(8,128)S(1)}, f32[8,160,128]{2,1,0:T(8,128)S(1)}, u32[]{:S(2)}, u32[]{:S(2)}) %collective-permute-start.22) | collective-permute-done | bytes 655392 | tf_op jit(solution)/shard_map/ppermute | solution.py:134
  84.1 1.6 collective-permute-start.26
  85.7 5.6 %shard_map.278 = (f32[512,512]{1,0:T(8,128)S(1)}, f32[512,512]{1,0:T(8,128)S(1)}) custom-call(f32[512,1536]{1,0:T(8,128)S(1)} %get-tuple-element.152.q.k.v, f32[512,1536]{1,0:T(8,128)S(1)} %get-tuple-element.152.q.k.v, f32[512,1536]{1,0:T(8,128)S(1)} %get-tuple-element.152.q.k.v, ...), custom_call_target="tpu_custom_call", output_to_operand_aliasing={{0}: (10, {}), {1}: (11, {})} | custom-call | flops 427500000 | bytes 1187500 | tf_op jit(solution)/shard_map/pallas_call | solution.py:494
  92.8 1.6 collective-permute-start.31
  95.4 2.4 shard_map.279
  99.1 7.5 %collective-permute-done.31.rest_6_ = f32[8,128,128]{2,1,0:T(8,128)S(1)} collective-permute-done((f32[8,128,128]{2,1,0:T(8,128)S(1)}, f32[8,128,128]{2,1,0:T(8,128)S(1)}, u32[]{:S(2)}, u32[]{:S(2)}) %collective-permute-start.31) | collective-permute-done | bytes 524320 | tf_op jit(solution)/shard_map/ppermute | solution.py:132
  110.7 11.6 %shard_map.281 = (bf16[512,2048]{1,0:T(8,128)(2,1)S(1)}, bf16[512,2048]{1,0:T(8,128)(2,1)S(1)}, bf16[512,2048]{1,0:T(8,128)(2,1)S(1)}, bf16[512,2048]{1,0:T(8,12...) custom-call(s32[2]{0:T(128)S(1)} %copy-done.39, ...), custom_call_target="tpu_custom_call" | custom-call | flops 675000000 | bytes 1875000 | tf_op jit(solution)/shard_map/pallas_call | solution.py:693
  122.3 5.0 %shard_map.282 = (f32[512,512]{1,0:T(8,128)S(1)}, f32[8,512]{1,0:T(8,128)S(1)}) custom-call(f32[512,512]{1,0:T(8,128)S(1)} %bitcast.116, f32[512,512]{1,0:T(8,128)S(1)} %get-tuple-element.172.xhat_ref, f32[512,128]{1,0:T(8,128)S(1)} %get-tuple-element.164.inv_ref, f32[8,512]{1,0:T(8,128)S(1)} %get-tuple-element.165.ln_ref.ln_r, ...), custom_call_target="tpu_custom_call" | custom-call | flops 382500000 | bytes 1062500 | tf_op jit(solution)/shard_map/pallas_call | solution.py:853
  127.3 2.4 shard_map.283
  129.7 2.7 %shard_map.284 = f32[16,256,128]{2,1,0:T(8,128)S(1)} custom-call(s32[2]{0:T(128)S(1)} %copy-done.39, bf16[512,512]{1,0:T(8,128)(2,1)S(1)} %get-tuple-element.190.c0, bf16[512,512]{1,0:T(8,128)(2,1)S(1)} %get-tuple-element.185.c1, bf16[512,2048]{1,0:T(8,128)(2,1)S(1)} %get-tuple-element.186.h0, bf16[512,2048]{1,0:T(8,128)(2,1)S(1)} %get-tuple-element.187.h1), custom_call_target="tpu_custom_call" | custom-call | flops 12150000 | bytes 33750 | tf_op jit(solution)/shard_map/pallas_call | solution.py:732
  132.5 3.2 %shard_map.285 = f32[16,256,128]{2,1,0:T(8,128)S(1)} custom-call(s32[2]{0:T(128)S(1)} %copy-done.39, bf16[512,512]{1,0:T(8,128)(2,1)S(1)} %get-tuple-element.191.n0, bf16[512,512]{1,0:T(8,128)(2,1)S(1)} %get-tuple-element.189.n1, bf16[512,2048]{1,0:T(8,128)(2,1)S(1)} %get-tuple-element.175.p0, bf16[512,2048]{1,0:T(8,128)(2,1)S(1)} %get-tuple-element.176.p1), custom_call_target="tpu_custom_call" | custom-call | flops 14400000 | bytes 40000 | tf_op jit(solution)/shard_map/pallas_call | solution.py:785
  136.4 2.7 %shard_map.286 = f32[16,256,128]{2,1,0:T(8,128)S(1)} custom-call(s32[2]{0:T(128)S(1)} %copy-done.39, bf16[512,512]{1,0:T(8,128)(2,1)S(1)} %get-tuple-element.190.c0, bf16[512,512]{1,0:T(8,128)(2,1)S(1)} %get-tuple-element.185.c1, bf16[512,2048]{1,0:T(8,128)(2,1)S(1)} %get-tuple-element.186.h0, bf16[512,2048]{1,0:T(8,128)(2,1)S(1)} %get-tuple-element.187.h1), custom_call_target="tpu_custom_call" | custom-call | flops 12150000 | bytes 33750 | tf_op jit(solution)/shard_map/pallas_call | solution.py:732
  139.1 3.2 %shard_map.287 = f32[16,256,128]{2,1,0:T(8,128)S(1)} custom-call(s32[2]{0:T(128)S(1)} %copy-done.39, bf16[512,512]{1,0:T(8,128)(2,1)S(1)} %get-tuple-element.191.n0, bf16[512,512]{1,0:T(8,128)(2,1)S(1)} %get-tuple-element.189.n1, bf16[512,2048]{1,0:T(8,128)(2,1)S(1)} %get-tuple-element.175.p0, bf16[512,2048]{1,0:T(8,128)(2,1)S(1)} %get-tuple-element.176.p1), custom_call_target="tpu_custom_call" | custom-call | flops 14400000 | bytes 40000 | tf_op jit(solution)/shard_map/pallas_call | solution.py:785
  147.6 1.7 collective-permute-start.40
  149.2 9.7 %shard_map.288 = (f32[512,512]{1,0:T(8,128)S(1)}, f32[512,512]{1,0:T(8,128)S(1)}, f32[512,512]{1,0:T(8,128)S(1)}, f32[2,2,16,512]{3,2,1,0:T(8,128)S(1)}, f32[2,2...) custom-call(f32[512,1536]{1,0:T(8,128)S(1)} %get-tuple-element.152.q.k.v, f32[512,1536]{1,0:T(8,128)S(1)} %get-tuple-element.152.q.k.v, ...), custom_call_target="tpu_custom_call" | custom-call | flops 360000000 | bytes 1000000 | tf_op jit(solution)/shard_map/pallas_call | solution.py:566
  159.0 10.0 %shard_map.289 = (f32[512,512]{1,0:T(8,128)S(1)}, f32[512,512]{1,0:T(8,128)S(1)}, f32[512,512]{1,0:T(8,128)S(1)}, f32[2,2,16,512]{3,2,1,0:T(8,128)S(1)}, f32[2,2...) custom-call(f32[512,1536]{1,0:T(8,128)S(1)} %get-tuple-element.152.q, ...), custom_call_target="tpu_custom_call", output_to_operand_aliasing={{0}: (13, {}), {1}: (14, {}), {2}: (15, {}), {3}: (16, {}),... | custom-call | flops 360000000 | bytes 1000000 | tf_op jit(solution)/shard_map/pallas_call | solution.py:566
  169.0 5.8 %shard_map.290 = f32[512,512]{1,0:T(8,128)} custom-call(f32[512,512]{1,0:T(8,128)S(1)} %get-tuple-element.210.mid, bf16[512,2048]{1,0:T(8,128)(2,1)S(1)} %get-tuple-element.186.h0, bf16[512,2048]{1,0:T(8,128)(2,1)S(1)} %get-tuple-element.187.h1, bf16[512,2048]{1,0:T(8,128)(2,1)S(1)} %get-tuple-element.173.d0, bf16[512,2048]{1,0:T(8,128)(2,1)S(1)} %copy-done.11), custom_call_target="tpu_custom_call" | custom-call | flops 360000000 | bytes 1000000 | tf_op jit(solution)/shard_map/pallas_call | solution.py:817
  174.8 2.3 collective-permute-done.41
  179.1 3.1 %collective-permute-done.44.g5a_r = f32[2,2,8,512]{3,2,1,0:T(8,128)S(1)} collective-permute-done((f32[2,2,8,512]{3,2,1,0:T(8,128)S(1)}, f32[2,2,8,512]{3,2,1,0:T(8,128)S(1)}, u32[]{:S(2)}, u32[]{:S(2)}) %collective-permute-start.44) | collective-permute-done | bytes 65568 | tf_op jit(solution)/shard_map/ppermute | solution.py:1003
  183.9 3.7 %shard_map.292 = (f32[16,192,128]{2,1,0:T(8,128)}, f32[8,512]{1,0:T(8,128)S(1)}) custom-call(s32[2]{0:T(128)S(1)} %copy-done.39, bf16[512,1536]{1,0:T(8,128)(2,1)S(1)} %get-tuple-element.214.gph_r, bf16[512,1536]{1,0:T(8,128)(2,1)S(1)} %get-tuple-element.215.gpl_r, f32[1536,128]{1,0:T(8,128)S(1)} %get-tuple-element.219.col_r, ...), custom_call_target="tpu_custom_call" | custom-call | flops 11250000 | bytes 31250 | tf_op jit(solution)/shard_map/pallas_call | solution.py:985
  190.9 2.6 %shard_map.293 = (f32[16,192,128]{2,1,0:T(8,128)S(1)}, f32[8,512]{1,0:T(8,128)S(1)}) custom-call(s32[2]{0:T(128)S(1)} %copy-done.39, bf16[512,1536]{1,0:T(8,128)(2,1)S(1)} %get-tuple-element.214.gph_r, bf16[512,1536]{1,0:T(8,128)(2,1)S(1)} %get-tuple-element.215.gpl_r, f32[1536,128]{1,0:T(8,128)S(1)} %get-tuple-element.219.col_r, ...), custom_call_target="tpu_custom_call" | custom-call | flops 11250000 | bytes 31250 | tf_op jit(solution)/shard_map/pallas_call | solution.py:985
  194.7 1.7 slice_add_fusion.5
  197.6 1.8 collective-permute-start.49
  201.1 4.3 %collective-permute-done.51 = f32[4,256,128]{2,1,0:T(8,128)} collective-permute-done((f32[4,256,128]{2,1,0:T(8,128)}, f32[4,256,128]{2,1,0:T(8,128)}, u32[]{:S(2)}, u32[]{:S(2)}) %collective-permute-start.51) | collective-permute-done | bytes 524320 | tf_op jit(solution)/shard_map/ppermute | solution.py:132
  208.2 1.7 collective-permute-start.50
  209.9 1.9 fusion.2
  211.9 1.7 collective-permute-start.52
  218.9 3.8 %shard_map.294 = f32[512,512]{1,0:T(8,128)} custom-call(bf16[512,1536]{1,0:T(8,128)(2,1)S(1)} %copy-done.3, bf16[512,1536]{1,0:T(8,128)(2,1)S(1)} %copy-done.5, bf16[1536,512]{1,0:T(8,128)(2,1)S(1)} %get-tuple-element.216.wh_r.wh, bf16[1536,512]{1,0:T(8,128)(2,1)S(1)} %get-tuple-element.217.wl_r.wl, f32[512,512]{1,0:T(8,128)S(1)} %copy-done.8, ...), custom_call_target="tpu_custom_call" | custom-call | flops 333000000 | bytes 925000 | tf_op jit(solution)/shard_map/pallas_call | solution.py:937
  228.3 2.2 collective-permute-start.54
  230.5 1.9 collective-permute-start.55
  236.9 2.9 %collective-permute-done.54 = f32[1,208,128]{2,1,0:T(8,128)S(1)} collective-permute-done((f32[1,208,128]{2,1,0:T(8,128)S(1)}, f32[1,208,128]{2,1,0:T(8,128)S(1)}, u32[]{:S(2)}, u32[]{:S(2)}) %collective-permute-start.54) | collective-permute-done | bytes 106528 | tf_op jit(solution)/shard_map/ppermute | solution.py:132
  240.6 1.7 fusion.17
  (343 shorter events, 82.7 us)
Async XLA Ops:
  3.2 14.7 %collective-permute-start = (f32[1,208,128]{2,1,0:T(8,128)S(1)}, f32[1,208,128]{2,1,0:T(8,128)S(1)}, u32[]{:S(2)}, u32[]{:S(2)}) collective-permute-start(f32[1,208,128]{2,1,0:T(8,128)S(1)} %bitcast.119), channel_id=1, source_target_pairs={{0,8},{4,12},{8,0},{12,4},{16,24},{20,28},{24,16},{28,20},{1,9},{5... | collective-permute-start | bytes 319496 | tf_op jit(solution)/shard_map/ppermute | solution.py:132
  6.2 11.7 %collective-permute-start.1 = (f32[1,208,128]{2,1,0:T(8,128)S(1)}, f32[1,208,128]{2,1,0:T(8,128)S(1)}, u32[]{:S(2)}, u32[]{:S(2)}) collective-permute-start(f32[1,208,128]{2,1,0:T(8,128)S(1)} %bitcast.120), channel_id=1, source_target_pairs={{0,16},{4,20},{8,24},{12,28},{16,0},{20,4},{24,8},{28,12},{1,17},{... | collective-permute-start | bytes 319496 | tf_op jit(solution)/shard_map/ppermute | solution.py:132
  8.8 9.1 %collective-permute-start.2 = (f32[1,208,128]{2,1,0:T(8,128)S(1)}, f32[1,208,128]{2,1,0:T(8,128)S(1)}, u32[]{:S(2)}, u32[]{:S(2)}) collective-permute-start(f32[1,208,128]{2,1,0:T(8,128)S(1)} %bitcast.121), channel_id=1, source_target_pairs={{0,24},{4,28},{8,16},{12,20},{16,8},{20,12},{24,0},{28,4},{1,25},{... | collective-permute-start | bytes 319496 | tf_op jit(solution)/shard_map/ppermute | solution.py:132
  8.8 8.5 %collective-permute-start.8 = (s32[2,256]{1,0:T(2,128)}, s32[2,256]{1,0:T(2,128)S(1)}, u32[]{:S(2)}, u32[]{:S(2)}) collective-permute-start(s32[2,256]{1,0:T(2,128)} %param.22), channel_id=1, source_target_pairs={{0,1},{1,0},{2,3},{3,2},{4,5},{5,4},{6,7},{7,6},{8,9},{9,8},{10,11... | collective-permute-start | bytes 6152 | tf_op jit(solution)/shard_map/ppermute | solution.py:1003
  17.9 5.9 %collective-permute-start.9 = (s32[2,2,256]{2,1,0:T(2,128)S(1)}, s32[2,2,256]{2,1,0:T(2,128)S(1)}, u32[]{:S(2)}, u32[]{:S(2)}) collective-permute-start(s32[2,2,256]{2,1,0:T(2,128)S(1)} %pad_add_fusion), channel_id=1, source_target_pairs={{0,2},{1,3},{2,0},{3,1},{4,6},{5,7},{6,4},{7,5},{8,10},{9,11},{10,... | collective-permute-start | bytes 12296 | tf_op jit(solution)/shard_map/ppermute | solution.py:1003
  19.7 7.1 %collective-permute-start.4 = (f32[4,96,128]{2,1,0:T(8,128)S(1)}, f32[4,96,128]{2,1,0:T(8,128)S(1)}, u32[]{:S(2)}, u32[]{:S(2)}) collective-permute-start(f32[4,96,128]{2,1,0:T(8,128)S(1)} %pad_maximum_fusion.16), channel_id=1, source_target_pairs={{0,2},{1,3},{2,0},{3,1},{4,6},{5,7},{6,4},{7,5},{8,10},{9,11},{10,... | collective-permute-start | bytes 589832 | tf_op jit(solution)/shard_map/ppermute | solution.py:134
  20.1 7.6 %collective-permute-start.3 = (f32[4,112,128]{2,1,0:T(8,128)S(1)}, f32[4,112,128]{2,1,0:T(8,128)S(1)}, u32[]{:S(2)}, u32[]{:S(2)}) collective-permute-start(f32[4,112,128]{2,1,0:T(8,128)S(1)} %slice.580), channel_id=1, source_target_pairs={{0,4},{4,0},{8,12},{12,8},{16,20},{20,16},{24,28},{28,24},{1,5},{5... | collective-permute-start | bytes 688136 | tf_op jit(solution)/shard_map/ppermute | solution.py:132
  22.0 10.3 %collective-permute-start.7 = (f32[1,320,128]{2,1,0:T(8,128)S(1)}, f32[1,320,128]{2,1,0:T(8,128)}, u32[]{:S(2)}, u32[]{:S(2)}) collective-permute-start(f32[1,320,128]{2,1,0:T(8,128)S(1)} %maximum_bitcast_fusion), channel_id=1, source_target_pairs={{0,16},{4,20},{8,24},{12,28},{16,0},{20,4},{24,8},{28,12},{1,17},{... | collective-permute-start | bytes 491528 | tf_op jit(solution)/shard_map/ppermute | solution.py:132
  27.7 17.2 %collective-permute-start.6 = (f32[8,96,128]{2,1,0:T(8,128)S(1)}, f32[8,96,128]{2,1,0:T(8,128)S(1)}, u32[]{:S(2)}, u32[]{:S(2)}) collective-permute-start(f32[8,96,128]{2,1,0:T(8,128)S(1)} %pad_maximum_fusion.12.rest_2_), channel_id=1, source_target_pairs={{0,4},{4,0},{8,12},{12,8},{16,20},{20,16},{24,28},{28,24},{1,5},{5... | collective-permute-start | bytes 1179656 | tf_op jit(solution)/shard_map/ppermute | solution.py:132
  29.5 15.4 %collective-permute-start.5 = (f32[8,112,128]{2,1,0:T(8,128)S(1)}, f32[8,112,128]{2,1,0:T(8,128)S(1)}, u32[]{:S(2)}, u32[]{:S(2)}) collective-permute-start(f32[8,112,128]{2,1,0:T(8,128)S(1)} %pad_maximum_fusion.10.rest_0_), channel_id=1, source_target_pairs={{0,2},{1,3},{2,0},{3,1},{4,6},{5,7},{6,4},{7,5},{8,10},{9,11},{10,... | collective-permute-start | bytes 1376264 | tf_op jit(solution)/shard_map/ppermute | solution.py:134
  33.3 11.6 %collective-permute-start.10 = (f32[2,320,128]{2,1,0:T(8,128)S(1)}, f32[2,320,128]{2,1,0:T(8,128)}, u32[]{:S(2)}, u32[]{:S(2)}) collective-permute-start(f32[2,320,128]{2,1,0:T(8,128)S(1)} %pad_maximum_fusion.13), channel_id=1, source_target_pairs={{0,8},{4,12},{8,0},{12,4},{16,24},{20,28},{24,16},{28,20},{1,9},{5... | collective-permute-start | bytes 983048 | tf_op jit(solution)/shard_map/ppermute | solution.py:132
  33.5 9.6 %collective-permute-start.11 = (f32[1,256,128]{2,1,0:T(8,128)}, f32[1,256,128]{2,1,0:T(8,128)}, u32[]{:S(2)}, u32[]{:S(2)}) collective-permute-start(f32[1,256,128]{2,1,0:T(8,128)} %bitcast.20), channel_id=1, source_target_pairs={{0,16},{4,20},{8,24},{12,28},{16,0},{20,4},{24,8},{28,12},{1,17},{... | collective-permute-start | bytes 393224 | tf_op jit(solution)/shard_map/ppermute | solution.py:132
  48.6 14.0 %collective-permute-start.16 = (f32[4,160,128]{2,1,0:T(8,128)S(1)}, f32[4,160,128]{2,1,0:T(8,128)S(1)}, u32[]{:S(2)}, u32[]{:S(2)}) collective-permute-start(f32[4,160,128]{2,1,0:T(8,128)S(1)} %get-tuple-element.140), channel_id=1, source_target_pairs={{0,4},{4,0},{8,12},{12,8},{16,20},{20,16},{24,28},{28,24},{1,5},{5... | collective-permute-start | bytes 983048 | tf_op jit(solution)/shard_map/ppermute | solution.py:132
  48.9 13.7 %collective-permute-start.17 = (f32[4,160,128]{2,1,0:T(8,128)S(1)}, f32[4,160,128]{2,1,0:T(8,128)S(1)}, u32[]{:S(2)}, u32[]{:S(2)}) collective-permute-start(f32[4,160,128]{2,1,0:T(8,128)S(1)} %get-tuple-element.141), channel_id=1, source_target_pairs={{0,2},{1,3},{2,0},{3,1},{4,6},{5,7},{6,4},{7,5},{8,10},{9,11},{10,... | collective-permute-start | bytes 983048 | tf_op jit(solution)/shard_map/ppermute | solution.py:134
  51.6 11.1 %collective-permute-start.18 = (f32[2,256,128]{2,1,0:T(8,128)S(1)}, f32[2,256,128]{2,1,0:T(8,128)S(1)}, u32[]{:S(2)}, u32[]{:S(2)}) collective-permute-start(f32[2,256,128]{2,1,0:T(8,128)S(1)} %pad_maximum_fusion.15), channel_id=1, source_target_pairs={{0,8},{4,12},{8,0},{12,4},{16,24},{20,28},{24,16},{28,20},{1,9},{5... | collective-permute-start | bytes 786440 | tf_op jit(solution)/shard_map/ppermute | solution.py:132
  62.7 5.0 %collective-permute-start.20 = (f32[2,2,8,512]{3,2,1,0:T(8,128)S(1)}, f32[2,2,8,512]{3,2,1,0:T(8,128)S(1)}, u32[]{:S(2)}, u32[]{:S(2)}) collective-permute-start(f32[2,2,8,512]{3,2,1,0:T(8,128)S(1)} %get-tuple-element.144), channel_id=1, source_target_pairs={{0,2},{1,3},{2,0},{3,1},{4,6},{5,7},{6,4},{7,5},{8,10},{9,11},{10,... | collective-permute-start | bytes 196616 | tf_op jit(solution)/shard_map/ppermute | solution.py:1003
  65.0 17.4 %collective-permute-start.22 = (f32[8,160,128]{2,1,0:T(8,128)S(1)}, f32[8,160,128]{2,1,0:T(8,128)S(1)}, u32[]{:S(2)}, u32[]{:S(2)}) collective-permute-start(f32[8,160,128]{2,1,0:T(8,128)S(1)} %pad_maximum_fusion.3.rest_0_), channel_id=1, source_target_pairs={{0,2},{1,3},{2,0},{3,1},{4,6},{5,7},{6,4},{7,5},{8,10},{9,11},{10,... | collective-permute-start | bytes 1966088 | tf_op jit(solution)/shard_map/ppermute | solution.py:134
  65.6 16.8 %collective-permute-start.23 = (f32[8,160,128]{2,1,0:T(8,128)S(1)}, f32[8,160,128]{2,1,0:T(8,128)S(1)}, u32[]{:S(2)}, u32[]{:S(2)}) collective-permute-start(f32[8,160,128]{2,1,0:T(8,128)S(1)} %pad_maximum_fusion.4.rest_2_), channel_id=1, source_target_pairs={{0,4},{4,0},{8,12},{12,8},{16,20},{20,16},{24,28},{28,24},{1,5},{5... | collective-permute-start | bytes 1966088 | tf_op jit(solution)/shard_map/ppermute | solution.py:132
  67.7 14.7 %collective-permute-start.25 = (f32[8,160,128]{2,1,0:T(8,128)S(1)}, f32[8,160,128]{2,1,0:T(8,128)S(1)}, u32[]{:S(2)}, u32[]{:S(2)}) collective-permute-start(f32[8,160,128]{2,1,0:T(8,128)S(1)} %pad_maximum_fusion.4.rest_2_), channel_id=1, source_target_pairs={{0,1},{1,0},{2,3},{3,2},{4,5},{5,4},{6,7},{7,6},{8,9},{9,8},{10,11... | collective-permute-start | bytes 1966088 | tf_op jit(solution)/shard_map/ppermute | solution.py:134
  68.9 13.6 %collective-permute-start.24 = (f32[8,160,128]{2,1,0:T(8,128)S(1)}, f32[8,160,128]{2,1,0:T(8,128)S(1)}, u32[]{:S(2)}, u32[]{:S(2)}) collective-permute-start(f32[8,160,128]{2,1,0:T(8,128)S(1)} %pad_maximum_fusion.3.rest_0_), channel_id=1, source_target_pairs={{0,1},{1,0},{2,3},{3,2},{4,5},{5,4},{6,7},{7,6},{8,9},{9,8},{10,11... | collective-permute-start | bytes 1966088 | tf_op jit(solution)/shard_map/ppermute | solution.py:134
  82.5 9.7 %collective-permute-start.28 = (f32[8,160,128]{2,1,0:T(8,128)S(1)}, f32[8,160,128]{2,1,0:T(8,128)S(1)}, u32[]{:S(2)}, u32[]{:S(2)}) collective-permute-start(f32[8,160,128]{2,1,0:T(8,128)S(1)} %collective-permute-done.22.rest_4_), channel_id=1, source_target_pairs={{0,1},{1,0},{2,3},{3,2},{4,5},{5,4},{6,7},{7,6},{8,9},{9,8},{10,11... | collective-permute-start | bytes 1966088 | tf_op jit(solution)/shard_map/ppermute | solution.py:134
  82.5 9.6 %collective-permute-start.29 = (f32[8,160,128]{2,1,0:T(8,128)S(1)}, f32[8,160,128]{2,1,0:T(8,128)S(1)}, u32[]{:S(2)}, u32[]{:S(2)}) collective-permute-start(f32[8,160,128]{2,1,0:T(8,128)S(1)} %collective-permute-done.23.rest_6_), channel_id=1, source_target_pairs={{0,1},{1,0},{2,3},{3,2},{4,5},{5,4},{6,7},{7,6},{8,9},{9,8},{10,11... | collective-permute-start | bytes 1966088 | tf_op jit(solution)/shard_map/ppermute | solution.py:134
  83.1 8.4 %collective-permute-start.27 = (f32[4,128,128]{2,1,0:T(8,128)S(1)}, f32[4,128,128]{2,1,0:T(8,128)S(1)}, u32[]{:S(2)}, u32[]{:S(2)}) collective-permute-start(f32[4,128,128]{2,1,0:T(8,128)S(1)} %get-tuple-element.155), channel_id=1, source_target_pairs={{0,2},{1,3},{2,0},{3,1},{4,6},{5,7},{6,4},{7,5},{8,10},{9,11},{10,... | collective-permute-start | bytes 786440 | tf_op jit(solution)/shard_map/ppermute | solution.py:134
  84.1 8.0 %collective-permute-start.26 = (f32[4,128,128]{2,1,0:T(8,128)S(1)}, f32[4,128,128]{2,1,0:T(8,128)S(1)}, u32[]{:S(2)}, u32[]{:S(2)}) collective-permute-start(f32[4,128,128]{2,1,0:T(8,128)S(1)} %get-tuple-element.154), channel_id=1, source_target_pairs={{0,4},{4,0},{8,12},{12,8},{16,20},{20,16},{24,28},{28,24},{1,5},{5... | collective-permute-start | bytes 786440 | tf_op jit(solution)/shard_map/ppermute | solution.py:132
  92.2 6.9 %collective-permute-start.33 = (f32[8,128,128]{2,1,0:T(8,128)S(1)}, f32[8,128,128]{2,1,0:T(8,128)S(1)}, u32[]{:S(2)}, u32[]{:S(2)}) collective-permute-start(f32[8,128,128]{2,1,0:T(8,128)S(1)} %pad_maximum_fusion.9.rest_2_), channel_id=1, source_target_pairs={{0,1},{1,0},{2,3},{3,2},{4,5},{5,4},{6,7},{7,6},{8,9},{9,8},{10,11... | collective-permute-start | bytes 1572872 | tf_op jit(solution)/shard_map/ppermute | solution.py:134
  92.3 6.9 %collective-permute-start.32 = (f32[8,128,128]{2,1,0:T(8,128)S(1)}, f32[8,128,128]{2,1,0:T(8,128)S(1)}, u32[]{:S(2)}, u32[]{:S(2)}) collective-permute-start(f32[8,128,128]{2,1,0:T(8,128)S(1)} %pad_maximum_fusion.8.rest_0_), channel_id=1, source_target_pairs={{0,1},{1,0},{2,3},{3,2},{4,5},{5,4},{6,7},{7,6},{8,9},{9,8},{10,11... | collective-permute-start | bytes 1572872 | tf_op jit(solution)/shard_map/ppermute | solution.py:134
  92.8 13.9 %collective-permute-start.31 = (f32[8,128,128]{2,1,0:T(8,128)S(1)}, f32[8,128,128]{2,1,0:T(8,128)S(1)}, u32[]{:S(2)}, u32[]{:S(2)}) collective-permute-start(f32[8,128,128]{2,1,0:T(8,128)S(1)} %pad_maximum_fusion.9.rest_2_), channel_id=1, source_target_pairs={{0,4},{4,0},{8,12},{12,8},{16,20},{20,16},{24,28},{28,24},{1,5},{5... | collective-permute-start | bytes 1572872 | tf_op jit(solution)/shard_map/ppermute | solution.py:132
  94.3 13.6 %collective-permute-start.30 = (f32[8,128,128]{2,1,0:T(8,128)S(1)}, f32[8,128,128]{2,1,0:T(8,128)S(1)}, u32[]{:S(2)}, u32[]{:S(2)}) collective-permute-start(f32[8,128,128]{2,1,0:T(8,128)S(1)} %pad_maximum_fusion.8.rest_0_), channel_id=1, source_target_pairs={{0,2},{1,3},{2,0},{3,1},{4,6},{5,7},{6,4},{7,5},{8,10},{9,11},{10,... | collective-permute-start | bytes 1572872 | tf_op jit(solution)/shard_map/ppermute | solution.py:134
  135.6 8.0 %collective-permute-start.37 = (f32[16,256,128]{2,1,0:T(8,128)S(1)}, f32[16,256,128]{2,1,0:T(8,128)S(1)}, u32[]{:S(2)}, u32[]{:S(2)}) collective-permute-start(f32[16,256,128]{2,1,0:T(8,128)S(1)} %shard_map.285), channel_id=1, source_target_pairs={{0,1},{1,0},{2,3},{3,2},{4,5},{5,4},{6,7},{7,6},{8,9},{9,8},{10,11... | collective-permute-start | bytes 6291464 | tf_op jit(solution)/shard_map/ppermute | solution.py:134
  135.8 7.8 %collective-permute-start.36 = (f32[16,256,128]{2,1,0:T(8,128)S(1)}, f32[16,256,128]{2,1,0:T(8,128)S(1)}, u32[]{:S(2)}, u32[]{:S(2)}) collective-permute-start(f32[16,256,128]{2,1,0:T(8,128)S(1)} %shard_map.284), channel_id=1, source_target_pairs={{0,1},{1,0},{2,3},{3,2},{4,5},{5,4},{6,7},{7,6},{8,9},{9,8},{10,11... | collective-permute-start | bytes 6291464 | tf_op jit(solution)/shard_map/ppermute | solution.py:134
  136.2 7.4 %collective-permute-start.38 = (f32[16,64,128]{2,1,0:T(8,128)S(1)}, f32[16,64,128]{2,1,0:T(8,128)S(1)}, u32[]{:S(2)}, u32[]{:S(2)}) collective-permute-start(f32[16,64,128]{2,1,0:T(8,128)S(1)} %get-tuple-element.183), channel_id=1, source_target_pairs={{0,1},{1,0},{2,3},{3,2},{4,5},{5,4},{6,7},{7,6},{8,9},{9,8},{10,11... | collective-permute-start | bytes 1572872 | tf_op jit(solution)/shard_map/ppermute | solution.py:134
  145.2 31.9 %collective-permute-start.39 = (f32[8,256,128]{2,1,0:T(8,128)S(1)}, f32[8,256,128]{2,1,0:T(8,128)S(1)}, u32[]{:S(2)}, u32[]{:S(2)}) collective-permute-start(f32[8,256,128]{2,1,0:T(8,128)S(1)} %slice_add_fusion), channel_id=1, source_target_pairs={{0,8},{4,12},{8,0},{12,4},{16,24},{20,28},{24,16},{28,20},{1,9},{5... | collective-permute-start | bytes 3145736 | tf_op jit(solution)/shard_map/ppermute | solution.py:132
  145.5 29.3 %collective-permute-start.42 = (f32[4,320,128]{2,1,0:T(8,128)S(1)}, f32[4,320,128]{2,1,0:T(8,128)S(1)}, u32[]{:S(2)}, u32[]{:S(2)}) collective-permute-start(f32[4,320,128]{2,1,0:T(8,128)S(1)} %pad_maximum_fusion.7), channel_id=1, source_target_pairs={{0,6},{1,7},{2,4},{3,5},{4,2},{5,3},{6,0},{7,1},{8,14},{9,15},{10,... | collective-permute-start | bytes 1966088 | tf_op jit(solution)/shard_map/ppermute | solution.py:137
  146.5 30.6 %collective-permute-start.41 = (f32[4,320,128]{2,1,0:T(8,128)S(1)}, f32[4,320,128]{2,1,0:T(8,128)S(1)}, u32[]{:S(2)}, u32[]{:S(2)}) collective-permute-start(f32[4,320,128]{2,1,0:T(8,128)S(1)} %pad_maximum_fusion.6), channel_id=1, source_target_pairs={{0,2},{1,3},{2,0},{3,1},{4,6},{5,7},{6,4},{7,5},{8,10},{9,11},{10,... | collective-permute-start | bytes 1966088 | tf_op jit(solution)/shard_map/ppermute | solution.py:134
  147.6 29.5 %collective-permute-start.40 = (f32[4,320,128]{2,1,0:T(8,128)S(1)}, f32[4,320,128]{2,1,0:T(8,128)S(1)}, u32[]{:S(2)}, u32[]{:S(2)}) collective-permute-start(f32[4,320,128]{2,1,0:T(8,128)S(1)} %pad_maximum_fusion.5), channel_id=1, source_target_pairs={{0,4},{4,0},{8,12},{12,8},{16,20},{20,16},{24,28},{28,24},{1,5},{5... | collective-permute-start | bytes 1966088 | tf_op jit(solution)/shard_map/ppermute | solution.py:132
  177.1 5.5 %collective-permute-start.43 = (f32[2,2,16,512]{3,2,1,0:T(8,128)S(1)}, f32[2,2,16,512]{3,2,1,0:T(8,128)S(1)}, u32[]{:S(2)}, u32[]{:S(2)}) collective-permute-start(f32[2,2,16,512]{3,2,1,0:T(8,128)S(1)} %get-tuple-element.211), channel_id=1, source_target_pairs={{0,1},{1,0},{2,3},{3,2},{4,5},{5,4},{6,7},{7,6},{8,9},{9,8},{10,11... | collective-permute-start | bytes 393224 | tf_op jit(solution)/shard_map/ppermute | solution.py:1003
  187.6 7.1 %collective-permute-start.46 = (f32[16,192,128]{2,1,0:T(8,128)}, f32[16,192,128]{2,1,0:T(8,128)}, u32[]{:S(2)}, u32[]{:S(2)}) collective-permute-start(f32[16,192,128]{2,1,0:T(8,128)} %get-tuple-element.220), channel_id=1, source_target_pairs={{0,1},{1,0},{2,3},{3,2},{4,5},{5,4},{6,7},{7,6},{8,9},{9,8},{10,11... | collective-permute-start | bytes 4718600 | tf_op jit(solution)/shard_map/ppermute | solution.py:134
  190.3 15.1 %collective-permute-start.51 = (f32[4,256,128]{2,1,0:T(8,128)}, f32[4,256,128]{2,1,0:T(8,128)}, u32[]{:S(2)}, u32[]{:S(2)}) collective-permute-start(f32[4,256,128]{2,1,0:T(8,128)} %fusion), channel_id=1, source_target_pairs={{0,4},{4,0},{8,12},{12,8},{16,20},{20,16},{24,28},{28,24},{1,5},{5... | collective-permute-start | bytes 1572872 | tf_op jit(solution)/shard_map/ppermute | solution.py:132
  197.6 27.0 %collective-permute-start.49 = (f32[4,208,128]{2,1,0:T(8,128)}, f32[4,208,128]{2,1,0:T(8,128)}, u32[]{:S(2)}, u32[]{:S(2)}) collective-permute-start(f32[4,208,128]{2,1,0:T(8,128)} %get-tuple-element.258), channel_id=1, source_target_pairs={{0,6},{1,7},{2,4},{3,5},{4,2},{5,3},{6,0},{7,1},{8,14},{9,15},{10,... | collective-permute-start | bytes 1277960 | tf_op jit(solution)/shard_map/ppermute | solution.py:137
  199.5 26.2 %collective-permute-start.47 = (f32[4,208,128]{2,1,0:T(8,128)}, f32[4,208,128]{2,1,0:T(8,128)}, u32[]{:S(2)}, u32[]{:S(2)}) collective-permute-start(f32[4,208,128]{2,1,0:T(8,128)} %get-tuple-element.260), channel_id=1, source_target_pairs={{0,4},{4,0},{8,12},{12,8},{16,20},{20,16},{24,28},{28,24},{1,5},{5... | collective-permute-start | bytes 1277960 | tf_op jit(solution)/shard_map/ppermute | solution.py:132
  200.1 25.6 %collective-permute-start.48 = (f32[4,208,128]{2,1,0:T(8,128)}, f32[4,208,128]{2,1,0:T(8,128)}, u32[]{:S(2)}, u32[]{:S(2)}) collective-permute-start(f32[4,208,128]{2,1,0:T(8,128)} %get-tuple-element.259), channel_id=1, source_target_pairs={{0,2},{1,3},{2,0},{3,1},{4,6},{5,7},{6,4},{7,5},{8,10},{9,11},{10,... | collective-permute-start | bytes 1277960 | tf_op jit(solution)/shard_map/ppermute | solution.py:134
  208.2 14.4 %collective-permute-start.50 = (f32[2,320,128]{2,1,0:T(8,128)}, f32[2,320,128]{2,1,0:T(8,128)}, u32[]{:S(2)}, u32[]{:S(2)}) collective-permute-start(f32[2,320,128]{2,1,0:T(8,128)} %pad_maximum_fusion.14), channel_id=1, source_target_pairs={{0,8},{4,12},{8,0},{12,4},{16,24},{20,28},{24,16},{28,20},{1,9},{5... | collective-permute-start | bytes 983048 | tf_op jit(solution)/shard_map/ppermute | solution.py:132
  211.9 13.8 %collective-permute-start.52 = (f32[2,256,128]{2,1,0:T(8,128)}, f32[2,256,128]{2,1,0:T(8,128)}, u32[]{:S(2)}, u32[]{:S(2)}) collective-permute-start(f32[2,256,128]{2,1,0:T(8,128)} %fusion.2), channel_id=1, source_target_pairs={{0,16},{4,20},{8,24},{12,28},{16,0},{20,4},{24,8},{28,12},{1,17},{... | collective-permute-start | bytes 786440 | tf_op jit(solution)/shard_map/ppermute | solution.py:132
  227.9 8.9 %collective-permute-start.53 = (f32[1,208,128]{2,1,0:T(8,128)S(1)}, f32[1,208,128]{2,1,0:T(8,128)S(1)}, u32[]{:S(2)}, u32[]{:S(2)}) collective-permute-start(f32[1,208,128]{2,1,0:T(8,128)S(1)} %get-tuple-element.265), channel_id=1, source_target_pairs={{0,8},{4,12},{8,0},{12,4},{16,24},{20,28},{24,16},{28,20},{1,9},{5... | collective-permute-start | bytes 319496 | tf_op jit(solution)/shard_map/ppermute | solution.py:132
  228.3 11.5 %collective-permute-start.54 = (f32[1,208,128]{2,1,0:T(8,128)S(1)}, f32[1,208,128]{2,1,0:T(8,128)S(1)}, u32[]{:S(2)}, u32[]{:S(2)}) collective-permute-start(f32[1,208,128]{2,1,0:T(8,128)S(1)} %get-tuple-element.266), channel_id=1, source_target_pairs={{0,16},{4,20},{8,24},{12,28},{16,0},{20,4},{24,8},{28,12},{1,17},{... | collective-permute-start | bytes 319496 | tf_op jit(solution)/shard_map/ppermute | solution.py:132
  230.5 9.3 %collective-permute-start.55 = (f32[1,208,128]{2,1,0:T(8,128)S(1)}, f32[1,208,128]{2,1,0:T(8,128)S(1)}, u32[]{:S(2)}, u32[]{:S(2)}) collective-permute-start(f32[1,208,128]{2,1,0:T(8,128)S(1)} %get-tuple-element.267), channel_id=1, source_target_pairs={{0,24},{4,28},{8,16},{12,20},{16,8},{20,12},{24,0},{28,4},{1,25},{... | collective-permute-start | bytes 319496 | tf_op jit(solution)/shard_map/ppermute | solution.py:132
  233.6 9.4 %collective-permute-start.58 = (f32[1,256,128]{2,1,0:T(8,128)S(1)}, f32[1,256,128]{2,1,0:T(8,128)S(1)}, u32[]{:S(2)}, u32[]{:S(2)}) collective-permute-start(f32[1,256,128]{2,1,0:T(8,128)S(1)} %fusion.8), channel_id=1, source_target_pairs={{0,2},{1,3},{2,0},{3,1},{4,6},{5,7},{6,4},{7,5},{8,10},{9,11},{10,... | collective-permute-start | bytes 393224 | tf_op jit(solution)/shard_map/ppermute | solution.py:134
  236.5 9.4 %collective-permute-start.57 = (f32[1,320,128]{2,1,0:T(8,128)S(1)}, f32[1,320,128]{2,1,0:T(8,128)S(1)}, u32[]{:S(2)}, u32[]{:S(2)}) collective-permute-start(f32[1,320,128]{2,1,0:T(8,128)S(1)} %pad_maximum_fusion.20), channel_id=1, source_target_pairs={{0,16},{4,20},{8,24},{12,28},{16,0},{20,4},{24,8},{28,12},{1,17},{... | collective-permute-start | bytes 491528 | tf_op jit(solution)/shard_map/ppermute | solution.py:132
  (74 other events, 835.6 us)

commit v3 on v2

--- a/solution.py
+++ b/solution.py
@@ -263,26 +263,24 @@
         self.slots >>= len(group)
         n = self.slots
         count = range(len(self.terms[0]))
-        sizes = [part.shape[1] for part in self.terms[0]]
-        cuts = np.cumsum([0] + sizes)
+        join = len(count) > 1 or rider is not None
         out = []
-        for v in range(1, 1 << len(group)):
+        for v in range(0 if join else 1, 1 << len(group)):
             parts = [sum(term[i][v * n : (v + 1) * n] for term in self.terms) for i in count]
             if rider is not None:
                 parts.append(jnp.broadcast_to(rider[None], (n,) + rider.shape))
             out.append(parts[0] if len(parts) == 1 else jnp.concatenate(parts, axis=1))
-        self.last, self.rode = [], rider
+        if join:
+            self.terms = [[out.pop(0)]]
+        self.last = []
         for v, value in enumerate(out):
             got = self.plan.send(value, self.plan.corner(group, v + 1))
             self.last.append(got)
-            self.terms.append([got[:, a:b] for a, b in zip(cuts[:-1], cuts[1:])])
-            if rider is not None:
-                self.rode = self.rode + got[0, cuts[-1] :]
+            self.terms.append([got])
         return out
 
-    def total(self, *earlier):
-        count = range(len(self.terms[0]))
-        return [sum(term[i][0] for term in self.terms) for i in count]
+    def total(self):
+        return sum(term[0][0] for term in self.terms)
 
 
 def after(value, *earlier):
@@ -1146,23 +1144,26 @@
     down_sum.send(sent)
     up_sum.send(sent)
     gtok = input_grad_stage(gph, gpl, wqh, wql, after(xhat1, sent), inv1, ln, gm)
-    rode = qkv_sum.rode
     gate = (up_sum.last, down_sum.last, gtok)
-    sent = qkv_sum.send(qkv_sum.last, gate, rider=rode)
+    sent = qkv_sum.send(qkv_sum.last, gate)
     while qkv_sum.stages:
-        sent = qkv_sum.send(qkv_sum.last, rider=qkv_sum.rode)
+        sent = qkv_sum.send(qkv_sum.last)
     for total in (down_sum, up_sum):
         while total.stages:
             total.send(gate, sent)
-    sums = qkv_sum.rode
-    sums = (sums + plan.send(sums, ("c",))).reshape(4, width)
-    (g_down,), (g_up, g_out), (g_qkv,) = (t.total() for t in (down_sum, up_sum, qkv_sum))
-    mine = lax.dynamic_slice(sums, (0, me_d * share), (4, share))
+    g_down, g_up = down_sum.total(), up_sum.total()
+    g_up, g_out = g_up[:rows_up], g_up[rows_up:]
     if rows_up % 128 == 0:
         g_up = g_up.reshape(-1, width // fsdp, 128).transpose(1, 0, 2).reshape(-1, rows_up)
     else:
         g_up = g_up.T
     g_down = g_down.reshape(chunks, rows_d, 128).transpose(0, 2, 1).reshape(-1, rows_d)
+    g_out = g_out.T
+    qkv_sum.terms[-1] = after(qkv_sum.terms[-1], g_down, g_up, g_out)
+    g_qkv = qkv_sum.total()
+    g_qkv, sums = g_qkv[:rows_qkv], g_qkv[rows_qkv:]
+    sums = (sums + plan.send(sums, ("c",))).reshape(4, width)
+    mine = lax.dynamic_slice(sums, (0, me_d * share), (4, share))
     shape = tokens.shape
     return (
         output.reshape(shape),
@@ -1170,7 +1171,7 @@
         mine[0],
         mine[1],
         g_qkv.T,
-        g_out.T,
+        g_out,
         mine[2],
         mine[3],
         g_up,

time: 251 us -> 244 us (0.972)
  waiting for transfers between devices: 46.8 us -> 64.3 us
  other arithmetic: 26.8 us -> 15.2 us
  local copies, waits for them, and re-layouts: 29.5 us -> 19.7 us
    ppermute x26, waiting for transfers between devices: 18.8 us -> 28.1 us  [send(): return lax.ppermute(x, 'fsdp', [(i, i ^ f) for i in range(self.fsdp)])]
    ppermute x23, waiting for transfers between devices: 23.9 us -> 30.6 us  [send(): return lax.ppermute(x, 'dp', [(i, i ^ d) for i in range(self.dp)])]
    unnamed x141 -> x131, local copies, waits for them, and re-layouts: 12.7 us -> 6.16 us
    slice x5 -> x2, local copies, waits for them, and re-layouts: 4.47 us -> 0.01 us  [the longest x1 0.01 us: local(): g_up, g_out = (g_up[:rows_up], g_up[rows_up:])]
    add x12 -> x10, other arithmetic: 11.4 us -> 7.31 us  [send(): sum((term[i][v * n:(v + 1) * n] for term in self.terms))]
    transpose x2 -> x0, other arithmetic: 3.14 us -> none  [local(): return (output.reshape(shape), gtok.reshape(shape), mine[0], mine[1], g_q...]
  transfers between devices with their start and end apart: 59 -> 59, of which waited for: 22 -> 26; matrix products, arithmetic and copies ran while one was open for 15% -> 11% of each run, Pallas kernels for 23% -> 24%
where the time goes in v3:
time: 244 us; the launch traced here: 243 us
  Pallas kernels  87.8 us (36%)
  waiting for transfers between devices  64.3 us (26%)
  starting transfers between devices  54.3 us (22%)
  local copies, waits for them, and re-layouts  19.7 us (8%)
  other arithmetic  15.2 us (6%)
    ppermute x23, starting transfers between devices, send(): return lax.ppermute(x, 'dp', [(i, i ^ d) for i in range(self.dp)])  31.9 us
    ppermute x23, waiting for transfers between devices, send(): return lax.ppermute(x, 'dp', [(i, i ^ d) for i in range(self.dp)])  30.6 us
    ppermute x26, waiting for transfers between devices, send(): return lax.ppermute(x, 'fsdp', [(i, i ^ f) for i in range(self.fsdp)])  28.1 us
    pallas_call x2, Pallas kernels, attention_backward(): pl.pallas_call(body, compiler_params=ROOM, cost_estimate=cost(8), grid=(c...  19.7 us
    ppermute x26, starting transfers between devices, send(): return lax.ppermute(x, 'fsdp', [(i, i ^ f) for i in range(self.fsdp)])  13.5 us
    pallas_call x1, Pallas kernels, hidden_stage(): pl.pallas_call(body, compiler_params=ROOM, cost_estimate=cost(15), grid=(...  11.6 us
    pallas_call x2, Pallas kernels, attention_forward(): pl.pallas_call(body, compiler_params=ROOM, cost_estimate=cost(9.5), grid=...  11.2 us
    add x10, other arithmetic, send(): sum((term[i][v * n:(v + 1) * n] for term in self.terms))  7.31 us
  transfers between devices with their start and end apart: 59, of which 26 were waited for; matrix products, arithmetic and copies ran while one was open for 11% of the time, Pallas kernels for 24%

profile of v3, /device:TPU:0, one launch (start us, length us, event | category | flops | bytes accessed | tf_op | source)
XLA Modules:
  0.0 243.2 jit_solution(3397200114678720595)
XLA Ops:
  3.1 5.0 %collective-permute-start.2 = (f32[1,208,128]{2,1,0:T(8,128)S(1)}, f32[1,208,128]{2,1,0:T(8,128)S(1)}, u32[]{:S(2)}, u32[]{:S(2)}) collective-permute-start(f32[1,208,128]{2,1,0:T(8,128)S(1)} %bitcast.95), channel_id=1, source_target_pairs={{0,24},{4,28},{8,16},{12,20},{16,8},{20,12},{24,0},{28,4},{1,25},{... | collective-permute-start | bytes 319496 | tf_op jit(solution)/shard_map/ppermute | solution.py:132
  17.9 1.7 collective-permute-start.9
  19.7 2.1 collective-permute-start.7
  22.4 1.7 collective-permute-start.3
  24.8 3.9 %collective-permute-done.4 = f32[4,96,128]{2,1,0:T(8,128)S(1)} collective-permute-done((f32[4,96,128]{2,1,0:T(8,128)S(1)}, f32[4,96,128]{2,1,0:T(8,128)S(1)}, u32[]{:S(2)}, u32[]{:S(2)}) %collective-permute-start.4) | collective-permute-done | bytes 196640 | tf_op jit(solution)/shard_map/ppermute | solution.py:134
  29.7 1.7 collective-permute-start.6
  31.4 1.5 collective-permute-start.5
  33.9 2.1 collective-permute-start.10
  37.3 2.1 concatenate.86.outer_bias
  39.4 4.9 %collective-permute-done.11 = f32[1,256,128]{2,1,0:T(8,128)} collective-permute-done((f32[1,256,128]{2,1,0:T(8,128)}, f32[1,256,128]{2,1,0:T(8,128)}, u32[]{:S(2)}, u32[]{:S(2)}) %collective-permute-start.11) | collective-permute-done | bytes 131104 | tf_op jit(solution)/shard_map/ppermute | solution.py:132
  50.6 2.2 collective-permute-start.18
  55.9 5.5 %shard_map.276 = (f32[512,1536]{1,0:T(8,128)S(1)}, bf16[1536,512]{1,0:T(8,128)(2,1)S(1)}, bf16[1536,512]{1,0:T(8,128)(2,1)S(1)}, f32[512,512]{1,0:T(8,128)S(1)},...) custom-call(s32[2]{0:T(128)S(1)} %copy-done.37, ...), custom_call_target="tpu_custom_call" | custom-call | flops 333000000 | bytes 925000 | tf_op jit(solution)/shard_map/pallas_call | solution.py:365
  63.6 1.6 collective-permute-start.22
  65.6 1.9 collective-permute-done.20
  68.2 5.6 %shard_map.277 = (f32[512,512]{1,0:T(8,128)S(1)}, f32[512,512]{1,0:T(8,128)S(1)}) custom-call(f32[512,1536]{1,0:T(8,128)S(1)} %get-tuple-element.151.q.k.v, f32[512,1536]{1,0:T(8,128)S(1)} %get-tuple-element.151.q.k.v, f32[512,1536]{1,0:T(8,128)S(1)} %get-tuple-element.151.q.k.v, f32[2,2,32,512]{3,2,1,0:T(8,128)S(1)} %constant_dynamic-update-slice_fusion.2.fk.fv, ...), custom_call_target="tpu_custom_call" | custom-call | flops 427500000 | bytes 1187500 | tf_op jit(solution)/shard_map/pallas_call | solution.py:492
  73.8 7.6 %collective-permute-done.22.rest_4_ = f32[8,160,128]{2,1,0:T(8,128)S(1)} collective-permute-done((f32[8,160,128]{2,1,0:T(8,128)S(1)}, f32[8,160,128]{2,1,0:T(8,128)S(1)}, u32[]{:S(2)}, u32[]{:S(2)}) %collective-permute-start.22) | collective-permute-done | bytes 655392 | tf_op jit(solution)/shard_map/ppermute | solution.py:134
  83.6 5.6 %shard_map.278 = (f32[512,512]{1,0:T(8,128)S(1)}, f32[512,512]{1,0:T(8,128)S(1)}) custom-call(f32[512,1536]{1,0:T(8,128)S(1)} %get-tuple-element.151.q.k.v, f32[512,1536]{1,0:T(8,128)S(1)} %get-tuple-element.151.q.k.v, f32[512,1536]{1,0:T(8,128)S(1)} %get-tuple-element.151.q.k.v, ...), custom_call_target="tpu_custom_call", output_to_operand_aliasing={{0}: (10, {}), {1}: (11, {})} | custom-call | flops 427500000 | bytes 1187500 | tf_op jit(solution)/shard_map/pallas_call | solution.py:492
  92.2 1.6 collective-permute-start.31
  93.8 2.4 shard_map.279
  97.5 6.2 %collective-permute-done.30.rest_4_ = f32[8,128,128]{2,1,0:T(8,128)S(1)} collective-permute-done((f32[8,128,128]{2,1,0:T(8,128)S(1)}, f32[8,128,128]{2,1,0:T(8,128)S(1)}, u32[]{:S(2)}, u32[]{:S(2)}) %collective-permute-start.30) | collective-permute-done | bytes 524320 | tf_op jit(solution)/shard_map/ppermute | solution.py:134
  103.7 2.3 collective-permute-done.31.rest_6_
  106.6 1.4 collective-permute-done.34.rest_5_
  108.8 11.6 %shard_map.281 = (bf16[512,2048]{1,0:T(8,128)(2,1)S(1)}, bf16[512,2048]{1,0:T(8,128)(2,1)S(1)}, bf16[512,2048]{1,0:T(8,128)(2,1)S(1)}, bf16[512,2048]{1,0:T(8,12...) custom-call(s32[2]{0:T(128)S(1)} %copy-done.37, ...), custom_call_target="tpu_custom_call" | custom-call | flops 675000000 | bytes 1875000 | tf_op jit(solution)/shard_map/pallas_call | solution.py:691
  120.4 5.0 %shard_map.282 = (f32[512,512]{1,0:T(8,128)S(1)}, f32[8,512]{1,0:T(8,128)S(1)}) custom-call(f32[512,512]{1,0:T(8,128)S(1)} %bitcast.92, f32[512,512]{1,0:T(8,128)S(1)} %get-tuple-element.171.xhat_ref, f32[512,128]{1,0:T(8,128)S(1)} %get-tuple-element.163.inv_ref, f32[8,512]{1,0:T(8,128)S(1)} %get-tuple-element.164.ln_ref.ln_r, ...), custom_call_target="tpu_custom_call" | custom-call | flops 382500000 | bytes 1062500 | tf_op jit(solution)/shard_map/pallas_call | solution.py:851
  125.4 2.4 %shard_map.283 = (f32[512,512]{1,0:T(8,128)S(1)}, f32[16,64,128]{2,1,0:T(8,128)S(1)}, f32[16,64,128]{2,1,0:T(8,128)S(1)}) custom-call(s32[2]{0:T(128)S(1)} %copy-done.37, f32[512,512]{1,0:T(8,128)S(1)} %get-tuple-element.178.gm_ref.gm_r, f32[512,512]{1,0:T(8,128)S(1)} %get-tuple-element.152.att.rest_0_, ...), custom_call_target="tpu_custom_call" | custom-call | flops 225000000 | bytes 625000 | tf_op jit(solution)/shard_map/pallas_call | solution.py:883
  127.8 2.7 %shard_map.284 = f32[16,256,128]{2,1,0:T(8,128)S(1)} custom-call(s32[2]{0:T(128)S(1)} %copy-done.37, bf16[512,512]{1,0:T(8,128)(2,1)S(1)} %get-tuple-element.189.c0, bf16[512,512]{1,0:T(8,128)(2,1)S(1)} %get-tuple-element.184.c1, bf16[512,2048]{1,0:T(8,128)(2,1)S(1)} %get-tuple-element.185.h0, bf16[512,2048]{1,0:T(8,128)(2,1)S(1)} %get-tuple-element.186.h1), custom_call_target="tpu_custom_call" | custom-call | flops 12150000 | bytes 33750 | tf_op jit(solution)/shard_map/pallas_call | solution.py:730
  130.6 3.2 %shard_map.285 = f32[16,256,128]{2,1,0:T(8,128)S(1)} custom-call(s32[2]{0:T(128)S(1)} %copy-done.37, bf16[512,512]{1,0:T(8,128)(2,1)S(1)} %get-tuple-element.190.n0, bf16[512,512]{1,0:T(8,128)(2,1)S(1)} %get-tuple-element.188.n1, bf16[512,2048]{1,0:T(8,128)(2,1)S(1)} %get-tuple-element.174.p0, bf16[512,2048]{1,0:T(8,128)(2,1)S(1)} %get-tuple-element.175.p1), custom_call_target="tpu_custom_call" | custom-call | flops 14400000 | bytes 40000 | tf_op jit(solution)/shard_map/pallas_call | solution.py:783
  134.4 2.7 %shard_map.286 = f32[16,256,128]{2,1,0:T(8,128)S(1)} custom-call(s32[2]{0:T(128)S(1)} %copy-done.37, bf16[512,512]{1,0:T(8,128)(2,1)S(1)} %get-tuple-element.189.c0, bf16[512,512]{1,0:T(8,128)(2,1)S(1)} %get-tuple-element.184.c1, bf16[512,2048]{1,0:T(8,128)(2,1)S(1)} %get-tuple-element.185.h0, bf16[512,2048]{1,0:T(8,128)(2,1)S(1)} %get-tuple-element.186.h1), custom_call_target="tpu_custom_call" | custom-call | flops 12150000 | bytes 33750 | tf_op jit(solution)/shard_map/pallas_call | solution.py:730
  137.1 3.2 %shard_map.287 = f32[16,256,128]{2,1,0:T(8,128)S(1)} custom-call(s32[2]{0:T(128)S(1)} %copy-done.37, bf16[512,512]{1,0:T(8,128)(2,1)S(1)} %get-tuple-element.190.n0, bf16[512,512]{1,0:T(8,128)(2,1)S(1)} %get-tuple-element.188.n1, bf16[512,2048]{1,0:T(8,128)(2,1)S(1)} %get-tuple-element.174.p0, bf16[512,2048]{1,0:T(8,128)(2,1)S(1)} %get-tuple-element.175.p1), custom_call_target="tpu_custom_call" | custom-call | flops 14400000 | bytes 40000 | tf_op jit(solution)/shard_map/pallas_call | solution.py:783
  140.3 1.4 collective-permute-done.38
  146.8 1.7 collective-permute-start.42
  148.5 9.7 %shard_map.288 = (f32[512,512]{1,0:T(8,128)S(1)}, f32[512,512]{1,0:T(8,128)S(1)}, f32[512,512]{1,0:T(8,128)S(1)}, f32[2,2,16,512]{3,2,1,0:T(8,128)S(1)}, f32[2,2...) custom-call(f32[512,1536]{1,0:T(8,128)S(1)} %get-tuple-element.151.q.k.v, f32[512,1536]{1,0:T(8,128)S(1)} %get-tuple-element.151.q.k.v, ...), custom_call_target="tpu_custom_call" | custom-call | flops 360000000 | bytes 1000000 | tf_op jit(solution)/shard_map/pallas_call | solution.py:564
  158.3 10.0 %shard_map.289 = (f32[512,512]{1,0:T(8,128)S(1)}, f32[512,512]{1,0:T(8,128)S(1)}, f32[512,512]{1,0:T(8,128)S(1)}, f32[2,2,16,512]{3,2,1,0:T(8,128)S(1)}, f32[2,2...) custom-call(f32[512,1536]{1,0:T(8,128)S(1)} %get-tuple-element.151.q, ...), custom_call_target="tpu_custom_call", output_to_operand_aliasing={{0}: (13, {}), {1}: (14, {}), {2}: (15, {}), {3}: (16, {}),... | custom-call | flops 360000000 | bytes 1000000 | tf_op jit(solution)/shard_map/pallas_call | solution.py:564
  168.3 5.8 %shard_map.290 = f32[512,512]{1,0:T(8,128)} custom-call(f32[512,512]{1,0:T(8,128)S(1)} %get-tuple-element.209.mid, bf16[512,2048]{1,0:T(8,128)(2,1)S(1)} %get-tuple-element.185.h0, bf16[512,2048]{1,0:T(8,128)(2,1)S(1)} %get-tuple-element.186.h1, bf16[512,2048]{1,0:T(8,128)(2,1)S(1)} %get-tuple-element.172.d0, bf16[512,2048]{1,0:T(8,128)(2,1)S(1)} %copy-done.11), custom_call_target="tpu_custom_call" | custom-call | flops 360000000 | bytes 1000000 | tf_op jit(solution)/shard_map/pallas_call | solution.py:815
  174.1 2.2 collective-permute-done.41
  178.2 3.0 %collective-permute-done.44.g5a_r = f32[2,2,8,512]{3,2,1,0:T(8,128)S(1)} collective-permute-done((f32[2,2,8,512]{3,2,1,0:T(8,128)S(1)}, f32[2,2,8,512]{3,2,1,0:T(8,128)S(1)}, u32[]{:S(2)}, u32[]{:S(2)}) %collective-permute-start.44) | collective-permute-done | bytes 65568 | tf_op jit(solution)/shard_map/ppermute | solution.py:1001
  183.1 3.7 %shard_map.292 = (f32[16,192,128]{2,1,0:T(8,128)}, f32[8,512]{1,0:T(8,128)S(1)}) custom-call(s32[2]{0:T(128)S(1)} %copy-done.37, bf16[512,1536]{1,0:T(8,128)(2,1)S(1)} %get-tuple-element.213.gph_r, bf16[512,1536]{1,0:T(8,128)(2,1)S(1)} %get-tuple-element.214.gpl_r, f32[1536,128]{1,0:T(8,128)S(1)} %get-tuple-element.218.col_r, ...), custom_call_target="tpu_custom_call" | custom-call | flops 11250000 | bytes 31250 | tf_op jit(solution)/shard_map/pallas_call | solution.py:983
  189.0 2.6 %shard_map.293 = (f32[16,192,128]{2,1,0:T(8,128)S(1)}, f32[8,512]{1,0:T(8,128)S(1)}) custom-call(s32[2]{0:T(128)S(1)} %copy-done.37, bf16[512,1536]{1,0:T(8,128)(2,1)S(1)} %get-tuple-element.213.gph_r, bf16[512,1536]{1,0:T(8,128)(2,1)S(1)} %get-tuple-element.214.gpl_r, f32[1536,128]{1,0:T(8,128)S(1)} %get-tuple-element.218.col_r, ...), custom_call_target="tpu_custom_call" | custom-call | flops 11250000 | bytes 31250 | tf_op jit(solution)/shard_map/pallas_call | solution.py:983
  192.8 2.2 slice_add_fusion.6
  195.1 1.6 collective-permute-start.49
  198.7 4.3 %collective-permute-done.51 = f32[4,256,128]{2,1,0:T(8,128)} collective-permute-done((f32[4,256,128]{2,1,0:T(8,128)}, f32[4,256,128]{2,1,0:T(8,128)}, u32[]{:S(2)}, u32[]{:S(2)}) %collective-permute-start.51) | collective-permute-done | bytes 524320 | tf_op jit(solution)/shard_map/ppermute | solution.py:132
  203.2 1.6 collective-permute-start.50
  205.9 1.8 collective-permute-start.52
  207.7 3.8 %shard_map.294 = f32[512,512]{1,0:T(8,128)} custom-call(bf16[512,1536]{1,0:T(8,128)(2,1)S(1)} %copy-done.3, bf16[512,1536]{1,0:T(8,128)(2,1)S(1)} %copy-done.5, bf16[1536,512]{1,0:T(8,128)(2,1)S(1)} %get-tuple-element.215.wh_r.wh, bf16[1536,512]{1,0:T(8,128)(2,1)S(1)} %get-tuple-element.216.wl_r.wl, f32[512,512]{1,0:T(8,128)S(1)} %copy-done.8, ...), custom_call_target="tpu_custom_call" | custom-call | flops 333000000 | bytes 925000 | tf_op jit(solution)/shard_map/pallas_call | solution.py:935
  211.5 7.8 %collective-permute-done.52 = f32[2,256,128]{2,1,0:T(8,128)S(1)} collective-permute-done((f32[2,256,128]{2,1,0:T(8,128)S(1)}, f32[2,256,128]{2,1,0:T(8,128)S(1)}, u32[]{:S(2)}, u32[]{:S(2)}) %collective-permute-start.52) | collective-permute-done | bytes 262176 | tf_op jit(solution)/shard_map/ppermute | solution.py:132
  220.7 2.2 collective-permute-start.54
  228.7 2.6 %collective-permute-done.56 = f32[1,256,128]{2,1,0:T(8,128)S(1)} collective-permute-done((f32[1,256,128]{2,1,0:T(8,128)S(1)}, f32[1,256,128]{2,1,0:T(8,128)S(1)}, u32[]{:S(2)}, u32[]{:S(2)}) %collective-permute-start.56) | collective-permute-done | bytes 131104 | tf_op jit(solution)/shard_map/ppermute | solution.py:134
  233.0 6.9 %collective-permute-done.57 = f32[1,320,128]{2,1,0:T(8,128)S(1)} collective-permute-done((f32[1,320,128]{2,1,0:T(8,128)S(1)}, f32[1,320,128]{2,1,0:T(8,128)S(1)}, u32[]{:S(2)}, u32[]{:S(2)}) %collective-permute-start.57) | collective-permute-done | bytes 163872 | tf_op jit(solution)/shard_map/ppermute | solution.py:132
  (323 shorter events, 65.0 us)
Async XLA Ops:
  3.1 14.8 %collective-permute-start.2 = (f32[1,208,128]{2,1,0:T(8,128)S(1)}, f32[1,208,128]{2,1,0:T(8,128)S(1)}, u32[]{:S(2)}, u32[]{:S(2)}) collective-permute-start(f32[1,208,128]{2,1,0:T(8,128)S(1)} %bitcast.95), channel_id=1, source_target_pairs={{0,24},{4,28},{8,16},{12,20},{16,8},{20,12},{24,0},{28,4},{1,25},{... | collective-permute-start | bytes 319496 | tf_op jit(solution)/shard_map/ppermute | solution.py:132
  8.2 9.7 %collective-permute-start.1 = (f32[1,208,128]{2,1,0:T(8,128)S(1)}, f32[1,208,128]{2,1,0:T(8,128)S(1)}, u32[]{:S(2)}, u32[]{:S(2)}) collective-permute-start(f32[1,208,128]{2,1,0:T(8,128)S(1)} %bitcast.96), channel_id=1, source_target_pairs={{0,16},{4,20},{8,24},{12,28},{16,0},{20,4},{24,8},{28,12},{1,17},{... | collective-permute-start | bytes 319496 | tf_op jit(solution)/shard_map/ppermute | solution.py:132
  8.2 9.7 %collective-permute-start = (f32[1,208,128]{2,1,0:T(8,128)S(1)}, f32[1,208,128]{2,1,0:T(8,128)S(1)}, u32[]{:S(2)}, u32[]{:S(2)}) collective-permute-start(f32[1,208,128]{2,1,0:T(8,128)S(1)} %bitcast.97), channel_id=1, source_target_pairs={{0,8},{4,12},{8,0},{12,4},{16,24},{20,28},{24,16},{28,20},{1,9},{5... | collective-permute-start | bytes 319496 | tf_op jit(solution)/shard_map/ppermute | solution.py:132
  8.8 8.5 %collective-permute-start.8 = (s32[2,256]{1,0:T(2,128)}, s32[2,256]{1,0:T(2,128)S(1)}, u32[]{:S(2)}, u32[]{:S(2)}) collective-permute-start(s32[2,256]{1,0:T(2,128)} %param.22), channel_id=1, source_target_pairs={{0,1},{1,0},{2,3},{3,2},{4,5},{5,4},{6,7},{7,6},{8,9},{9,8},{10,11... | collective-permute-start | bytes 6152 | tf_op jit(solution)/shard_map/ppermute | solution.py:1001
  17.9 6.2 %collective-permute-start.9 = (s32[2,2,256]{2,1,0:T(2,128)S(1)}, s32[2,2,256]{2,1,0:T(2,128)S(1)}, u32[]{:S(2)}, u32[]{:S(2)}) collective-permute-start(s32[2,2,256]{2,1,0:T(2,128)S(1)} %pad_add_fusion), channel_id=1, source_target_pairs={{0,2},{1,3},{2,0},{3,1},{4,6},{5,7},{6,4},{7,5},{8,10},{9,11},{10,... | collective-permute-start | bytes 12296 | tf_op jit(solution)/shard_map/ppermute | solution.py:1001
  19.7 13.2 %collective-permute-start.7 = (f32[1,320,128]{2,1,0:T(8,128)S(1)}, f32[1,320,128]{2,1,0:T(8,128)}, u32[]{:S(2)}, u32[]{:S(2)}) collective-permute-start(f32[1,320,128]{2,1,0:T(8,128)S(1)} %maximum_bitcast_fusion), channel_id=1, source_target_pairs={{0,16},{4,20},{8,24},{12,28},{16,0},{20,4},{24,8},{28,12},{1,17},{... | collective-permute-start | bytes 491528 | tf_op jit(solution)/shard_map/ppermute | solution.py:132
  21.8 6.8 %collective-permute-start.4 = (f32[4,96,128]{2,1,0:T(8,128)S(1)}, f32[4,96,128]{2,1,0:T(8,128)S(1)}, u32[]{:S(2)}, u32[]{:S(2)}) collective-permute-start(f32[4,96,128]{2,1,0:T(8,128)S(1)} %pad_maximum_fusion.15), channel_id=1, source_target_pairs={{0,2},{1,3},{2,0},{3,1},{4,6},{5,7},{6,4},{7,5},{8,10},{9,11},{10,... | collective-permute-start | bytes 589832 | tf_op jit(solution)/shard_map/ppermute | solution.py:134
  22.4 7.2 %collective-permute-start.3 = (f32[4,112,128]{2,1,0:T(8,128)S(1)}, f32[4,112,128]{2,1,0:T(8,128)S(1)}, u32[]{:S(2)}, u32[]{:S(2)}) collective-permute-start(f32[4,112,128]{2,1,0:T(8,128)S(1)} %slice.438), channel_id=1, source_target_pairs={{0,4},{4,0},{8,12},{12,8},{16,20},{20,16},{24,28},{28,24},{1,5},{5... | collective-permute-start | bytes 688136 | tf_op jit(solution)/shard_map/ppermute | solution.py:132
  29.7 15.3 %collective-permute-start.6 = (f32[8,96,128]{2,1,0:T(8,128)S(1)}, f32[8,96,128]{2,1,0:T(8,128)S(1)}, u32[]{:S(2)}, u32[]{:S(2)}) collective-permute-start(f32[8,96,128]{2,1,0:T(8,128)S(1)} %pad_maximum_fusion.12.rest_2_), channel_id=1, source_target_pairs={{0,4},{4,0},{8,12},{12,8},{16,20},{20,16},{24,28},{28,24},{1,5},{5... | collective-permute-start | bytes 1179656 | tf_op jit(solution)/shard_map/ppermute | solution.py:132
  31.4 13.6 %collective-permute-start.5 = (f32[8,112,128]{2,1,0:T(8,128)S(1)}, f32[8,112,128]{2,1,0:T(8,128)S(1)}, u32[]{:S(2)}, u32[]{:S(2)}) collective-permute-start(f32[8,112,128]{2,1,0:T(8,128)S(1)} %pad_maximum_fusion.10.rest_0_), channel_id=1, source_target_pairs={{0,2},{1,3},{2,0},{3,1},{4,6},{5,7},{6,4},{7,5},{8,10},{9,11},{10,... | collective-permute-start | bytes 1376264 | tf_op jit(solution)/shard_map/ppermute | solution.py:134
  33.9 11.1 %collective-permute-start.10 = (f32[2,320,128]{2,1,0:T(8,128)S(1)}, f32[2,320,128]{2,1,0:T(8,128)}, u32[]{:S(2)}, u32[]{:S(2)}) collective-permute-start(f32[2,320,128]{2,1,0:T(8,128)S(1)} %pad_maximum_fusion.13), channel_id=1, source_target_pairs={{0,8},{4,12},{8,0},{12,4},{16,24},{20,28},{24,16},{28,20},{1,9},{5... | collective-permute-start | bytes 983048 | tf_op jit(solution)/shard_map/ppermute | solution.py:132
  36.1 8.2 %collective-permute-start.11 = (f32[1,256,128]{2,1,0:T(8,128)}, f32[1,256,128]{2,1,0:T(8,128)}, u32[]{:S(2)}, u32[]{:S(2)}) collective-permute-start(f32[1,256,128]{2,1,0:T(8,128)} %bitcast.20), channel_id=1, source_target_pairs={{0,16},{4,20},{8,24},{12,28},{16,0},{20,4},{24,8},{28,12},{1,17},{... | collective-permute-start | bytes 393224 | tf_op jit(solution)/shard_map/ppermute | solution.py:132
  48.7 12.8 %collective-permute-start.16 = (f32[4,160,128]{2,1,0:T(8,128)S(1)}, f32[4,160,128]{2,1,0:T(8,128)S(1)}, u32[]{:S(2)}, u32[]{:S(2)}) collective-permute-start(f32[4,160,128]{2,1,0:T(8,128)S(1)} %get-tuple-element.139), channel_id=1, source_target_pairs={{0,4},{4,0},{8,12},{12,8},{16,20},{20,16},{24,28},{28,24},{1,5},{5... | collective-permute-start | bytes 983048 | tf_op jit(solution)/shard_map/ppermute | solution.py:132
  49.1 12.3 %collective-permute-start.17 = (f32[4,160,128]{2,1,0:T(8,128)S(1)}, f32[4,160,128]{2,1,0:T(8,128)S(1)}, u32[]{:S(2)}, u32[]{:S(2)}) collective-permute-start(f32[4,160,128]{2,1,0:T(8,128)S(1)} %get-tuple-element.140), channel_id=1, source_target_pairs={{0,2},{1,3},{2,0},{3,1},{4,6},{5,7},{6,4},{7,5},{8,10},{9,11},{10,... | collective-permute-start | bytes 983048 | tf_op jit(solution)/shard_map/ppermute | solution.py:134
  50.6 10.8 %collective-permute-start.18 = (f32[2,256,128]{2,1,0:T(8,128)S(1)}, f32[2,256,128]{2,1,0:T(8,128)S(1)}, u32[]{:S(2)}, u32[]{:S(2)}) collective-permute-start(f32[2,256,128]{2,1,0:T(8,128)S(1)} %pad_maximum_fusion.14), channel_id=1, source_target_pairs={{0,8},{4,12},{8,0},{12,4},{16,24},{20,28},{24,16},{28,20},{1,9},{5... | collective-permute-start | bytes 786440 | tf_op jit(solution)/shard_map/ppermute | solution.py:132
  61.5 5.9 %collective-permute-start.21 = (f32[2,2,8,512]{3,2,1,0:T(8,128)S(1)}, f32[2,2,8,512]{3,2,1,0:T(8,128)S(1)}, u32[]{:S(2)}, u32[]{:S(2)}) collective-permute-start(f32[2,2,8,512]{3,2,1,0:T(8,128)S(1)} %get-tuple-element.143), channel_id=1, source_target_pairs={{0,3},{1,2},{2,1},{3,0},{4,7},{5,6},{6,5},{7,4},{8,11},{9,10},{10,... | collective-permute-start | bytes 196616 | tf_op jit(solution)/shard_map/ppermute | solution.py:1001
  62.0 5.5 %collective-permute-start.20 = (f32[2,2,8,512]{3,2,1,0:T(8,128)S(1)}, f32[2,2,8,512]{3,2,1,0:T(8,128)S(1)}, u32[]{:S(2)}, u32[]{:S(2)}) collective-permute-start(f32[2,2,8,512]{3,2,1,0:T(8,128)S(1)} %get-tuple-element.143), channel_id=1, source_target_pairs={{0,2},{1,3},{2,0},{3,1},{4,6},{5,7},{6,4},{7,5},{8,10},{9,11},{10,... | collective-permute-start | bytes 196616 | tf_op jit(solution)/shard_map/ppermute | solution.py:1001
  63.6 17.9 %collective-permute-start.22 = (f32[8,160,128]{2,1,0:T(8,128)S(1)}, f32[8,160,128]{2,1,0:T(8,128)S(1)}, u32[]{:S(2)}, u32[]{:S(2)}) collective-permute-start(f32[8,160,128]{2,1,0:T(8,128)S(1)} %pad_maximum_fusion.3.rest_0_), channel_id=1, source_target_pairs={{0,2},{1,3},{2,0},{3,1},{4,6},{5,7},{6,4},{7,5},{8,10},{9,11},{10,... | collective-permute-start | bytes 1966088 | tf_op jit(solution)/shard_map/ppermute | solution.py:134
  65.2 16.4 %collective-permute-start.23 = (f32[8,160,128]{2,1,0:T(8,128)S(1)}, f32[8,160,128]{2,1,0:T(8,128)S(1)}, u32[]{:S(2)}, u32[]{:S(2)}) collective-permute-start(f32[8,160,128]{2,1,0:T(8,128)S(1)} %pad_maximum_fusion.4.rest_2_), channel_id=1, source_target_pairs={{0,4},{4,0},{8,12},{12,8},{16,20},{20,16},{24,28},{28,24},{1,5},{5... | collective-permute-start | bytes 1966088 | tf_op jit(solution)/shard_map/ppermute | solution.py:132
  67.5 14.0 %collective-permute-start.24 = (f32[8,160,128]{2,1,0:T(8,128)S(1)}, f32[8,160,128]{2,1,0:T(8,128)S(1)}, u32[]{:S(2)}, u32[]{:S(2)}) collective-permute-start(f32[8,160,128]{2,1,0:T(8,128)S(1)} %pad_maximum_fusion.3.rest_0_), channel_id=1, source_target_pairs={{0,1},{1,0},{2,3},{3,2},{4,5},{5,4},{6,7},{7,6},{8,9},{9,8},{10,11... | collective-permute-start | bytes 1966088 | tf_op jit(solution)/shard_map/ppermute | solution.py:134
  67.6 13.9 %collective-permute-start.25 = (f32[8,160,128]{2,1,0:T(8,128)S(1)}, f32[8,160,128]{2,1,0:T(8,128)S(1)}, u32[]{:S(2)}, u32[]{:S(2)}) collective-permute-start(f32[8,160,128]{2,1,0:T(8,128)S(1)} %pad_maximum_fusion.4.rest_2_), channel_id=1, source_target_pairs={{0,1},{1,0},{2,3},{3,2},{4,5},{5,4},{6,7},{7,6},{8,9},{9,8},{10,11... | collective-permute-start | bytes 1966088 | tf_op jit(solution)/shard_map/ppermute | solution.py:134
  81.5 9.1 %collective-permute-start.28 = (f32[8,160,128]{2,1,0:T(8,128)S(1)}, f32[8,160,128]{2,1,0:T(8,128)S(1)}, u32[]{:S(2)}, u32[]{:S(2)}) collective-permute-start(f32[8,160,128]{2,1,0:T(8,128)S(1)} %collective-permute-done.22.rest_4_), channel_id=1, source_target_pairs={{0,1},{1,0},{2,3},{3,2},{4,5},{5,4},{6,7},{7,6},{8,9},{9,8},{10,11... | collective-permute-start | bytes 1966088 | tf_op jit(solution)/shard_map/ppermute | solution.py:134
  81.6 9.1 %collective-permute-start.29 = (f32[8,160,128]{2,1,0:T(8,128)S(1)}, f32[8,160,128]{2,1,0:T(8,128)S(1)}, u32[]{:S(2)}, u32[]{:S(2)}) collective-permute-start(f32[8,160,128]{2,1,0:T(8,128)S(1)} %collective-permute-done.23.rest_6_), channel_id=1, source_target_pairs={{0,1},{1,0},{2,3},{3,2},{4,5},{5,4},{6,7},{7,6},{8,9},{9,8},{10,11... | collective-permute-start | bytes 1966088 | tf_op jit(solution)/shard_map/ppermute | solution.py:134
  82.1 8.4 %collective-permute-start.26 = (f32[4,128,128]{2,1,0:T(8,128)S(1)}, f32[4,128,128]{2,1,0:T(8,128)S(1)}, u32[]{:S(2)}, u32[]{:S(2)}) collective-permute-start(f32[4,128,128]{2,1,0:T(8,128)S(1)} %get-tuple-element.153), channel_id=1, source_target_pairs={{0,4},{4,0},{8,12},{12,8},{16,20},{20,16},{24,28},{28,24},{1,5},{5... | collective-permute-start | bytes 786440 | tf_op jit(solution)/shard_map/ppermute | solution.py:132
  82.6 8.0 %collective-permute-start.27 = (f32[4,128,128]{2,1,0:T(8,128)S(1)}, f32[4,128,128]{2,1,0:T(8,128)S(1)}, u32[]{:S(2)}, u32[]{:S(2)}) collective-permute-start(f32[4,128,128]{2,1,0:T(8,128)S(1)} %get-tuple-element.154), channel_id=1, source_target_pairs={{0,2},{1,3},{2,0},{3,1},{4,6},{5,7},{6,4},{7,5},{8,10},{9,11},{10,... | collective-permute-start | bytes 786440 | tf_op jit(solution)/shard_map/ppermute | solution.py:134
  90.7 13.0 %collective-permute-start.30 = (f32[8,128,128]{2,1,0:T(8,128)S(1)}, f32[8,128,128]{2,1,0:T(8,128)S(1)}, u32[]{:S(2)}, u32[]{:S(2)}) collective-permute-start(f32[8,128,128]{2,1,0:T(8,128)S(1)} %pad_maximum_fusion.8.rest_0_), channel_id=1, source_target_pairs={{0,2},{1,3},{2,0},{3,1},{4,6},{5,7},{6,4},{7,5},{8,10},{9,11},{10,... | collective-permute-start | bytes 1572872 | tf_op jit(solution)/shard_map/ppermute | solution.py:134
  91.7 5.8 %collective-permute-start.32 = (f32[8,128,128]{2,1,0:T(8,128)S(1)}, f32[8,128,128]{2,1,0:T(8,128)S(1)}, u32[]{:S(2)}, u32[]{:S(2)}) collective-permute-start(f32[8,128,128]{2,1,0:T(8,128)S(1)} %pad_maximum_fusion.8.rest_0_), channel_id=1, source_target_pairs={{0,1},{1,0},{2,3},{3,2},{4,5},{5,4},{6,7},{7,6},{8,9},{9,8},{10,11... | collective-permute-start | bytes 1572872 | tf_op jit(solution)/shard_map/ppermute | solution.py:134
  91.7 12.0 %collective-permute-start.33 = (f32[8,128,128]{2,1,0:T(8,128)S(1)}, f32[8,128,128]{2,1,0:T(8,128)S(1)}, u32[]{:S(2)}, u32[]{:S(2)}) collective-permute-start(f32[8,128,128]{2,1,0:T(8,128)S(1)} %pad_maximum_fusion.9.rest_2_), channel_id=1, source_target_pairs={{0,1},{1,0},{2,3},{3,2},{4,5},{5,4},{6,7},{7,6},{8,9},{9,8},{10,11... | collective-permute-start | bytes 1572872 | tf_op jit(solution)/shard_map/ppermute | solution.py:134
  92.2 13.8 %collective-permute-start.31 = (f32[8,128,128]{2,1,0:T(8,128)S(1)}, f32[8,128,128]{2,1,0:T(8,128)S(1)}, u32[]{:S(2)}, u32[]{:S(2)}) collective-permute-start(f32[8,128,128]{2,1,0:T(8,128)S(1)} %pad_maximum_fusion.9.rest_2_), channel_id=1, source_target_pairs={{0,4},{4,0},{8,12},{12,8},{16,20},{20,16},{24,28},{28,24},{1,5},{5... | collective-permute-start | bytes 1572872 | tf_op jit(solution)/shard_map/ppermute | solution.py:132
  133.7 8.0 %collective-permute-start.37 = (f32[16,256,128]{2,1,0:T(8,128)S(1)}, f32[16,256,128]{2,1,0:T(8,128)S(1)}, u32[]{:S(2)}, u32[]{:S(2)}) collective-permute-start(f32[16,256,128]{2,1,0:T(8,128)S(1)} %shard_map.285), channel_id=1, source_target_pairs={{0,1},{1,0},{2,3},{3,2},{4,5},{5,4},{6,7},{7,6},{8,9},{9,8},{10,11... | collective-permute-start | bytes 6291464 | tf_op jit(solution)/shard_map/ppermute | solution.py:134
  133.9 7.8 %collective-permute-start.36 = (f32[16,256,128]{2,1,0:T(8,128)S(1)}, f32[16,256,128]{2,1,0:T(8,128)S(1)}, u32[]{:S(2)}, u32[]{:S(2)}) collective-permute-start(f32[16,256,128]{2,1,0:T(8,128)S(1)} %shard_map.284), channel_id=1, source_target_pairs={{0,1},{1,0},{2,3},{3,2},{4,5},{5,4},{6,7},{7,6},{8,9},{9,8},{10,11... | collective-permute-start | bytes 6291464 | tf_op jit(solution)/shard_map/ppermute | solution.py:134
  134.3 7.4 %collective-permute-start.38 = (f32[16,64,128]{2,1,0:T(8,128)S(1)}, f32[16,64,128]{2,1,0:T(8,128)S(1)}, u32[]{:S(2)}, u32[]{:S(2)}) collective-permute-start(f32[16,64,128]{2,1,0:T(8,128)S(1)} %get-tuple-element.182), channel_id=1, source_target_pairs={{0,1},{1,0},{2,3},{3,2},{4,5},{5,4},{6,7},{7,6},{8,9},{9,8},{10,11... | collective-permute-start | bytes 1572872 | tf_op jit(solution)/shard_map/ppermute | solution.py:134
  141.8 34.4 %collective-permute-start.39 = (f32[8,256,128]{2,1,0:T(8,128)S(1)}, f32[8,256,128]{2,1,0:T(8,128)S(1)}, u32[]{:S(2)}, u32[]{:S(2)}) collective-permute-start(f32[8,256,128]{2,1,0:T(8,128)S(1)} %slice_add_fusion), channel_id=1, source_target_pairs={{0,8},{4,12},{8,0},{12,4},{16,24},{20,28},{24,16},{28,20},{1,9},{5... | collective-permute-start | bytes 3145736 | tf_op jit(solution)/shard_map/ppermute | solution.py:132
  144.7 29.3 %collective-permute-start.40 = (f32[4,320,128]{2,1,0:T(8,128)S(1)}, f32[4,320,128]{2,1,0:T(8,128)S(1)}, u32[]{:S(2)}, u32[]{:S(2)}) collective-permute-start(f32[4,320,128]{2,1,0:T(8,128)S(1)} %pad_maximum_fusion.5), channel_id=1, source_target_pairs={{0,4},{4,0},{8,12},{12,8},{16,20},{20,16},{24,28},{28,24},{1,5},{5... | collective-permute-start | bytes 1966088 | tf_op jit(solution)/shard_map/ppermute | solution.py:132
  145.8 30.5 %collective-permute-start.41 = (f32[4,320,128]{2,1,0:T(8,128)S(1)}, f32[4,320,128]{2,1,0:T(8,128)S(1)}, u32[]{:S(2)}, u32[]{:S(2)}) collective-permute-start(f32[4,320,128]{2,1,0:T(8,128)S(1)} %pad_maximum_fusion.6), channel_id=1, source_target_pairs={{0,2},{1,3},{2,0},{3,1},{4,6},{5,7},{6,4},{7,5},{8,10},{9,11},{10,... | collective-permute-start | bytes 1966088 | tf_op jit(solution)/shard_map/ppermute | solution.py:134
  146.8 29.4 %collective-permute-start.42 = (f32[4,320,128]{2,1,0:T(8,128)S(1)}, f32[4,320,128]{2,1,0:T(8,128)S(1)}, u32[]{:S(2)}, u32[]{:S(2)}) collective-permute-start(f32[4,320,128]{2,1,0:T(8,128)S(1)} %pad_maximum_fusion.7), channel_id=1, source_target_pairs={{0,6},{1,7},{2,4},{3,5},{4,2},{5,3},{6,0},{7,1},{8,14},{9,15},{10,... | collective-permute-start | bytes 1966088 | tf_op jit(solution)/shard_map/ppermute | solution.py:137
  176.3 5.6 %collective-permute-start.43 = (f32[2,2,16,512]{3,2,1,0:T(8,128)S(1)}, f32[2,2,16,512]{3,2,1,0:T(8,128)S(1)}, u32[]{:S(2)}, u32[]{:S(2)}) collective-permute-start(f32[2,2,16,512]{3,2,1,0:T(8,128)S(1)} %get-tuple-element.210), channel_id=1, source_target_pairs={{0,1},{1,0},{2,3},{3,2},{4,5},{5,4},{6,7},{7,6},{8,9},{9,8},{10,11... | collective-permute-start | bytes 393224 | tf_op jit(solution)/shard_map/ppermute | solution.py:1001
  186.8 5.9 %collective-permute-start.46 = (f32[16,192,128]{2,1,0:T(8,128)}, f32[16,192,128]{2,1,0:T(8,128)}, u32[]{:S(2)}, u32[]{:S(2)}) collective-permute-start(f32[16,192,128]{2,1,0:T(8,128)} %get-tuple-element.219), channel_id=1, source_target_pairs={{0,1},{1,0},{2,3},{3,2},{4,5},{5,4},{6,7},{7,6},{8,9},{9,8},{10,11... | collective-permute-start | bytes 4718600 | tf_op jit(solution)/shard_map/ppermute | solution.py:134
  188.0 15.1 %collective-permute-start.51 = (f32[4,256,128]{2,1,0:T(8,128)}, f32[4,256,128]{2,1,0:T(8,128)}, u32[]{:S(2)}, u32[]{:S(2)}) collective-permute-start(f32[4,256,128]{2,1,0:T(8,128)} %fusion), channel_id=1, source_target_pairs={{0,4},{4,0},{8,12},{12,8},{16,20},{20,16},{24,28},{28,24},{1,5},{5... | collective-permute-start | bytes 1572872 | tf_op jit(solution)/shard_map/ppermute | solution.py:132
  195.1 24.1 %collective-permute-start.49 = (f32[4,208,128]{2,1,0:T(8,128)S(1)}, f32[4,208,128]{2,1,0:T(8,128)S(1)}, u32[]{:S(2)}, u32[]{:S(2)}) collective-permute-start(f32[4,208,128]{2,1,0:T(8,128)S(1)} %get-tuple-element.259), channel_id=1, source_target_pairs={{0,6},{1,7},{2,4},{3,5},{4,2},{5,3},{6,0},{7,1},{8,14},{9,15},{10,... | collective-permute-start | bytes 1277960 | tf_op jit(solution)/shard_map/ppermute | solution.py:137
  196.8 22.5 %collective-permute-start.48 = (f32[4,208,128]{2,1,0:T(8,128)S(1)}, f32[4,208,128]{2,1,0:T(8,128)S(1)}, u32[]{:S(2)}, u32[]{:S(2)}) collective-permute-start(f32[4,208,128]{2,1,0:T(8,128)S(1)} %get-tuple-element.260), channel_id=1, source_target_pairs={{0,2},{1,3},{2,0},{3,1},{4,6},{5,7},{6,4},{7,5},{8,10},{9,11},{10,... | collective-permute-start | bytes 1277960 | tf_op jit(solution)/shard_map/ppermute | solution.py:134
  197.7 22.9 %collective-permute-start.47 = (f32[4,208,128]{2,1,0:T(8,128)S(1)}, f32[4,208,128]{2,1,0:T(8,128)S(1)}, u32[]{:S(2)}, u32[]{:S(2)}) collective-permute-start(f32[4,208,128]{2,1,0:T(8,128)S(1)} %get-tuple-element.261), channel_id=1, source_target_pairs={{0,4},{4,0},{8,12},{12,8},{16,20},{20,16},{24,28},{28,24},{1,5},{5... | collective-permute-start | bytes 1277960 | tf_op jit(solution)/shard_map/ppermute | solution.py:132
  203.2 16.1 %collective-permute-start.50 = (f32[2,320,128]{2,1,0:T(8,128)S(1)}, f32[2,320,128]{2,1,0:T(8,128)S(1)}, u32[]{:S(2)}, u32[]{:S(2)}) collective-permute-start(f32[2,320,128]{2,1,0:T(8,128)S(1)} %fusion.4), channel_id=1, source_target_pairs={{0,8},{4,12},{8,0},{12,4},{16,24},{20,28},{24,16},{28,20},{1,9},{5... | collective-permute-start | bytes 983048 | tf_op jit(solution)/shard_map/ppermute | solution.py:132
  205.9 13.4 %collective-permute-start.52 = (f32[2,256,128]{2,1,0:T(8,128)S(1)}, f32[2,256,128]{2,1,0:T(8,128)S(1)}, u32[]{:S(2)}, u32[]{:S(2)}) collective-permute-start(f32[2,256,128]{2,1,0:T(8,128)S(1)} %fusion.6), channel_id=1, source_target_pairs={{0,16},{4,20},{8,24},{12,28},{16,0},{20,4},{24,8},{28,12},{1,17},{... | collective-permute-start | bytes 786440 | tf_op jit(solution)/shard_map/ppermute | solution.py:132
  220.7 20.5 %collective-permute-start.54 = (f32[1,208,128]{2,1,0:T(8,128)S(1)}, f32[1,208,128]{2,1,0:T(8,128)S(1)}, u32[]{:S(2)}, u32[]{:S(2)}) collective-permute-start(f32[1,208,128]{2,1,0:T(8,128)S(1)} %get-tuple-element.248), channel_id=1, source_target_pairs={{0,16},{4,20},{8,24},{12,28},{16,0},{20,4},{24,8},{28,12},{1,17},{... | collective-permute-start | bytes 319496 | tf_op jit(solution)/shard_map/ppermute | solution.py:132
  222.9 18.3 %collective-permute-start.53 = (f32[1,208,128]{2,1,0:T(8,128)S(1)}, f32[1,208,128]{2,1,0:T(8,128)S(1)}, u32[]{:S(2)}, u32[]{:S(2)}) collective-permute-start(f32[1,208,128]{2,1,0:T(8,128)S(1)} %get-tuple-element.249), channel_id=1, source_target_pairs={{0,8},{4,12},{8,0},{12,4},{16,24},{20,28},{24,16},{28,20},{1,9},{5... | collective-permute-start | bytes 319496 | tf_op jit(solution)/shard_map/ppermute | solution.py:132
  224.0 17.2 %collective-permute-start.55 = (f32[1,208,128]{2,1,0:T(8,128)S(1)}, f32[1,208,128]{2,1,0:T(8,128)S(1)}, u32[]{:S(2)}, u32[]{:S(2)}) collective-permute-start(f32[1,208,128]{2,1,0:T(8,128)S(1)} %get-tuple-element.250), channel_id=1, source_target_pairs={{0,24},{4,28},{8,16},{12,20},{16,8},{20,12},{24,0},{28,4},{1,25},{... | collective-permute-start | bytes 319496 | tf_op jit(solution)/shard_map/ppermute | solution.py:132
  227.3 12.6 %collective-permute-start.57 = (f32[1,320,128]{2,1,0:T(8,128)S(1)}, f32[1,320,128]{2,1,0:T(8,128)S(1)}, u32[]{:S(2)}, u32[]{:S(2)}) collective-permute-start(f32[1,320,128]{2,1,0:T(8,128)S(1)} %fusion.16), channel_id=1, source_target_pairs={{0,16},{4,20},{8,24},{12,28},{16,0},{20,4},{24,8},{28,12},{1,17},{... | collective-permute-start | bytes 491528 | tf_op jit(solution)/shard_map/ppermute | solution.py:132
  (69 other events, 834.6 us)

commit v4 on v3

--- a/solution.py
+++ b/solution.py
@@ -278,6 +278,12 @@
             self.last.append(got)
             self.terms.append([got])
         return out
+
+    def absorb(self, other, *earlier):
+        n = self.slots
+        other.terms[-1] = after(other.terms[-1], *earlier)
+        parts = [sum(term[0][0:n] for term in x.terms) for x in (self, other)]
+        self.terms = [[jnp.concatenate(parts, axis=1)]]
 
     def total(self):
         return sum(term[0][0] for term in self.terms)
@@ -1104,19 +1110,17 @@
     qkv = Stream(plan, rows_qkv, double)
     down_sum, up_sum, qkv_sum = Reduce(plan, outer), Reduce(plan, single), Reduce(plan, double)
 
-    gm, gln = middle_grad_stage(cot, xhat2, inv2, ln, ph, plo, uh, ul)
-    gmix, away_out, keep_out = mixture_grad_stage(me, gm, attended, oh, ol, plan, out)
-    away = grad_down_stage(me, after(cth, away_out), ctl, hh, hl, plan, down, 1)
+    away = grad_down_stage(me, cth, ctl, hh, hl, plan, down, 1)
     cores = down_sum.begin(away)
     away = grad_up_stage(me, after(nth, away), ntl, ph, plo, plan, up, 1)
     cores += up_sum.begin(away)
-    cores += up_sum.begin(away_out)
     keep = grad_down_stage(me, after(cth, away), ctl, hh, hl, plan, down, 0)
     down_sum.keep(keep)
     keep = grad_up_stage(me, after(nth, keep), ntl, ph, plo, plan, up, 0)
     up_sum.keep(keep)
-    up_sum.keep(keep_out)
     sent = (down_sum.send(keep, cores), up_sum.send(keep, cores))
+    gm, gln = middle_grad_stage(after(cot, sent), xhat2, inv2, ln, ph, plo, uh, ul)
+    gmix, away_out, keep_out = mixture_grad_stage(me, gm, attended, oh, ol, plan, out)
     before = ()
     calls = [(s, 1, 0, width // 128) for s in range(seqs)]
     for which in calls:
@@ -1124,16 +1128,19 @@
         before = attention_backward(
             packed, far, bias, *attend, attended, lse, grad, seqs, local_rows, which, before
         )
-    output = output_stage(after(middle, before), hh, hl, dh, dl)
-    gate = (output, down_sum.last, up_sum.last)
+    gate = (before, down_sum.last, up_sum.last)
     dq, dk, dv, f4, f5a, f5b = before
     f4, f5a, f5b = after((f4, f5a, f5b), gate)
     g4, g5a, g5b = swap(f4, 1), swap(f5a, 2), swap(f5b, 3)
     down_sum.send(gate)
+    out_sum = Reduce(plan, single)
+    out_cores = out_sum.begin(away_out, gate)
+    out_sum.keep(keep_out)
     gph, gpl, column = packed_grad_stage(dq, dk, dv, g4, g5a, g5b, far_pool, seqs)
     away, sums_away = grad_qkv_stage(
         me, gph, gpl, column, xhat1, ln, wqh, wql, plan, qkv, 1
     )
+    out_sum.send(gph, out_cores)
     got = qkv_sum.begin(away)
     keep, sums_keep = grad_qkv_stage(
         me, gph, gpl, column, after(xhat1, away), ln, wqh, wql, plan, qkv, 0
@@ -1142,9 +1149,11 @@
     sums = jnp.concatenate([(sums_away + sums_keep)[0:2], gln[0:2]], axis=0)
     sent = qkv_sum.send(got, rider=sums.reshape(-1, 128))
     down_sum.send(sent)
-    up_sum.send(sent)
+    up_sum.absorb(out_sum, sent)
+    up_sum.send()
     gtok = input_grad_stage(gph, gpl, wqh, wql, after(xhat1, sent), inv1, ln, gm)
-    gate = (up_sum.last, down_sum.last, gtok)
+    output = output_stage(after(middle, gtok), hh, hl, dh, dl)
+    gate = (up_sum.last, down_sum.last, output)
     sent = qkv_sum.send(qkv_sum.last, gate)
     while qkv_sum.stages:
         sent = qkv_sum.send(qkv_sum.last)

time: 244 us -> 241 us (0.988)
  waiting for transfers between devices: 64.3 us -> 52.4 us
  other arithmetic: 15.2 us -> 20 us
    ppermute x26 -> x27, waiting for transfers between devices: 28.1 us -> 18.2 us  [send(): return lax.ppermute(x, 'fsdp', [(i, i ^ f) for i in range(self.fsdp)])]
    ppermute x23 -> x24, waiting for transfers between devices: 30.6 us -> 21.7 us  [send(): return lax.ppermute(x, 'dp', [(i, i ^ d) for i in range(self.dp)])]
    ppermute x2 -> x3, waiting for transfers between devices: 0.01 us -> 7.81 us  [send(): return lax.ppermute(x, ('dp', 'fsdp'), pairs)]
    ppermute x23 -> x24, starting transfers between devices: 31.9 us -> 33.7 us  [send(): return lax.ppermute(x, 'dp', [(i, i ^ d) for i in range(self.dp)])]
    unnamed x131 -> x105, local copies, waits for them, and re-layouts: 6.16 us -> 7.38 us
    add x10 -> x9, other arithmetic: 7.31 us -> 7.87 us  [send(): sum((term[i][v * n:(v + 1) * n] for term in self.terms))]
    ppermute x26 -> x27, starting transfers between devices: 13.5 us -> 13.2 us  [send(): return lax.ppermute(x, 'fsdp', [(i, i ^ f) for i in range(self.fsdp)])]
  transfers between devices with their start and end apart: 59 -> 62, of which waited for: 26 -> 21; matrix products, arithmetic and copies ran while one was open for 11% -> 14% of each run, Pallas kernels for 24% -> 29%
where the time goes in v4:
time: 241 us
  Pallas kernels  89.6 us (37%)
  starting transfers between devices  56.4 us (23%)
  waiting for transfers between devices  52.4 us (22%)
  local copies, waits for them, and re-layouts  20.4 us (8%)
  other arithmetic  20 us (8%)
    ppermute x24, starting transfers between devices, send(): return lax.ppermute(x, 'dp', [(i, i ^ d) for i in range(self.dp)])  33.7 us
    ppermute x24, waiting for transfers between devices, send(): return lax.ppermute(x, 'dp', [(i, i ^ d) for i in range(self.dp)])  21.7 us
    pallas_call x2, Pallas kernels, attention_backward(): pl.pallas_call(body, compiler_params=ROOM, cost_estimate=cost(8), grid=(c...  19.9 us
    ppermute x27, waiting for transfers between devices, send(): return lax.ppermute(x, 'fsdp', [(i, i ^ f) for i in range(self.fsdp)])  18.2 us
    ppermute x27, starting transfers between devices, send(): return lax.ppermute(x, 'fsdp', [(i, i ^ f) for i in range(self.fsdp)])  13.2 us
    pallas_call x1, Pallas kernels, hidden_stage(): pl.pallas_call(body, compiler_params=ROOM, cost_estimate=cost(15), grid=(...  11.6 us
    pallas_call x2, Pallas kernels, attention_forward(): pl.pallas_call(body, compiler_params=ROOM, cost_estimate=cost(9.5), grid=...  11.2 us
    add x9, other arithmetic, send(): sum((term[i][v * n:(v + 1) * n] for term in self.terms))  7.87 us
  transfers between devices with their start and end apart: 62, of which 21 were waited for; matrix products, arithmetic and copies ran while one was open for 14% of the time, Pallas kernels for 29%

profile of v4, /device:TPU:0, one launch (start us, length us, event | category | flops | bytes accessed | tf_op | source)
XLA Modules:
  0.0 240.5 jit_solution(12081202453766652257)
XLA Ops:
  2.7 3.0 %collective-permute-start = (f32[1,208,128]{2,1,0:T(8,128)S(1)}, f32[1,208,128]{2,1,0:T(8,128)S(1)}, u32[]{:S(2)}, u32[]{:S(2)}) collective-permute-start(f32[1,208,128]{2,1,0:T(8,128)S(1)} %bitcast.95), channel_id=1, source_target_pairs={{0,8},{4,12},{8,0},{12,4},{16,24},{20,28},{24,16},{28,20},{1,9},{5... | collective-permute-start | bytes 319496 | tf_op jit(solution)/shard_map/ppermute | solution.py:132
  5.7 2.6 %collective-permute-start.1 = (f32[1,208,128]{2,1,0:T(8,128)S(1)}, f32[1,208,128]{2,1,0:T(8,128)S(1)}, u32[]{:S(2)}, u32[]{:S(2)}) collective-permute-start(f32[1,208,128]{2,1,0:T(8,128)S(1)} %bitcast.96), channel_id=1, source_target_pairs={{0,16},{4,20},{8,24},{12,28},{16,0},{20,4},{24,8},{28,12},{1,17},{... | collective-permute-start | bytes 319496 | tf_op jit(solution)/shard_map/ppermute | solution.py:132
  19.4 2.0 collective-permute-start.7
  21.4 1.5 collective-permute-start.9
  23.0 1.7 collective-permute-start.3
  25.9 5.3 %collective-permute-done.4 = f32[4,96,128]{2,1,0:T(8,128)S(1)} collective-permute-done((f32[4,96,128]{2,1,0:T(8,128)S(1)}, f32[4,96,128]{2,1,0:T(8,128)S(1)}, u32[]{:S(2)}, u32[]{:S(2)}) %collective-permute-start.4) | collective-permute-done | bytes 196640 | tf_op jit(solution)/shard_map/ppermute | solution.py:134
  32.7 1.7 pad_maximum_fusion.10
  34.4 2.5 %collective-permute-start.10 = (f32[2,320,128]{2,1,0:T(8,128)}, f32[2,320,128]{2,1,0:T(8,128)}, u32[]{:S(2)}, u32[]{:S(2)}) collective-permute-start(f32[2,320,128]{2,1,0:T(8,128)} %pad_maximum_fusion.10), channel_id=1, source_target_pairs={{0,8},{4,12},{8,0},{12,4},{16,24},{20,28},{24,16},{28,20},{1,9},{5... | collective-permute-start | bytes 983048 | tf_op jit(solution)/shard_map/ppermute | solution.py:132
  38.2 1.6 concatenate.77.outer_bias
  39.8 5.8 %collective-permute-done.11 = f32[1,256,128]{2,1,0:T(8,128)} collective-permute-done((f32[1,256,128]{2,1,0:T(8,128)}, f32[1,256,128]{2,1,0:T(8,128)}, u32[]{:S(2)}, u32[]{:S(2)}) %collective-permute-start.11) | collective-permute-done | bytes 131104 | tf_op jit(solution)/shard_map/ppermute | solution.py:132
  50.0 1.5 collective-permute-start.17
  53.4 1.2 collective-permute-start.18
  54.6 6.0 %shard_map.276 = (f32[512,1536]{1,0:T(8,128)S(1)}, bf16[1536,512]{1,0:T(8,128)(2,1)S(1)}, bf16[1536,512]{1,0:T(8,128)(2,1)S(1)}, f32[512,512]{1,0:T(8,128)S(1)},...) custom-call(s32[2]{0:T(128)S(1)} %pad_add_fusion.3.me_ref, ...), custom_call_target="tpu_custom_call" | custom-call | flops 333000000 | bytes 925000 | tf_op jit(solution)/shard_map/pallas_call | solution.py:371
  62.0 1.5 collective-permute-start.19
  67.0 5.6 %shard_map.277 = (f32[512,512]{1,0:T(8,128)S(1)}, f32[512,512]{1,0:T(8,128)S(1)}) custom-call(f32[512,1536]{1,0:T(8,128)S(1)} %get-tuple-element.152.q.k.v, f32[512,1536]{1,0:T(8,128)S(1)} %get-tuple-element.152.q.k.v, f32[512,1536]{1,0:T(8,128)S(1)} %get-tuple-element.152.q.k.v, f32[2,2,32,512]{3,2,1,0:T(8,128)S(1)} %constant_dynamic-update-slice_fusion.2.fk.fv, ...), custom_call_target="tpu_custom_call" | custom-call | flops 427500000 | bytes 1187500 | tf_op jit(solution)/shard_map/pallas_call | solution.py:498
  72.6 7.7 %collective-permute-done.23.rest_6_ = f32[8,160,128]{2,1,0:T(8,128)S(1)} collective-permute-done((f32[8,160,128]{2,1,0:T(8,128)S(1)}, f32[8,160,128]{2,1,0:T(8,128)S(1)}, u32[]{:S(2)}, u32[]{:S(2)}) %collective-permute-start.23) | collective-permute-done | bytes 655392 | tf_op jit(solution)/shard_map/ppermute | solution.py:132
  83.3 5.6 %shard_map.278 = (f32[512,512]{1,0:T(8,128)S(1)}, f32[512,512]{1,0:T(8,128)S(1)}) custom-call(f32[512,1536]{1,0:T(8,128)S(1)} %get-tuple-element.152.q.k.v, f32[512,1536]{1,0:T(8,128)S(1)} %get-tuple-element.152.q.k.v, f32[512,1536]{1,0:T(8,128)S(1)} %get-tuple-element.152.q.k.v, ...), custom_call_target="tpu_custom_call", output_to_operand_aliasing={{0}: (10, {}), {1}: (11, {})} | custom-call | flops 427500000 | bytes 1187500 | tf_op jit(solution)/shard_map/pallas_call | solution.py:498
  93.0 2.5 %shard_map.279 = (bf16[512,2048]{1,0:T(8,128)(2,1)S(1)}, bf16[512,2048]{1,0:T(8,128)(2,1)S(1)}, bf16[512,512]{1,0:T(8,128)(2,1)S(1)}, bf16[512,512]{1,0:T(8,128)(2,1)S(1)}) custom-call(s32[2]{0:T(128)S(1)} %pad_add_fusion.3.me_ref, f32[8,160,128]{2,1,0:T(8,128)S(1)} %pad_maximum_fusion.3.rest_0_, f32[8,160,128]{2,1,0:T(8,128)S(1)} %collective-permute-done.24.rest_1_, ...), custom_call_target="tpu_custom_call" | custom-call | flops 225000000 | bytes 625000 | tf_op jit(solution)/shard_map/pallas_call | solution.py:636
  97.8 5.8 %collective-permute-done.30.rest_4_ = f32[8,128,128]{2,1,0:T(8,128)S(1)} collective-permute-done((f32[8,128,128]{2,1,0:T(8,128)S(1)}, f32[8,128,128]{2,1,0:T(8,128)S(1)}, u32[]{:S(2)}, u32[]{:S(2)}) %collective-permute-start.30) | collective-permute-done | bytes 524320 | tf_op jit(solution)/shard_map/ppermute | solution.py:134
  104.4 1.4 collective-permute-done.34.rest_5_
  106.6 11.6 %shard_map.281 = (bf16[512,2048]{1,0:T(8,128)(2,1)S(1)}, bf16[512,2048]{1,0:T(8,128)(2,1)S(1)}, bf16[512,2048]{1,0:T(8,128)(2,1)S(1)}, bf16[512,2048]{1,0:T(8,12...) custom-call(s32[2]{0:T(128)S(1)} %pad_add_fusion.3.me_ref, ...), custom_call_target="tpu_custom_call" | custom-call | flops 675000000 | bytes 1875000 | tf_op jit(solution)/shard_map/pallas_call | solution.py:697
  118.2 2.7 %shard_map.282 = f32[16,256,128]{2,1,0:T(8,128)S(1)} custom-call(s32[2]{0:T(128)S(1)} %pad_add_fusion.3.me_ref, bf16[512,512]{1,0:T(8,128)(2,1)S(1)} %get-tuple-element.183.c0, bf16[512,512]{1,0:T(8,128)(2,1)S(1)} %get-tuple-element.176.c1, bf16[512,2048]{1,0:T(8,128)(2,1)S(1)} %get-tuple-element.177.h0, bf16[512,2048]{1,0:T(8,128)(2,1)S(1)} %get-tuple-element.178.h1), custom_call_target="tpu_custom_call" | custom-call | flops 12150000 | bytes 33750 | tf_op jit(solution)/shard_map/pallas_call | solution.py:736
  121.2 3.2 %shard_map.283 = f32[16,256,128]{2,1,0:T(8,128)S(1)} custom-call(s32[2]{0:T(128)S(1)} %pad_add_fusion.3.me_ref, bf16[512,512]{1,0:T(8,128)(2,1)S(1)} %get-tuple-element.184.n0, bf16[512,512]{1,0:T(8,128)(2,1)S(1)} %get-tuple-element.180.n1, bf16[512,2048]{1,0:T(8,128)(2,1)S(1)} %get-tuple-element.181.p0, bf16[512,2048]{1,0:T(8,128)(2,1)S(1)} %get-tuple-element.182.p1), custom_call_target="tpu_custom_call" | custom-call | flops 14400000 | bytes 40000 | tf_op jit(solution)/shard_map/pallas_call | solution.py:789
  124.8 2.7 %shard_map.284 = f32[16,256,128]{2,1,0:T(8,128)S(1)} custom-call(s32[2]{0:T(128)S(1)} %pad_add_fusion.3.me_ref, bf16[512,512]{1,0:T(8,128)(2,1)S(1)} %get-tuple-element.183.c0, bf16[512,512]{1,0:T(8,128)(2,1)S(1)} %get-tuple-element.176.c1, bf16[512,2048]{1,0:T(8,128)(2,1)S(1)} %get-tuple-element.177.h0, bf16[512,2048]{1,0:T(8,128)(2,1)S(1)} %get-tuple-element.178.h1), custom_call_target="tpu_custom_call" | custom-call | flops 12150000 | bytes 33750 | tf_op jit(solution)/shard_map/pallas_call | solution.py:736
  127.5 3.2 %shard_map.285 = f32[16,256,128]{2,1,0:T(8,128)S(1)} custom-call(s32[2]{0:T(128)S(1)} %pad_add_fusion.3.me_ref, bf16[512,512]{1,0:T(8,128)(2,1)S(1)} %get-tuple-element.184.n0, bf16[512,512]{1,0:T(8,128)(2,1)S(1)} %get-tuple-element.180.n1, bf16[512,2048]{1,0:T(8,128)(2,1)S(1)} %get-tuple-element.181.p0, bf16[512,2048]{1,0:T(8,128)(2,1)S(1)} %get-tuple-element.182.p1), custom_call_target="tpu_custom_call" | custom-call | flops 14400000 | bytes 40000 | tf_op jit(solution)/shard_map/pallas_call | solution.py:789
  133.8 1.5 collective-permute-start.40
  136.2 5.0 %shard_map.286 = (f32[512,512]{1,0:T(8,128)S(1)}, f32[8,512]{1,0:T(8,128)S(1)}) custom-call(f32[512,512]{1,0:T(8,128)S(1)} %bitcast.92, f32[512,512]{1,0:T(8,128)S(1)} %copy-done.25, f32[512,128]{1,0:T(8,128)S(1)} %get-tuple-element.188.inv_ref, f32[8,512]{1,0:T(8,128)S(1)} %get-tuple-element.171.ln_ref.ln_r, bf16[512,2048]{1,0:T(8,128)(2,1)S(1)} %get-tuple-element.181.p0, ...), custom_call_target="tpu_custom_call" | custom-call | flops 382500000 | bytes 1062500 | tf_op jit(solution)/shard_map/pallas_call | solution.py:857
  141.3 3.2 %shard_map.287 = (f32[512,512]{1,0:T(8,128)S(1)}, f32[16,64,128]{2,1,0:T(8,128)}, f32[16,64,128]{2,1,0:T(8,128)S(1)}) custom-call(s32[2]{0:T(128)S(1)} %pad_add_fusion.3.me_ref, f32[512,512]{1,0:T(8,128)S(1)} %get-tuple-element.191.gm_ref.gm_r, f32[512,512]{1,0:T(8,128)S(1)} %get-tuple-element.153.att.rest_0_, ...), custom_call_target="tpu_custom_call" | custom-call | flops 225000000 | bytes 625000 | tf_op jit(solution)/shard_map/pallas_call | solution.py:889
  145.5 9.8 %shard_map.288 = (f32[512,512]{1,0:T(8,128)S(1)}, f32[512,512]{1,0:T(8,128)S(1)}, f32[512,512]{1,0:T(8,128)S(1)}, f32[2,2,16,512]{3,2,1,0:T(8,128)S(1)}, f32[2,2...) custom-call(f32[512,1536]{1,0:T(8,128)S(1)} %get-tuple-element.152.q.k.v, f32[512,1536]{1,0:T(8,128)S(1)} %get-tuple-element.152.q.k.v, ...), custom_call_target="tpu_custom_call" | custom-call | flops 360000000 | bytes 1000000 | tf_op jit(solution)/shard_map/pallas_call | solution.py:570
  155.3 10.1 %shard_map.289 = (f32[512,512]{1,0:T(8,128)S(1)}, f32[512,512]{1,0:T(8,128)S(1)}, f32[512,512]{1,0:T(8,128)S(1)}, f32[2,2,16,512]{3,2,1,0:T(8,128)S(1)}, f32[2,2...) custom-call(f32[512,1536]{1,0:T(8,128)S(1)} %get-tuple-element.152.q, ...), custom_call_target="tpu_custom_call", output_to_operand_aliasing={{0}: (13, {}), {1}: (14, {}), {2}: (15, {}), {3}: (16, {}),... | custom-call | flops 360000000 | bytes 1000000 | tf_op jit(solution)/shard_map/pallas_call | solution.py:570
  165.5 1.5 collective-permute-start.43
  167.4 2.6 %collective-permute-done.43.g5a_r = f32[2,2,8,512]{3,2,1,0:T(8,128)S(1)} collective-permute-done((f32[2,2,8,512]{3,2,1,0:T(8,128)S(1)}, f32[2,2,8,512]{3,2,1,0:T(8,128)S(1)}, u32[]{:S(2)}, u32[]{:S(2)}) %collective-permute-start.43) | collective-permute-done | bytes 65568 | tf_op jit(solution)/shard_map/ppermute | solution.py:1007
  172.3 3.7 %shard_map.291 = (f32[16,192,128]{2,1,0:T(8,128)}, f32[8,512]{1,0:T(8,128)S(1)}) custom-call(s32[2]{0:T(128)S(1)} %pad_add_fusion.3.me_ref, bf16[512,1536]{1,0:T(8,128)(2,1)S(1)} %get-tuple-element.210.gph_r, bf16[512,1536]{1,0:T(8,128)(2,1)S(1)} %get-tuple-element.211.gpl_r, f32[1536,128]{1,0:T(8,128)S(1)} %get-tuple-element.215.col_r, ...), custom_call_target="tpu_custom_call" | custom-call | flops 11250000 | bytes 31250 | tf_op jit(solution)/shard_map/pallas_call | solution.py:989
  177.9 2.0 fusion
  181.0 2.6 %shard_map.292 = (f32[16,192,128]{2,1,0:T(8,128)S(1)}, f32[8,512]{1,0:T(8,128)S(1)}) custom-call(s32[2]{0:T(128)S(1)} %pad_add_fusion.3.me_ref, bf16[512,1536]{1,0:T(8,128)(2,1)S(1)} %get-tuple-element.210.gph_r, bf16[512,1536]{1,0:T(8,128)(2,1)S(1)} %get-tuple-element.211.gpl_r, f32[1536,128]{1,0:T(8,128)S(1)} %get-tuple-element.215.col_r, ...), custom_call_target="tpu_custom_call" | custom-call | flops 11250000 | bytes 31250 | tf_op jit(solution)/shard_map/pallas_call | solution.py:989
  185.9 1.8 collective-permute-start.52
  189.5 2.2 slice_add_fusion.6
  191.8 1.4 collective-permute-start.47
  193.2 5.2 %collective-permute-done.52 = f32[4,64,128]{2,1,0:T(8,128)S(1)} collective-permute-done((f32[4,64,128]{2,1,0:T(8,128)S(1)}, f32[4,64,128]{2,1,0:T(8,128)S(1)}, u32[]{:S(2)}, u32[]{:S(2)}) %collective-permute-start.52) | collective-permute-done | bytes 131104 | tf_op jit(solution)/shard_map/ppermute | solution.py:137
  203.9 2.7 %collective-permute-start.55 = (f32[2,256,128]{2,1,0:T(8,128)S(1)}, f32[2,256,128]{2,1,0:T(8,128)S(1)}, u32[]{:S(2)}, u32[]{:S(2)}) collective-permute-start(f32[2,256,128]{2,1,0:T(8,128)S(1)} %fusion.6), channel_id=1, source_target_pairs={{0,16},{4,20},{8,24},{12,28},{16,0},{20,4},{24,8},{28,12},{1,17},{... | collective-permute-start | bytes 786440 | tf_op jit(solution)/shard_map/ppermute | solution.py:132
  206.7 3.8 %shard_map.293 = f32[512,512]{1,0:T(8,128)} custom-call(bf16[512,1536]{1,0:T(8,128)(2,1)S(1)} %copy-done.9, bf16[512,1536]{1,0:T(8,128)(2,1)S(1)} %copy-done.11, bf16[1536,512]{1,0:T(8,128)(2,1)S(1)} %copy-done.5, bf16[1536,512]{1,0:T(8,128)(2,1)S(1)} %copy-done.7, f32[512,512]{1,0:T(8,128)S(1)} %copy-done.13, f32[512,128]{1,0:T(8,128)S(1)} %copy-done.32, ...), custom_call_target="tpu_custom_call" | custom-call | flops 333000000 | bytes 925000 | tf_op jit(solution)/shard_map/pallas_call | solution.py:941
  210.5 5.8 %shard_map.294 = f32[512,512]{1,0:T(8,128)} custom-call(f32[512,512]{1,0:T(8,128)S(1)} %copy-done.30, bf16[512,2048]{1,0:T(8,128)(2,1)S(1)} %get-tuple-element.177.h0, bf16[512,2048]{1,0:T(8,128)(2,1)S(1)} %copy-done.3, bf16[512,2048]{1,0:T(8,128)(2,1)S(1)} %copy-done.15, bf16[512,2048]{1,0:T(8,128)(2,1)S(1)} %copy-done.17), custom_call_target="tpu_custom_call" | custom-call | flops 360000000 | bytes 1000000 | tf_op jit(solution)/shard_map/pallas_call | solution.py:821
  216.3 2.6 %collective-permute-done.48 = f32[4,208,128]{2,1,0:T(8,128)S(1)} collective-permute-done((f32[4,208,128]{2,1,0:T(8,128)S(1)}, f32[4,208,128]{2,1,0:T(8,128)S(1)}, u32[]{:S(2)}, u32[]{:S(2)}) %collective-permute-start.48) | collective-permute-done | bytes 426016 | tf_op jit(solution)/shard_map/ppermute | solution.py:137
  218.9 3.2 %collective-permute-start.58 = (f32[1,208,128]{2,1,0:T(8,128)S(1)}, f32[1,208,128]{2,1,0:T(8,128)S(1)}, u32[]{:S(2)}, u32[]{:S(2)}) collective-permute-start(f32[1,208,128]{2,1,0:T(8,128)S(1)} %get-tuple-element.251), channel_id=1, source_target_pairs={{0,24},{4,28},{8,16},{12,20},{16,8},{20,12},{24,0},{28,4},{1,25},{... | collective-permute-start | bytes 319496 | tf_op jit(solution)/shard_map/ppermute | solution.py:132
  222.1 1.3 collective-permute-start.56
  225.3 1.9 collective-permute-start.60
  227.2 2.3 collective-permute-done.59
  231.3 6.0 %collective-permute-done.60 = f32[1,320,128]{2,1,0:T(8,128)S(1)} collective-permute-done((f32[1,320,128]{2,1,0:T(8,128)S(1)}, f32[1,320,128]{2,1,0:T(8,128)S(1)}, u32[]{:S(2)}, u32[]{:S(2)}) %collective-permute-start.60) | collective-permute-done | bytes 163872 | tf_op jit(solution)/shard_map/ppermute | solution.py:132
  (302 shorter events, 66.8 us)
Async XLA Ops:
  2.7 16.8 %collective-permute-start = (f32[1,208,128]{2,1,0:T(8,128)S(1)}, f32[1,208,128]{2,1,0:T(8,128)S(1)}, u32[]{:S(2)}, u32[]{:S(2)}) collective-permute-start(f32[1,208,128]{2,1,0:T(8,128)S(1)} %bitcast.95), channel_id=1, source_target_pairs={{0,8},{4,12},{8,0},{12,4},{16,24},{20,28},{24,16},{28,20},{1,9},{5... | collective-permute-start | bytes 319496 | tf_op jit(solution)/shard_map/ppermute | solution.py:132
  5.7 13.7 %collective-permute-start.1 = (f32[1,208,128]{2,1,0:T(8,128)S(1)}, f32[1,208,128]{2,1,0:T(8,128)S(1)}, u32[]{:S(2)}, u32[]{:S(2)}) collective-permute-start(f32[1,208,128]{2,1,0:T(8,128)S(1)} %bitcast.96), channel_id=1, source_target_pairs={{0,16},{4,20},{8,24},{12,28},{16,0},{20,4},{24,8},{28,12},{1,17},{... | collective-permute-start | bytes 319496 | tf_op jit(solution)/shard_map/ppermute | solution.py:132
  8.3 11.2 %collective-permute-start.2 = (f32[1,208,128]{2,1,0:T(8,128)S(1)}, f32[1,208,128]{2,1,0:T(8,128)S(1)}, u32[]{:S(2)}, u32[]{:S(2)}) collective-permute-start(f32[1,208,128]{2,1,0:T(8,128)S(1)} %bitcast.97), channel_id=1, source_target_pairs={{0,24},{4,28},{8,16},{12,20},{16,8},{20,12},{24,0},{28,4},{1,25},{... | collective-permute-start | bytes 319496 | tf_op jit(solution)/shard_map/ppermute | solution.py:132
  8.3 9.9 %collective-permute-start.8 = (s32[2,256]{1,0:T(2,128)}, s32[2,256]{1,0:T(2,128)S(1)}, u32[]{:S(2)}, u32[]{:S(2)}) collective-permute-start(s32[2,256]{1,0:T(2,128)} %param.22), channel_id=1, source_target_pairs={{0,1},{1,0},{2,3},{3,2},{4,5},{5,4},{6,7},{7,6},{8,9},{9,8},{10,11... | collective-permute-start | bytes 6152 | tf_op jit(solution)/shard_map/ppermute | solution.py:1007
  19.4 13.3 %collective-permute-start.7 = (f32[1,320,128]{2,1,0:T(8,128)S(1)}, f32[1,320,128]{2,1,0:T(8,128)}, u32[]{:S(2)}, u32[]{:S(2)}) collective-permute-start(f32[1,320,128]{2,1,0:T(8,128)S(1)} %maximum_bitcast_fusion), channel_id=1, source_target_pairs={{0,16},{4,20},{8,24},{12,28},{16,0},{20,4},{24,8},{28,12},{1,17},{... | collective-permute-start | bytes 491528 | tf_op jit(solution)/shard_map/ppermute | solution.py:132
  23.0 8.2 %collective-permute-start.3 = (f32[4,112,128]{2,1,0:T(8,128)S(1)}, f32[4,112,128]{2,1,0:T(8,128)S(1)}, u32[]{:S(2)}, u32[]{:S(2)}) collective-permute-start(f32[4,112,128]{2,1,0:T(8,128)S(1)} %slice.405), channel_id=1, source_target_pairs={{0,4},{4,0},{8,12},{12,8},{16,20},{20,16},{24,28},{28,24},{1,5},{5... | collective-permute-start | bytes 688136 | tf_op jit(solution)/shard_map/ppermute | solution.py:132
  24.7 6.5 %collective-permute-start.4 = (f32[4,96,128]{2,1,0:T(8,128)S(1)}, f32[4,96,128]{2,1,0:T(8,128)S(1)}, u32[]{:S(2)}, u32[]{:S(2)}) collective-permute-start(f32[4,96,128]{2,1,0:T(8,128)S(1)} %pad_maximum_fusion.12), channel_id=1, source_target_pairs={{0,2},{1,3},{2,0},{3,1},{4,6},{5,7},{6,4},{7,5},{8,10},{9,11},{10,... | collective-permute-start | bytes 589832 | tf_op jit(solution)/shard_map/ppermute | solution.py:134
  31.3 15.1 %collective-permute-start.5 = (f32[8,112,128]{2,1,0:T(8,128)S(1)}, f32[8,112,128]{2,1,0:T(8,128)S(1)}, u32[]{:S(2)}, u32[]{:S(2)}) collective-permute-start(f32[8,112,128]{2,1,0:T(8,128)S(1)} %pad_maximum_fusion.7.rest_0_), channel_id=1, source_target_pairs={{0,2},{1,3},{2,0},{3,1},{4,6},{5,7},{6,4},{7,5},{8,10},{9,11},{10,... | collective-permute-start | bytes 1376264 | tf_op jit(solution)/shard_map/ppermute | solution.py:134
  31.9 14.5 %collective-permute-start.6 = (f32[8,96,128]{2,1,0:T(8,128)S(1)}, f32[8,96,128]{2,1,0:T(8,128)}, u32[]{:S(2)}, u32[]{:S(2)}) collective-permute-start(f32[8,96,128]{2,1,0:T(8,128)S(1)} %pad_maximum_fusion.9.rest_2_), channel_id=1, source_target_pairs={{0,4},{4,0},{8,12},{12,8},{16,20},{20,16},{24,28},{28,24},{1,5},{5... | collective-permute-start | bytes 1179656 | tf_op jit(solution)/shard_map/ppermute | solution.py:132
  34.4 12.0 %collective-permute-start.10 = (f32[2,320,128]{2,1,0:T(8,128)}, f32[2,320,128]{2,1,0:T(8,128)}, u32[]{:S(2)}, u32[]{:S(2)}) collective-permute-start(f32[2,320,128]{2,1,0:T(8,128)} %pad_maximum_fusion.10), channel_id=1, source_target_pairs={{0,8},{4,12},{8,0},{12,4},{16,24},{20,28},{24,16},{28,20},{1,9},{5... | collective-permute-start | bytes 983048 | tf_op jit(solution)/shard_map/ppermute | solution.py:132
  36.9 8.7 %collective-permute-start.11 = (f32[1,256,128]{2,1,0:T(8,128)}, f32[1,256,128]{2,1,0:T(8,128)}, u32[]{:S(2)}, u32[]{:S(2)}) collective-permute-start(f32[1,256,128]{2,1,0:T(8,128)} %bitcast.20), channel_id=1, source_target_pairs={{0,16},{4,20},{8,24},{12,28},{16,0},{20,4},{24,8},{28,12},{1,17},{... | collective-permute-start | bytes 393224 | tf_op jit(solution)/shard_map/ppermute | solution.py:132
  50.0 11.3 %collective-permute-start.17 = (f32[4,160,128]{2,1,0:T(8,128)S(1)}, f32[4,160,128]{2,1,0:T(8,128)S(1)}, u32[]{:S(2)}, u32[]{:S(2)}) collective-permute-start(f32[4,160,128]{2,1,0:T(8,128)S(1)} %get-tuple-element.141), channel_id=1, source_target_pairs={{0,2},{1,3},{2,0},{3,1},{4,6},{5,7},{6,4},{7,5},{8,10},{9,11},{10,... | collective-permute-start | bytes 983048 | tf_op jit(solution)/shard_map/ppermute | solution.py:134
  51.5 9.8 %collective-permute-start.16 = (f32[4,160,128]{2,1,0:T(8,128)S(1)}, f32[4,160,128]{2,1,0:T(8,128)S(1)}, u32[]{:S(2)}, u32[]{:S(2)}) collective-permute-start(f32[4,160,128]{2,1,0:T(8,128)S(1)} %get-tuple-element.140), channel_id=1, source_target_pairs={{0,4},{4,0},{8,12},{12,8},{16,20},{20,16},{24,28},{28,24},{1,5},{5... | collective-permute-start | bytes 983048 | tf_op jit(solution)/shard_map/ppermute | solution.py:132
  53.4 7.9 %collective-permute-start.18 = (f32[2,256,128]{2,1,0:T(8,128)S(1)}, f32[2,256,128]{2,1,0:T(8,128)S(1)}, u32[]{:S(2)}, u32[]{:S(2)}) collective-permute-start(f32[2,256,128]{2,1,0:T(8,128)S(1)} %pad_maximum_fusion.11), channel_id=1, source_target_pairs={{0,8},{4,12},{8,0},{12,4},{16,24},{20,28},{24,16},{28,20},{1,9},{5... | collective-permute-start | bytes 786440 | tf_op jit(solution)/shard_map/ppermute | solution.py:132
  63.6 16.7 %collective-permute-start.23 = (f32[8,160,128]{2,1,0:T(8,128)S(1)}, f32[8,160,128]{2,1,0:T(8,128)S(1)}, u32[]{:S(2)}, u32[]{:S(2)}) collective-permute-start(f32[8,160,128]{2,1,0:T(8,128)S(1)} %pad_maximum_fusion.4.rest_2_), channel_id=1, source_target_pairs={{0,4},{4,0},{8,12},{12,8},{16,20},{20,16},{24,28},{28,24},{1,5},{5... | collective-permute-start | bytes 1966088 | tf_op jit(solution)/shard_map/ppermute | solution.py:132
  64.8 16.4 %collective-permute-start.22 = (f32[8,160,128]{2,1,0:T(8,128)S(1)}, f32[8,160,128]{2,1,0:T(8,128)S(1)}, u32[]{:S(2)}, u32[]{:S(2)}) collective-permute-start(f32[8,160,128]{2,1,0:T(8,128)S(1)} %pad_maximum_fusion.3.rest_0_), channel_id=1, source_target_pairs={{0,2},{1,3},{2,0},{3,1},{4,6},{5,7},{6,4},{7,5},{8,10},{9,11},{10,... | collective-permute-start | bytes 1966088 | tf_op jit(solution)/shard_map/ppermute | solution.py:134
  66.3 14.9 %collective-permute-start.24 = (f32[8,160,128]{2,1,0:T(8,128)S(1)}, f32[8,160,128]{2,1,0:T(8,128)S(1)}, u32[]{:S(2)}, u32[]{:S(2)}) collective-permute-start(f32[8,160,128]{2,1,0:T(8,128)S(1)} %pad_maximum_fusion.3.rest_0_), channel_id=1, source_target_pairs={{0,1},{1,0},{2,3},{3,2},{4,5},{5,4},{6,7},{7,6},{8,9},{9,8},{10,11... | collective-permute-start | bytes 1966088 | tf_op jit(solution)/shard_map/ppermute | solution.py:134
  66.8 14.4 %collective-permute-start.25 = (f32[8,160,128]{2,1,0:T(8,128)S(1)}, f32[8,160,128]{2,1,0:T(8,128)S(1)}, u32[]{:S(2)}, u32[]{:S(2)}) collective-permute-start(f32[8,160,128]{2,1,0:T(8,128)S(1)} %pad_maximum_fusion.4.rest_2_), channel_id=1, source_target_pairs={{0,1},{1,0},{2,3},{3,2},{4,5},{5,4},{6,7},{7,6},{8,9},{9,8},{10,11... | collective-permute-start | bytes 1966088 | tf_op jit(solution)/shard_map/ppermute | solution.py:134
  81.2 9.6 %collective-permute-start.28 = (f32[8,160,128]{2,1,0:T(8,128)S(1)}, f32[8,160,128]{2,1,0:T(8,128)S(1)}, u32[]{:S(2)}, u32[]{:S(2)}) collective-permute-start(f32[8,160,128]{2,1,0:T(8,128)S(1)} %collective-permute-done.22.rest_4_), channel_id=1, source_target_pairs={{0,1},{1,0},{2,3},{3,2},{4,5},{5,4},{6,7},{7,6},{8,9},{9,8},{10,11... | collective-permute-start | bytes 1966088 | tf_op jit(solution)/shard_map/ppermute | solution.py:134
  81.2 9.6 %collective-permute-start.29 = (f32[8,160,128]{2,1,0:T(8,128)S(1)}, f32[8,160,128]{2,1,0:T(8,128)S(1)}, u32[]{:S(2)}, u32[]{:S(2)}) collective-permute-start(f32[8,160,128]{2,1,0:T(8,128)S(1)} %collective-permute-done.23.rest_6_), channel_id=1, source_target_pairs={{0,1},{1,0},{2,3},{3,2},{4,5},{5,4},{6,7},{7,6},{8,9},{9,8},{10,11... | collective-permute-start | bytes 1966088 | tf_op jit(solution)/shard_map/ppermute | solution.py:134
  81.8 8.3 %collective-permute-start.26 = (f32[4,128,128]{2,1,0:T(8,128)S(1)}, f32[4,128,128]{2,1,0:T(8,128)S(1)}, u32[]{:S(2)}, u32[]{:S(2)}) collective-permute-start(f32[4,128,128]{2,1,0:T(8,128)S(1)} %get-tuple-element.154), channel_id=1, source_target_pairs={{0,4},{4,0},{8,12},{12,8},{16,20},{20,16},{24,28},{28,24},{1,5},{5... | collective-permute-start | bytes 786440 | tf_op jit(solution)/shard_map/ppermute | solution.py:132
  82.8 8.0 %collective-permute-start.27 = (f32[4,128,128]{2,1,0:T(8,128)S(1)}, f32[4,128,128]{2,1,0:T(8,128)S(1)}, u32[]{:S(2)}, u32[]{:S(2)}) collective-permute-start(f32[4,128,128]{2,1,0:T(8,128)S(1)} %get-tuple-element.155), channel_id=1, source_target_pairs={{0,2},{1,3},{2,0},{3,1},{4,6},{5,7},{6,4},{7,5},{8,10},{9,11},{10,... | collective-permute-start | bytes 786440 | tf_op jit(solution)/shard_map/ppermute | solution.py:134
  90.8 12.8 %collective-permute-start.30 = (f32[8,128,128]{2,1,0:T(8,128)S(1)}, f32[8,128,128]{2,1,0:T(8,128)S(1)}, u32[]{:S(2)}, u32[]{:S(2)}) collective-permute-start(f32[8,128,128]{2,1,0:T(8,128)S(1)} %pad_maximum_fusion.5.rest_0_), channel_id=1, source_target_pairs={{0,2},{1,3},{2,0},{3,1},{4,6},{5,7},{6,4},{7,5},{8,10},{9,11},{10,... | collective-permute-start | bytes 1572872 | tf_op jit(solution)/shard_map/ppermute | solution.py:134
  91.5 12.5 %collective-permute-start.31 = (f32[8,128,128]{2,1,0:T(8,128)S(1)}, f32[8,128,128]{2,1,0:T(8,128)S(1)}, u32[]{:S(2)}, u32[]{:S(2)}) collective-permute-start(f32[8,128,128]{2,1,0:T(8,128)S(1)} %pad_maximum_fusion.6.rest_2_), channel_id=1, source_target_pairs={{0,4},{4,0},{8,12},{12,8},{16,20},{20,16},{24,28},{28,24},{1,5},{5... | collective-permute-start | bytes 1572872 | tf_op jit(solution)/shard_map/ppermute | solution.py:132
  92.5 11.4 %collective-permute-start.32 = (f32[8,128,128]{2,1,0:T(8,128)S(1)}, f32[8,128,128]{2,1,0:T(8,128)S(1)}, u32[]{:S(2)}, u32[]{:S(2)}) collective-permute-start(f32[8,128,128]{2,1,0:T(8,128)S(1)} %pad_maximum_fusion.5.rest_0_), channel_id=1, source_target_pairs={{0,1},{1,0},{2,3},{3,2},{4,5},{5,4},{6,7},{7,6},{8,9},{9,8},{10,11... | collective-permute-start | bytes 1572872 | tf_op jit(solution)/shard_map/ppermute | solution.py:134
  92.5 11.4 %collective-permute-start.33 = (f32[8,128,128]{2,1,0:T(8,128)S(1)}, f32[8,128,128]{2,1,0:T(8,128)S(1)}, u32[]{:S(2)}, u32[]{:S(2)}) collective-permute-start(f32[8,128,128]{2,1,0:T(8,128)S(1)} %pad_maximum_fusion.6.rest_2_), channel_id=1, source_target_pairs={{0,1},{1,0},{2,3},{3,2},{4,5},{5,4},{6,7},{7,6},{8,9},{9,8},{10,11... | collective-permute-start | bytes 1572872 | tf_op jit(solution)/shard_map/ppermute | solution.py:134
  121.0 9.7 %collective-permute-start.36 = (f32[16,256,128]{2,1,0:T(8,128)S(1)}, f32[16,256,128]{2,1,0:T(8,128)S(1)}, u32[]{:S(2)}, u32[]{:S(2)}) collective-permute-start(f32[16,256,128]{2,1,0:T(8,128)S(1)} %shard_map.282), channel_id=1, source_target_pairs={{0,1},{1,0},{2,3},{3,2},{4,5},{5,4},{6,7},{7,6},{8,9},{9,8},{10,11... | collective-permute-start | bytes 6291464 | tf_op jit(solution)/shard_map/ppermute | solution.py:134
  124.3 6.4 %collective-permute-start.37 = (f32[16,256,128]{2,1,0:T(8,128)S(1)}, f32[16,256,128]{2,1,0:T(8,128)S(1)}, u32[]{:S(2)}, u32[]{:S(2)}) collective-permute-start(f32[16,256,128]{2,1,0:T(8,128)S(1)} %shard_map.283), channel_id=1, source_target_pairs={{0,1},{1,0},{2,3},{3,2},{4,5},{5,4},{6,7},{7,6},{8,9},{9,8},{10,11... | collective-permute-start | bytes 6291464 | tf_op jit(solution)/shard_map/ppermute | solution.py:134
  130.9 34.5 %collective-permute-start.38 = (f32[8,256,128]{2,1,0:T(8,128)S(1)}, f32[8,256,128]{2,1,0:T(8,128)S(1)}, u32[]{:S(2)}, u32[]{:S(2)}) collective-permute-start(f32[8,256,128]{2,1,0:T(8,128)S(1)} %slice_add_fusion), channel_id=1, source_target_pairs={{0,8},{4,12},{8,0},{12,4},{16,24},{20,28},{24,16},{28,20},{1,9},{5... | collective-permute-start | bytes 3145736 | tf_op jit(solution)/shard_map/ppermute | solution.py:132
  132.7 32.7 %collective-permute-start.39 = (f32[4,256,128]{2,1,0:T(8,128)S(1)}, f32[4,256,128]{2,1,0:T(8,128)S(1)}, u32[]{:S(2)}, u32[]{:S(2)}) collective-permute-start(f32[4,256,128]{2,1,0:T(8,128)S(1)} %get-tuple-element.244), channel_id=1, source_target_pairs={{0,4},{4,0},{8,12},{12,8},{16,20},{20,16},{24,28},{28,24},{1,5},{5... | collective-permute-start | bytes 1572872 | tf_op jit(solution)/shard_map/ppermute | solution.py:132
  133.8 31.6 %collective-permute-start.40 = (f32[4,256,128]{2,1,0:T(8,128)S(1)}, f32[4,256,128]{2,1,0:T(8,128)S(1)}, u32[]{:S(2)}, u32[]{:S(2)}) collective-permute-start(f32[4,256,128]{2,1,0:T(8,128)S(1)} %get-tuple-element.243), channel_id=1, source_target_pairs={{0,2},{1,3},{2,0},{3,1},{4,6},{5,7},{6,4},{7,5},{8,10},{9,11},{10,... | collective-permute-start | bytes 1572872 | tf_op jit(solution)/shard_map/ppermute | solution.py:134
  135.3 30.1 %collective-permute-start.41 = (f32[4,256,128]{2,1,0:T(8,128)S(1)}, f32[4,256,128]{2,1,0:T(8,128)S(1)}, u32[]{:S(2)}, u32[]{:S(2)}) collective-permute-start(f32[4,256,128]{2,1,0:T(8,128)S(1)} %get-tuple-element.242), channel_id=1, source_target_pairs={{0,6},{1,7},{2,4},{3,5},{4,2},{5,3},{6,0},{7,1},{8,14},{9,15},{10,... | collective-permute-start | bytes 1572872 | tf_op jit(solution)/shard_map/ppermute | solution.py:137
  165.4 5.7 %collective-permute-start.42 = (f32[2,2,16,512]{3,2,1,0:T(8,128)S(1)}, f32[2,2,16,512]{3,2,1,0:T(8,128)S(1)}, u32[]{:S(2)}, u32[]{:S(2)}) collective-permute-start(f32[2,2,16,512]{3,2,1,0:T(8,128)S(1)} %get-tuple-element.207), channel_id=1, source_target_pairs={{0,1},{1,0},{2,3},{3,2},{4,5},{5,4},{6,7},{7,6},{8,9},{9,8},{10,11... | collective-permute-start | bytes 393224 | tf_op jit(solution)/shard_map/ppermute | solution.py:1007
  176.1 13.4 %collective-permute-start.45 = (f32[16,192,128]{2,1,0:T(8,128)}, f32[16,192,128]{2,1,0:T(8,128)}, u32[]{:S(2)}, u32[]{:S(2)}) collective-permute-start(f32[16,192,128]{2,1,0:T(8,128)} %get-tuple-element.216), channel_id=1, source_target_pairs={{0,1},{1,0},{2,3},{3,2},{4,5},{5,4},{6,7},{7,6},{8,9},{9,8},{10,11... | collective-permute-start | bytes 4718600 | tf_op jit(solution)/shard_map/ppermute | solution.py:134
  177.5 7.3 %collective-permute-start.49 = (f32[16,64,128]{2,1,0:T(8,128)}, f32[16,64,128]{2,1,0:T(8,128)}, u32[]{:S(2)}, u32[]{:S(2)}) collective-permute-start(f32[16,64,128]{2,1,0:T(8,128)} %get-tuple-element.227), channel_id=1, source_target_pairs={{0,1},{1,0},{2,3},{3,2},{4,5},{5,4},{6,7},{7,6},{8,9},{9,8},{10,11... | collective-permute-start | bytes 1572872 | tf_op jit(solution)/shard_map/ppermute | solution.py:134
  179.9 22.9 %collective-permute-start.54 = (f32[4,256,128]{2,1,0:T(8,128)}, f32[4,256,128]{2,1,0:T(8,128)}, u32[]{:S(2)}, u32[]{:S(2)}) collective-permute-start(f32[4,256,128]{2,1,0:T(8,128)} %fusion), channel_id=1, source_target_pairs={{0,4},{4,0},{8,12},{12,8},{16,20},{20,16},{24,28},{28,24},{1,5},{5... | collective-permute-start | bytes 1572872 | tf_op jit(solution)/shard_map/ppermute | solution.py:132
  185.9 12.5 %collective-permute-start.52 = (f32[4,64,128]{2,1,0:T(8,128)S(1)}, f32[4,64,128]{2,1,0:T(8,128)S(1)}, u32[]{:S(2)}, u32[]{:S(2)}) collective-permute-start(f32[4,64,128]{2,1,0:T(8,128)S(1)} %get-tuple-element.253), channel_id=1, source_target_pairs={{0,6},{1,7},{2,4},{3,5},{4,2},{5,3},{6,0},{7,1},{8,14},{9,15},{10,... | collective-permute-start | bytes 393224 | tf_op jit(solution)/shard_map/ppermute | solution.py:137
  187.7 11.8 %collective-permute-start.51 = (f32[4,64,128]{2,1,0:T(8,128)S(1)}, f32[4,64,128]{2,1,0:T(8,128)S(1)}, u32[]{:S(2)}, u32[]{:S(2)}) collective-permute-start(f32[4,64,128]{2,1,0:T(8,128)S(1)} %get-tuple-element.254), channel_id=1, source_target_pairs={{0,2},{1,3},{2,0},{3,1},{4,6},{5,7},{6,4},{7,5},{8,10},{9,11},{10,... | collective-permute-start | bytes 393224 | tf_op jit(solution)/shard_map/ppermute | solution.py:134
  188.4 12.2 %collective-permute-start.50 = (f32[4,64,128]{2,1,0:T(8,128)S(1)}, f32[4,64,128]{2,1,0:T(8,128)S(1)}, u32[]{:S(2)}, u32[]{:S(2)}) collective-permute-start(f32[4,64,128]{2,1,0:T(8,128)S(1)} %get-tuple-element.252), channel_id=1, source_target_pairs={{0,4},{4,0},{8,12},{12,8},{16,20},{20,16},{24,28},{28,24},{1,5},{5... | collective-permute-start | bytes 393224 | tf_op jit(solution)/shard_map/ppermute | solution.py:132
  191.8 24.5 %collective-permute-start.47 = (f32[4,208,128]{2,1,0:T(8,128)S(1)}, f32[4,208,128]{2,1,0:T(8,128)S(1)}, u32[]{:S(2)}, u32[]{:S(2)}) collective-permute-start(f32[4,208,128]{2,1,0:T(8,128)S(1)} %get-tuple-element.260), channel_id=1, source_target_pairs={{0,2},{1,3},{2,0},{3,1},{4,6},{5,7},{6,4},{7,5},{8,10},{9,11},{10,... | collective-permute-start | bytes 1277960 | tf_op jit(solution)/shard_map/ppermute | solution.py:134
  198.5 17.8 %collective-permute-start.46 = (f32[4,208,128]{2,1,0:T(8,128)S(1)}, f32[4,208,128]{2,1,0:T(8,128)S(1)}, u32[]{:S(2)}, u32[]{:S(2)}) collective-permute-start(f32[4,208,128]{2,1,0:T(8,128)S(1)} %get-tuple-element.261), channel_id=1, source_target_pairs={{0,4},{4,0},{8,12},{12,8},{16,20},{20,16},{24,28},{28,24},{1,5},{5... | collective-permute-start | bytes 1277960 | tf_op jit(solution)/shard_map/ppermute | solution.py:132
  199.5 19.3 %collective-permute-start.48 = (f32[4,208,128]{2,1,0:T(8,128)S(1)}, f32[4,208,128]{2,1,0:T(8,128)S(1)}, u32[]{:S(2)}, u32[]{:S(2)}) collective-permute-start(f32[4,208,128]{2,1,0:T(8,128)S(1)} %get-tuple-element.259), channel_id=1, source_target_pairs={{0,6},{1,7},{2,4},{3,5},{4,2},{5,3},{6,0},{7,1},{8,14},{9,15},{10,... | collective-permute-start | bytes 1277960 | tf_op jit(solution)/shard_map/ppermute | solution.py:137
  201.6 14.7 %collective-permute-start.53 = (f32[2,320,128]{2,1,0:T(8,128)S(1)}, f32[2,320,128]{2,1,0:T(8,128)S(1)}, u32[]{:S(2)}, u32[]{:S(2)}) collective-permute-start(f32[2,320,128]{2,1,0:T(8,128)S(1)} %fusion.4), channel_id=1, source_target_pairs={{0,8},{4,12},{8,0},{12,4},{16,24},{20,28},{24,16},{28,20},{1,9},{5... | collective-permute-start | bytes 983048 | tf_op jit(solution)/shard_map/ppermute | solution.py:132
  203.9 12.4 %collective-permute-start.55 = (f32[2,256,128]{2,1,0:T(8,128)S(1)}, f32[2,256,128]{2,1,0:T(8,128)S(1)}, u32[]{:S(2)}, u32[]{:S(2)}) collective-permute-start(f32[2,256,128]{2,1,0:T(8,128)S(1)} %fusion.6), channel_id=1, source_target_pairs={{0,16},{4,20},{8,24},{12,28},{16,0},{20,4},{24,8},{28,12},{1,17},{... | collective-permute-start | bytes 786440 | tf_op jit(solution)/shard_map/ppermute | solution.py:132
  218.9 19.6 %collective-permute-start.58 = (f32[1,208,128]{2,1,0:T(8,128)S(1)}, f32[1,208,128]{2,1,0:T(8,128)S(1)}, u32[]{:S(2)}, u32[]{:S(2)}) collective-permute-start(f32[1,208,128]{2,1,0:T(8,128)S(1)} %get-tuple-element.251), channel_id=1, source_target_pairs={{0,24},{4,28},{8,16},{12,20},{16,8},{20,12},{24,0},{28,4},{1,25},{... | collective-permute-start | bytes 319496 | tf_op jit(solution)/shard_map/ppermute | solution.py:132
  222.1 16.5 %collective-permute-start.57 = (f32[1,208,128]{2,1,0:T(8,128)S(1)}, f32[1,208,128]{2,1,0:T(8,128)S(1)}, u32[]{:S(2)}, u32[]{:S(2)}) collective-permute-start(f32[1,208,128]{2,1,0:T(8,128)S(1)} %get-tuple-element.249), channel_id=1, source_target_pairs={{0,16},{4,20},{8,24},{12,28},{16,0},{20,4},{24,8},{28,12},{1,17},{... | collective-permute-start | bytes 319496 | tf_op jit(solution)/shard_map/ppermute | solution.py:132
  222.1 16.5 %collective-permute-start.56 = (f32[1,208,128]{2,1,0:T(8,128)S(1)}, f32[1,208,128]{2,1,0:T(8,128)S(1)}, u32[]{:S(2)}, u32[]{:S(2)}) collective-permute-start(f32[1,208,128]{2,1,0:T(8,128)S(1)} %get-tuple-element.250), channel_id=1, source_target_pairs={{0,8},{4,12},{8,0},{12,4},{16,24},{20,28},{24,16},{28,20},{1,9},{5... | collective-permute-start | bytes 319496 | tf_op jit(solution)/shard_map/ppermute | solution.py:132
  225.3 12.0 %collective-permute-start.60 = (f32[1,320,128]{2,1,0:T(8,128)S(1)}, f32[1,320,128]{2,1,0:T(8,128)S(1)}, u32[]{:S(2)}, u32[]{:S(2)}) collective-permute-start(f32[1,320,128]{2,1,0:T(8,128)S(1)} %fusion.12), channel_id=1, source_target_pairs={{0,16},{4,20},{8,24},{12,28},{16,0},{20,4},{24,8},{28,12},{1,17},{... | collective-permute-start | bytes 491528 | tf_op jit(solution)/shard_map/ppermute | solution.py:132
  (59 other events, 905.1 us)

commit v5 on v4

--- a/solution.py
+++ b/solution.py
@@ -1147,7 +1147,7 @@
     )
     qkv_sum.keep(keep)
     sums = jnp.concatenate([(sums_away + sums_keep)[0:2], gln[0:2]], axis=0)
-    sent = qkv_sum.send(got, rider=sums.reshape(-1, 128))
+    sent = qkv_sum.send(got, out_sum.last, rider=sums.reshape(-1, 128))
     down_sum.send(sent)
     up_sum.absorb(out_sum, sent)
     up_sum.send()

time: 241 us -> 243 us (level)
  waiting for transfers between devices: 52.4 us -> 58.7 us
    ppermute x24, waiting for transfers between devices: 21.7 us -> 30.2 us  [send(): return lax.ppermute(x, 'dp', [(i, i ^ d) for i in range(self.dp)])]
    ppermute x3, waiting for transfers between devices: 7.81 us -> 5.16 us  [send(): return lax.ppermute(x, ('dp', 'fsdp'), pairs)]
    unnamed x105 -> x107, local copies, waits for them, and re-layouts: 7.38 us -> 6.78 us
  transfers between devices with their start and end apart: 62 -> 62, of which waited for: 21 -> 22; matrix products, arithmetic and copies ran while one was open for 14% -> 13% of each run, Pallas kernels for 29% -> 29%
where the time goes in v5:
time: 243 us
  Pallas kernels  88.3 us (36%)
  waiting for transfers between devices  58.7 us (24%)
  starting transfers between devices  55.7 us (23%)
  local copies, waits for them, and re-layouts  19.8 us (8%)
  other arithmetic  18.2 us (7%)
    ppermute x24, starting transfers between devices, send(): return lax.ppermute(x, 'dp', [(i, i ^ d) for i in range(self.dp)])  33.4 us
    ppermute x24, waiting for transfers between devices, send(): return lax.ppermute(x, 'dp', [(i, i ^ d) for i in range(self.dp)])  30.2 us
    pallas_call x2, Pallas kernels, attention_backward(): pl.pallas_call(body, compiler_params=ROOM, cost_estimate=cost(8), grid=(c...  19.8 us
    ppermute x27, waiting for transfers between devices, send(): return lax.ppermute(x, 'fsdp', [(i, i ^ f) for i in range(self.fsdp)])  18.7 us
    ppermute x27, starting transfers between devices, send(): return lax.ppermute(x, 'fsdp', [(i, i ^ f) for i in range(self.fsdp)])  12.7 us
    pallas_call x1, Pallas kernels, hidden_stage(): pl.pallas_call(body, compiler_params=ROOM, cost_estimate=cost(15), grid=(...  11.6 us
    pallas_call x2, Pallas kernels, attention_forward(): pl.pallas_call(body, compiler_params=ROOM, cost_estimate=cost(9.5), grid=...  11.2 us
    unnamed x107, local copies, waits for them, and re-layouts  6.78 us
  transfers between devices with their start and end apart: 62, of which 22 were waited for; matrix products, arithmetic and copies ran while one was open for 13% of the time, Pallas kernels for 29%

profile of v5, /device:TPU:0, one launch (start us, length us, event | category | flops | bytes accessed | tf_op | source)
XLA Modules:
  0.0 242.5 jit_solution(4255938336163301970)
XLA Ops:
  3.2 3.0 %collective-permute-start = (f32[1,208,128]{2,1,0:T(8,128)S(1)}, f32[1,208,128]{2,1,0:T(8,128)S(1)}, u32[]{:S(2)}, u32[]{:S(2)}) collective-permute-start(f32[1,208,128]{2,1,0:T(8,128)S(1)} %bitcast.95), channel_id=1, source_target_pairs={{0,8},{4,12},{8,0},{12,4},{16,24},{20,28},{24,16},{28,20},{1,9},{5... | collective-permute-start | bytes 319496 | tf_op jit(solution)/shard_map/ppermute | solution.py:132
  6.2 2.6 %collective-permute-start.1 = (f32[1,208,128]{2,1,0:T(8,128)S(1)}, f32[1,208,128]{2,1,0:T(8,128)S(1)}, u32[]{:S(2)}, u32[]{:S(2)}) collective-permute-start(f32[1,208,128]{2,1,0:T(8,128)S(1)} %bitcast.96), channel_id=1, source_target_pairs={{0,16},{4,20},{8,24},{12,28},{16,0},{20,4},{24,8},{28,12},{1,17},{... | collective-permute-start | bytes 319496 | tf_op jit(solution)/shard_map/ppermute | solution.py:132
  19.9 2.0 collective-permute-start.7
  21.9 1.5 collective-permute-start.9
  23.5 1.7 collective-permute-start.3
  26.4 5.3 %collective-permute-done.4 = f32[4,96,128]{2,1,0:T(8,128)S(1)} collective-permute-done((f32[4,96,128]{2,1,0:T(8,128)S(1)}, f32[4,96,128]{2,1,0:T(8,128)S(1)}, u32[]{:S(2)}, u32[]{:S(2)}) %collective-permute-start.4) | collective-permute-done | bytes 196640 | tf_op jit(solution)/shard_map/ppermute | solution.py:134
  33.2 1.7 pad_maximum_fusion.10
  34.9 2.5 %collective-permute-start.10 = (f32[2,320,128]{2,1,0:T(8,128)}, f32[2,320,128]{2,1,0:T(8,128)}, u32[]{:S(2)}, u32[]{:S(2)}) collective-permute-start(f32[2,320,128]{2,1,0:T(8,128)} %pad_maximum_fusion.10), channel_id=1, source_target_pairs={{0,8},{4,12},{8,0},{12,4},{16,24},{20,28},{24,16},{28,20},{1,9},{5... | collective-permute-start | bytes 983048 | tf_op jit(solution)/shard_map/ppermute | solution.py:132
  38.7 1.6 concatenate.77.outer_bias
  40.3 5.8 %collective-permute-done.11 = f32[1,256,128]{2,1,0:T(8,128)} collective-permute-done((f32[1,256,128]{2,1,0:T(8,128)}, f32[1,256,128]{2,1,0:T(8,128)}, u32[]{:S(2)}, u32[]{:S(2)}) %collective-permute-start.11) | collective-permute-done | bytes 131104 | tf_op jit(solution)/shard_map/ppermute | solution.py:132
  50.5 1.5 collective-permute-start.17
  53.9 1.2 collective-permute-start.18
  55.1 6.0 %shard_map.276 = (f32[512,1536]{1,0:T(8,128)S(1)}, bf16[1536,512]{1,0:T(8,128)(2,1)S(1)}, bf16[1536,512]{1,0:T(8,128)(2,1)S(1)}, f32[512,512]{1,0:T(8,128)S(1)},...) custom-call(s32[2]{0:T(128)S(1)} %copy-done.33, ...), custom_call_target="tpu_custom_call" | custom-call | flops 333000000 | bytes 925000 | tf_op jit(solution)/shard_map/pallas_call | solution.py:371
  62.6 1.5 collective-permute-start.19
  67.5 5.6 %shard_map.277 = (f32[512,512]{1,0:T(8,128)S(1)}, f32[512,512]{1,0:T(8,128)S(1)}) custom-call(f32[512,1536]{1,0:T(8,128)S(1)} %get-tuple-element.153.q.k.v, f32[512,1536]{1,0:T(8,128)S(1)} %get-tuple-element.153.q.k.v, f32[512,1536]{1,0:T(8,128)S(1)} %get-tuple-element.153.q.k.v, f32[2,2,32,512]{3,2,1,0:T(8,128)S(1)} %constant_dynamic-update-slice_fusion.2.fk.fv, ...), custom_call_target="tpu_custom_call" | custom-call | flops 427500000 | bytes 1187500 | tf_op jit(solution)/shard_map/pallas_call | solution.py:498
  73.2 7.7 %collective-permute-done.23.rest_6_ = f32[8,160,128]{2,1,0:T(8,128)S(1)} collective-permute-done((f32[8,160,128]{2,1,0:T(8,128)S(1)}, f32[8,160,128]{2,1,0:T(8,128)S(1)}, u32[]{:S(2)}, u32[]{:S(2)}) %collective-permute-start.23) | collective-permute-done | bytes 655392 | tf_op jit(solution)/shard_map/ppermute | solution.py:132
  83.8 5.6 %shard_map.278 = (f32[512,512]{1,0:T(8,128)S(1)}, f32[512,512]{1,0:T(8,128)S(1)}) custom-call(f32[512,1536]{1,0:T(8,128)S(1)} %get-tuple-element.153.q.k.v, f32[512,1536]{1,0:T(8,128)S(1)} %get-tuple-element.153.q.k.v, f32[512,1536]{1,0:T(8,128)S(1)} %get-tuple-element.153.q.k.v, ...), custom_call_target="tpu_custom_call", output_to_operand_aliasing={{0}: (10, {}), {1}: (11, {})} | custom-call | flops 427500000 | bytes 1187500 | tf_op jit(solution)/shard_map/pallas_call | solution.py:498
  93.5 2.4 shard_map.279
  98.3 5.9 %collective-permute-done.30.rest_4_ = f32[8,128,128]{2,1,0:T(8,128)S(1)} collective-permute-done((f32[8,128,128]{2,1,0:T(8,128)S(1)}, f32[8,128,128]{2,1,0:T(8,128)S(1)}, u32[]{:S(2)}, u32[]{:S(2)}) %collective-permute-start.30) | collective-permute-done | bytes 524320 | tf_op jit(solution)/shard_map/ppermute | solution.py:134
  105.0 1.4 collective-permute-done.34.rest_5_
  107.1 11.6 %shard_map.281 = (bf16[512,2048]{1,0:T(8,128)(2,1)S(1)}, bf16[512,2048]{1,0:T(8,128)(2,1)S(1)}, bf16[512,2048]{1,0:T(8,128)(2,1)S(1)}, bf16[512,2048]{1,0:T(8,12...) custom-call(s32[2]{0:T(128)S(1)} %copy-done.33, ...), custom_call_target="tpu_custom_call" | custom-call | flops 675000000 | bytes 1875000 | tf_op jit(solution)/shard_map/pallas_call | solution.py:697
  118.7 2.7 %shard_map.282 = f32[16,256,128]{2,1,0:T(8,128)S(1)} custom-call(s32[2]{0:T(128)S(1)} %copy-done.33, bf16[512,512]{1,0:T(8,128)(2,1)S(1)} %get-tuple-element.184.c0, bf16[512,512]{1,0:T(8,128)(2,1)S(1)} %get-tuple-element.177.c1, bf16[512,2048]{1,0:T(8,128)(2,1)S(1)} %get-tuple-element.178.h0, bf16[512,2048]{1,0:T(8,128)(2,1)S(1)} %get-tuple-element.179.h1), custom_call_target="tpu_custom_call" | custom-call | flops 12150000 | bytes 33750 | tf_op jit(solution)/shard_map/pallas_call | solution.py:736
  121.7 3.2 %shard_map.283 = f32[16,256,128]{2,1,0:T(8,128)S(1)} custom-call(s32[2]{0:T(128)S(1)} %copy-done.33, bf16[512,512]{1,0:T(8,128)(2,1)S(1)} %get-tuple-element.185.n0, bf16[512,512]{1,0:T(8,128)(2,1)S(1)} %get-tuple-element.181.n1, bf16[512,2048]{1,0:T(8,128)(2,1)S(1)} %get-tuple-element.182.p0, bf16[512,2048]{1,0:T(8,128)(2,1)S(1)} %get-tuple-element.183.p1), custom_call_target="tpu_custom_call" | custom-call | flops 14400000 | bytes 40000 | tf_op jit(solution)/shard_map/pallas_call | solution.py:789
  125.3 2.7 %shard_map.284 = f32[16,256,128]{2,1,0:T(8,128)S(1)} custom-call(s32[2]{0:T(128)S(1)} %copy-done.33, bf16[512,512]{1,0:T(8,128)(2,1)S(1)} %get-tuple-element.184.c0, bf16[512,512]{1,0:T(8,128)(2,1)S(1)} %get-tuple-element.177.c1, bf16[512,2048]{1,0:T(8,128)(2,1)S(1)} %get-tuple-element.178.h0, bf16[512,2048]{1,0:T(8,128)(2,1)S(1)} %get-tuple-element.179.h1), custom_call_target="tpu_custom_call" | custom-call | flops 12150000 | bytes 33750 | tf_op jit(solution)/shard_map/pallas_call | solution.py:736
  128.0 3.2 %shard_map.285 = f32[16,256,128]{2,1,0:T(8,128)S(1)} custom-call(s32[2]{0:T(128)S(1)} %copy-done.33, bf16[512,512]{1,0:T(8,128)(2,1)S(1)} %get-tuple-element.185.n0, bf16[512,512]{1,0:T(8,128)(2,1)S(1)} %get-tuple-element.181.n1, bf16[512,2048]{1,0:T(8,128)(2,1)S(1)} %get-tuple-element.182.p0, bf16[512,2048]{1,0:T(8,128)(2,1)S(1)} %get-tuple-element.183.p1), custom_call_target="tpu_custom_call" | custom-call | flops 14400000 | bytes 40000 | tf_op jit(solution)/shard_map/pallas_call | solution.py:789
  133.7 1.5 collective-permute-start.40
  136.2 4.9 %shard_map.286 = (f32[512,512]{1,0:T(8,128)S(1)}, f32[8,512]{1,0:T(8,128)S(1)}) custom-call(f32[512,512]{1,0:T(8,128)S(1)} %bitcast.92, f32[512,512]{1,0:T(8,128)S(1)} %copy-done.25, f32[512,128]{1,0:T(8,128)S(1)} %get-tuple-element.189.inv_ref, f32[8,512]{1,0:T(8,128)S(1)} %get-tuple-element.172.ln_ref.ln_r, bf16[512,2048]{1,0:T(8,128)(2,1)S(1)} %get-tuple-element.182.p0, ...), custom_call_target="tpu_custom_call" | custom-call | flops 382500000 | bytes 1062500 | tf_op jit(solution)/shard_map/pallas_call | solution.py:857
  141.1 2.4 %shard_map.287 = (f32[512,512]{1,0:T(8,128)S(1)}, f32[16,64,128]{2,1,0:T(8,128)S(1)}, f32[16,64,128]{2,1,0:T(8,128)S(1)}) custom-call(s32[2]{0:T(128)S(1)} %copy-done.33, f32[512,512]{1,0:T(8,128)S(1)} %get-tuple-element.192.gm_ref.gm_r, f32[512,512]{1,0:T(8,128)S(1)} %get-tuple-element.154.att.rest_0_, ...), custom_call_target="tpu_custom_call" | custom-call | flops 225000000 | bytes 625000 | tf_op jit(solution)/shard_map/pallas_call | solution.py:889
  144.5 9.7 %shard_map.288 = (f32[512,512]{1,0:T(8,128)S(1)}, f32[512,512]{1,0:T(8,128)S(1)}, f32[512,512]{1,0:T(8,128)S(1)}, f32[2,2,16,512]{3,2,1,0:T(8,128)S(1)}, f32[2,2...) custom-call(f32[512,1536]{1,0:T(8,128)S(1)} %get-tuple-element.153.q.k.v, f32[512,1536]{1,0:T(8,128)S(1)} %get-tuple-element.153.q.k.v, ...), custom_call_target="tpu_custom_call" | custom-call | flops 360000000 | bytes 1000000 | tf_op jit(solution)/shard_map/pallas_call | solution.py:570
  154.3 10.0 %shard_map.289 = (f32[512,512]{1,0:T(8,128)S(1)}, f32[512,512]{1,0:T(8,128)S(1)}, f32[512,512]{1,0:T(8,128)S(1)}, f32[2,2,16,512]{3,2,1,0:T(8,128)S(1)}, f32[2,2...) custom-call(f32[512,1536]{1,0:T(8,128)S(1)} %get-tuple-element.153.q, ...), custom_call_target="tpu_custom_call", output_to_operand_aliasing={{0}: (13, {}), {1}: (14, {}), {2}: (15, {}), {3}: (16, {}),... | custom-call | flops 360000000 | bytes 1000000 | tf_op jit(solution)/shard_map/pallas_call | solution.py:570
  164.4 1.6 collective-permute-start.43
  166.3 2.6 %collective-permute-done.43.g5a_r = f32[2,2,8,512]{3,2,1,0:T(8,128)S(1)} collective-permute-done((f32[2,2,8,512]{3,2,1,0:T(8,128)S(1)}, f32[2,2,8,512]{3,2,1,0:T(8,128)S(1)}, u32[]{:S(2)}, u32[]{:S(2)}) %collective-permute-start.43) | collective-permute-done | bytes 65568 | tf_op jit(solution)/shard_map/ppermute | solution.py:1007
  171.2 3.7 %shard_map.291 = (f32[16,192,128]{2,1,0:T(8,128)}, f32[8,512]{1,0:T(8,128)S(1)}) custom-call(s32[2]{0:T(128)S(1)} %copy-done.33, bf16[512,1536]{1,0:T(8,128)(2,1)S(1)} %get-tuple-element.211.gph_r, bf16[512,1536]{1,0:T(8,128)(2,1)S(1)} %get-tuple-element.212.gpl_r, f32[1536,128]{1,0:T(8,128)S(1)} %get-tuple-element.216.col_r, ...), custom_call_target="tpu_custom_call" | custom-call | flops 11250000 | bytes 31250 | tf_op jit(solution)/shard_map/pallas_call | solution.py:989
  177.5 2.6 %shard_map.292 = (f32[16,192,128]{2,1,0:T(8,128)S(1)}, f32[8,512]{1,0:T(8,128)S(1)}) custom-call(s32[2]{0:T(128)S(1)} %copy-done.33, bf16[512,1536]{1,0:T(8,128)(2,1)S(1)} %get-tuple-element.211.gph_r, bf16[512,1536]{1,0:T(8,128)(2,1)S(1)} %get-tuple-element.212.gpl_r, f32[1536,128]{1,0:T(8,128)S(1)} %get-tuple-element.216.col_r, ...), custom_call_target="tpu_custom_call" | custom-call | flops 11250000 | bytes 31250 | tf_op jit(solution)/shard_map/pallas_call | solution.py:989
  183.1 1.3 collective-permute-start.48
  185.6 8.8 %collective-permute-done.47 = f32[4,64,128]{2,1,0:T(8,128)} collective-permute-done((f32[4,64,128]{2,1,0:T(8,128)}, f32[4,64,128]{2,1,0:T(8,128)}, u32[]{:S(2)}, u32[]{:S(2)}) %collective-permute-start.47) | collective-permute-done | bytes 131104 | tf_op jit(solution)/shard_map/ppermute | solution.py:132
  194.4 2.9 %collective-permute-done.49 = f32[4,64,128]{2,1,0:T(8,128)} collective-permute-done((f32[4,64,128]{2,1,0:T(8,128)S(1)}, f32[4,64,128]{2,1,0:T(8,128)}, u32[]{:S(2)}, u32[]{:S(2)}) %collective-permute-start.49) | collective-permute-done | bytes 131104 | tf_op jit(solution)/shard_map/ppermute | solution.py:137
  197.3 2.2 slice_add_fusion.6
  201.3 1.9 collective-permute-start.52
  206.6 2.7 %collective-permute-start.55 = (f32[2,256,128]{2,1,0:T(8,128)S(1)}, f32[2,256,128]{2,1,0:T(8,128)S(1)}, u32[]{:S(2)}, u32[]{:S(2)}) collective-permute-start(f32[2,256,128]{2,1,0:T(8,128)S(1)} %fusion.6), channel_id=1, source_target_pairs={{0,16},{4,20},{8,24},{12,28},{16,0},{20,4},{24,8},{28,12},{1,17},{... | collective-permute-start | bytes 786440 | tf_op jit(solution)/shard_map/ppermute | solution.py:132
  209.4 3.8 %shard_map.293 = f32[512,512]{1,0:T(8,128)} custom-call(bf16[512,1536]{1,0:T(8,128)(2,1)S(1)} %copy-done.9, bf16[512,1536]{1,0:T(8,128)(2,1)S(1)} %copy-done.11, bf16[1536,512]{1,0:T(8,128)(2,1)S(1)} %copy-done.5, bf16[1536,512]{1,0:T(8,128)(2,1)S(1)} %copy-done.7, f32[512,512]{1,0:T(8,128)S(1)} %copy-done.13, f32[512,128]{1,0:T(8,128)S(1)} %copy-done.32, ...), custom_call_target="tpu_custom_call" | custom-call | flops 333000000 | bytes 925000 | tf_op jit(solution)/shard_map/pallas_call | solution.py:941
  213.1 5.8 %shard_map.294 = f32[512,512]{1,0:T(8,128)} custom-call(f32[512,512]{1,0:T(8,128)S(1)} %copy-done.30, bf16[512,2048]{1,0:T(8,128)(2,1)S(1)} %get-tuple-element.178.h0, bf16[512,2048]{1,0:T(8,128)(2,1)S(1)} %copy-done.3, bf16[512,2048]{1,0:T(8,128)(2,1)S(1)} %copy-done.15, bf16[512,2048]{1,0:T(8,128)(2,1)S(1)} %copy-done.17), custom_call_target="tpu_custom_call" | custom-call | flops 360000000 | bytes 1000000 | tf_op jit(solution)/shard_map/pallas_call | solution.py:821
  219.0 2.2 collective-permute-done.52
  221.3 3.1 %collective-permute-start.58 = (f32[1,208,128]{2,1,0:T(8,128)S(1)}, f32[1,208,128]{2,1,0:T(8,128)S(1)}, u32[]{:S(2)}, u32[]{:S(2)}) collective-permute-start(f32[1,208,128]{2,1,0:T(8,128)S(1)} %get-tuple-element.253), channel_id=1, source_target_pairs={{0,24},{4,28},{8,16},{12,20},{16,8},{20,12},{24,0},{28,4},{1,25},{... | collective-permute-start | bytes 319496 | tf_op jit(solution)/shard_map/ppermute | solution.py:132
  224.4 1.3 collective-permute-start.56
  227.3 1.8 collective-permute-start.60
  229.1 2.7 %collective-permute-done.59 = f32[1,256,128]{2,1,0:T(8,128)S(1)} collective-permute-done((f32[1,256,128]{2,1,0:T(8,128)S(1)}, f32[1,256,128]{2,1,0:T(8,128)S(1)}, u32[]{:S(2)}, u32[]{:S(2)}) %collective-permute-start.59) | collective-permute-done | bytes 131104 | tf_op jit(solution)/shard_map/ppermute | solution.py:134
  233.5 5.7 %collective-permute-done.60 = f32[1,320,128]{2,1,0:T(8,128)S(1)} collective-permute-done((f32[1,320,128]{2,1,0:T(8,128)S(1)}, f32[1,320,128]{2,1,0:T(8,128)S(1)}, u32[]{:S(2)}, u32[]{:S(2)}) %collective-permute-start.60) | collective-permute-done | bytes 163872 | tf_op jit(solution)/shard_map/ppermute | solution.py:132
  (304 shorter events, 65.6 us)
Async XLA Ops:
  3.2 16.8 %collective-permute-start = (f32[1,208,128]{2,1,0:T(8,128)S(1)}, f32[1,208,128]{2,1,0:T(8,128)S(1)}, u32[]{:S(2)}, u32[]{:S(2)}) collective-permute-start(f32[1,208,128]{2,1,0:T(8,128)S(1)} %bitcast.95), channel_id=1, source_target_pairs={{0,8},{4,12},{8,0},{12,4},{16,24},{20,28},{24,16},{28,20},{1,9},{5... | collective-permute-start | bytes 319496 | tf_op jit(solution)/shard_map/ppermute | solution.py:132
  6.2 13.7 %collective-permute-start.1 = (f32[1,208,128]{2,1,0:T(8,128)S(1)}, f32[1,208,128]{2,1,0:T(8,128)S(1)}, u32[]{:S(2)}, u32[]{:S(2)}) collective-permute-start(f32[1,208,128]{2,1,0:T(8,128)S(1)} %bitcast.96), channel_id=1, source_target_pairs={{0,16},{4,20},{8,24},{12,28},{16,0},{20,4},{24,8},{28,12},{1,17},{... | collective-permute-start | bytes 319496 | tf_op jit(solution)/shard_map/ppermute | solution.py:132
  8.8 11.2 %collective-permute-start.2 = (f32[1,208,128]{2,1,0:T(8,128)S(1)}, f32[1,208,128]{2,1,0:T(8,128)S(1)}, u32[]{:S(2)}, u32[]{:S(2)}) collective-permute-start(f32[1,208,128]{2,1,0:T(8,128)S(1)} %bitcast.97), channel_id=1, source_target_pairs={{0,24},{4,28},{8,16},{12,20},{16,8},{20,12},{24,0},{28,4},{1,25},{... | collective-permute-start | bytes 319496 | tf_op jit(solution)/shard_map/ppermute | solution.py:132
  8.8 9.9 %collective-permute-start.8 = (s32[2,256]{1,0:T(2,128)}, s32[2,256]{1,0:T(2,128)S(1)}, u32[]{:S(2)}, u32[]{:S(2)}) collective-permute-start(s32[2,256]{1,0:T(2,128)} %param.22), channel_id=1, source_target_pairs={{0,1},{1,0},{2,3},{3,2},{4,5},{5,4},{6,7},{7,6},{8,9},{9,8},{10,11... | collective-permute-start | bytes 6152 | tf_op jit(solution)/shard_map/ppermute | solution.py:1007
  19.9 13.3 %collective-permute-start.7 = (f32[1,320,128]{2,1,0:T(8,128)S(1)}, f32[1,320,128]{2,1,0:T(8,128)}, u32[]{:S(2)}, u32[]{:S(2)}) collective-permute-start(f32[1,320,128]{2,1,0:T(8,128)S(1)} %maximum_bitcast_fusion), channel_id=1, source_target_pairs={{0,16},{4,20},{8,24},{12,28},{16,0},{20,4},{24,8},{28,12},{1,17},{... | collective-permute-start | bytes 491528 | tf_op jit(solution)/shard_map/ppermute | solution.py:132
  23.5 8.2 %collective-permute-start.3 = (f32[4,112,128]{2,1,0:T(8,128)S(1)}, f32[4,112,128]{2,1,0:T(8,128)S(1)}, u32[]{:S(2)}, u32[]{:S(2)}) collective-permute-start(f32[4,112,128]{2,1,0:T(8,128)S(1)} %slice.405), channel_id=1, source_target_pairs={{0,4},{4,0},{8,12},{12,8},{16,20},{20,16},{24,28},{28,24},{1,5},{5... | collective-permute-start | bytes 688136 | tf_op jit(solution)/shard_map/ppermute | solution.py:132
  25.2 6.5 %collective-permute-start.4 = (f32[4,96,128]{2,1,0:T(8,128)S(1)}, f32[4,96,128]{2,1,0:T(8,128)S(1)}, u32[]{:S(2)}, u32[]{:S(2)}) collective-permute-start(f32[4,96,128]{2,1,0:T(8,128)S(1)} %pad_maximum_fusion.12), channel_id=1, source_target_pairs={{0,2},{1,3},{2,0},{3,1},{4,6},{5,7},{6,4},{7,5},{8,10},{9,11},{10,... | collective-permute-start | bytes 589832 | tf_op jit(solution)/shard_map/ppermute | solution.py:134
  31.8 15.1 %collective-permute-start.5 = (f32[8,112,128]{2,1,0:T(8,128)S(1)}, f32[8,112,128]{2,1,0:T(8,128)S(1)}, u32[]{:S(2)}, u32[]{:S(2)}) collective-permute-start(f32[8,112,128]{2,1,0:T(8,128)S(1)} %pad_maximum_fusion.7.rest_0_), channel_id=1, source_target_pairs={{0,2},{1,3},{2,0},{3,1},{4,6},{5,7},{6,4},{7,5},{8,10},{9,11},{10,... | collective-permute-start | bytes 1376264 | tf_op jit(solution)/shard_map/ppermute | solution.py:134
  32.4 14.5 %collective-permute-start.6 = (f32[8,96,128]{2,1,0:T(8,128)S(1)}, f32[8,96,128]{2,1,0:T(8,128)}, u32[]{:S(2)}, u32[]{:S(2)}) collective-permute-start(f32[8,96,128]{2,1,0:T(8,128)S(1)} %pad_maximum_fusion.9.rest_2_), channel_id=1, source_target_pairs={{0,4},{4,0},{8,12},{12,8},{16,20},{20,16},{24,28},{28,24},{1,5},{5... | collective-permute-start | bytes 1179656 | tf_op jit(solution)/shard_map/ppermute | solution.py:132
  34.9 12.0 %collective-permute-start.10 = (f32[2,320,128]{2,1,0:T(8,128)}, f32[2,320,128]{2,1,0:T(8,128)}, u32[]{:S(2)}, u32[]{:S(2)}) collective-permute-start(f32[2,320,128]{2,1,0:T(8,128)} %pad_maximum_fusion.10), channel_id=1, source_target_pairs={{0,8},{4,12},{8,0},{12,4},{16,24},{20,28},{24,16},{28,20},{1,9},{5... | collective-permute-start | bytes 983048 | tf_op jit(solution)/shard_map/ppermute | solution.py:132
  37.4 8.7 %collective-permute-start.11 = (f32[1,256,128]{2,1,0:T(8,128)}, f32[1,256,128]{2,1,0:T(8,128)}, u32[]{:S(2)}, u32[]{:S(2)}) collective-permute-start(f32[1,256,128]{2,1,0:T(8,128)} %bitcast.20), channel_id=1, source_target_pairs={{0,16},{4,20},{8,24},{12,28},{16,0},{20,4},{24,8},{28,12},{1,17},{... | collective-permute-start | bytes 393224 | tf_op jit(solution)/shard_map/ppermute | solution.py:132
  50.5 11.3 %collective-permute-start.17 = (f32[4,160,128]{2,1,0:T(8,128)S(1)}, f32[4,160,128]{2,1,0:T(8,128)S(1)}, u32[]{:S(2)}, u32[]{:S(2)}) collective-permute-start(f32[4,160,128]{2,1,0:T(8,128)S(1)} %get-tuple-element.142), channel_id=1, source_target_pairs={{0,2},{1,3},{2,0},{3,1},{4,6},{5,7},{6,4},{7,5},{8,10},{9,11},{10,... | collective-permute-start | bytes 983048 | tf_op jit(solution)/shard_map/ppermute | solution.py:134
  52.0 9.8 %collective-permute-start.16 = (f32[4,160,128]{2,1,0:T(8,128)S(1)}, f32[4,160,128]{2,1,0:T(8,128)S(1)}, u32[]{:S(2)}, u32[]{:S(2)}) collective-permute-start(f32[4,160,128]{2,1,0:T(8,128)S(1)} %get-tuple-element.141), channel_id=1, source_target_pairs={{0,4},{4,0},{8,12},{12,8},{16,20},{20,16},{24,28},{28,24},{1,5},{5... | collective-permute-start | bytes 983048 | tf_op jit(solution)/shard_map/ppermute | solution.py:132
  53.9 8.0 %collective-permute-start.18 = (f32[2,256,128]{2,1,0:T(8,128)S(1)}, f32[2,256,128]{2,1,0:T(8,128)S(1)}, u32[]{:S(2)}, u32[]{:S(2)}) collective-permute-start(f32[2,256,128]{2,1,0:T(8,128)S(1)} %pad_maximum_fusion.11), channel_id=1, source_target_pairs={{0,8},{4,12},{8,0},{12,4},{16,24},{20,28},{24,16},{28,20},{1,9},{5... | collective-permute-start | bytes 786440 | tf_op jit(solution)/shard_map/ppermute | solution.py:132
  64.1 16.7 %collective-permute-start.23 = (f32[8,160,128]{2,1,0:T(8,128)S(1)}, f32[8,160,128]{2,1,0:T(8,128)S(1)}, u32[]{:S(2)}, u32[]{:S(2)}) collective-permute-start(f32[8,160,128]{2,1,0:T(8,128)S(1)} %pad_maximum_fusion.4.rest_2_), channel_id=1, source_target_pairs={{0,4},{4,0},{8,12},{12,8},{16,20},{20,16},{24,28},{28,24},{1,5},{5... | collective-permute-start | bytes 1966088 | tf_op jit(solution)/shard_map/ppermute | solution.py:132
  65.3 16.4 %collective-permute-start.22 = (f32[8,160,128]{2,1,0:T(8,128)S(1)}, f32[8,160,128]{2,1,0:T(8,128)S(1)}, u32[]{:S(2)}, u32[]{:S(2)}) collective-permute-start(f32[8,160,128]{2,1,0:T(8,128)S(1)} %pad_maximum_fusion.3.rest_0_), channel_id=1, source_target_pairs={{0,2},{1,3},{2,0},{3,1},{4,6},{5,7},{6,4},{7,5},{8,10},{9,11},{10,... | collective-permute-start | bytes 1966088 | tf_op jit(solution)/shard_map/ppermute | solution.py:134
  66.9 14.8 %collective-permute-start.24 = (f32[8,160,128]{2,1,0:T(8,128)S(1)}, f32[8,160,128]{2,1,0:T(8,128)S(1)}, u32[]{:S(2)}, u32[]{:S(2)}) collective-permute-start(f32[8,160,128]{2,1,0:T(8,128)S(1)} %pad_maximum_fusion.3.rest_0_), channel_id=1, source_target_pairs={{0,1},{1,0},{2,3},{3,2},{4,5},{5,4},{6,7},{7,6},{8,9},{9,8},{10,11... | collective-permute-start | bytes 1966088 | tf_op jit(solution)/shard_map/ppermute | solution.py:134
  67.4 14.3 %collective-permute-start.25 = (f32[8,160,128]{2,1,0:T(8,128)S(1)}, f32[8,160,128]{2,1,0:T(8,128)S(1)}, u32[]{:S(2)}, u32[]{:S(2)}) collective-permute-start(f32[8,160,128]{2,1,0:T(8,128)S(1)} %pad_maximum_fusion.4.rest_2_), channel_id=1, source_target_pairs={{0,1},{1,0},{2,3},{3,2},{4,5},{5,4},{6,7},{7,6},{8,9},{9,8},{10,11... | collective-permute-start | bytes 1966088 | tf_op jit(solution)/shard_map/ppermute | solution.py:134
  81.7 9.7 %collective-permute-start.28 = (f32[8,160,128]{2,1,0:T(8,128)S(1)}, f32[8,160,128]{2,1,0:T(8,128)S(1)}, u32[]{:S(2)}, u32[]{:S(2)}) collective-permute-start(f32[8,160,128]{2,1,0:T(8,128)S(1)} %collective-permute-done.22.rest_4_), channel_id=1, source_target_pairs={{0,1},{1,0},{2,3},{3,2},{4,5},{5,4},{6,7},{7,6},{8,9},{9,8},{10,11... | collective-permute-start | bytes 1966088 | tf_op jit(solution)/shard_map/ppermute | solution.py:134
  81.7 9.7 %collective-permute-start.29 = (f32[8,160,128]{2,1,0:T(8,128)S(1)}, f32[8,160,128]{2,1,0:T(8,128)S(1)}, u32[]{:S(2)}, u32[]{:S(2)}) collective-permute-start(f32[8,160,128]{2,1,0:T(8,128)S(1)} %collective-permute-done.23.rest_6_), channel_id=1, source_target_pairs={{0,1},{1,0},{2,3},{3,2},{4,5},{5,4},{6,7},{7,6},{8,9},{9,8},{10,11... | collective-permute-start | bytes 1966088 | tf_op jit(solution)/shard_map/ppermute | solution.py:134
  82.3 8.3 %collective-permute-start.26 = (f32[4,128,128]{2,1,0:T(8,128)S(1)}, f32[4,128,128]{2,1,0:T(8,128)S(1)}, u32[]{:S(2)}, u32[]{:S(2)}) collective-permute-start(f32[4,128,128]{2,1,0:T(8,128)S(1)} %get-tuple-element.155), channel_id=1, source_target_pairs={{0,4},{4,0},{8,12},{12,8},{16,20},{20,16},{24,28},{28,24},{1,5},{5... | collective-permute-start | bytes 786440 | tf_op jit(solution)/shard_map/ppermute | solution.py:132
  83.3 8.0 %collective-permute-start.27 = (f32[4,128,128]{2,1,0:T(8,128)S(1)}, f32[4,128,128]{2,1,0:T(8,128)S(1)}, u32[]{:S(2)}, u32[]{:S(2)}) collective-permute-start(f32[4,128,128]{2,1,0:T(8,128)S(1)} %get-tuple-element.156), channel_id=1, source_target_pairs={{0,2},{1,3},{2,0},{3,1},{4,6},{5,7},{6,4},{7,5},{8,10},{9,11},{10,... | collective-permute-start | bytes 786440 | tf_op jit(solution)/shard_map/ppermute | solution.py:134
  91.4 12.8 %collective-permute-start.30 = (f32[8,128,128]{2,1,0:T(8,128)S(1)}, f32[8,128,128]{2,1,0:T(8,128)S(1)}, u32[]{:S(2)}, u32[]{:S(2)}) collective-permute-start(f32[8,128,128]{2,1,0:T(8,128)S(1)} %pad_maximum_fusion.5.rest_0_), channel_id=1, source_target_pairs={{0,2},{1,3},{2,0},{3,1},{4,6},{5,7},{6,4},{7,5},{8,10},{9,11},{10,... | collective-permute-start | bytes 1572872 | tf_op jit(solution)/shard_map/ppermute | solution.py:134
  92.0 12.5 %collective-permute-start.31 = (f32[8,128,128]{2,1,0:T(8,128)S(1)}, f32[8,128,128]{2,1,0:T(8,128)S(1)}, u32[]{:S(2)}, u32[]{:S(2)}) collective-permute-start(f32[8,128,128]{2,1,0:T(8,128)S(1)} %pad_maximum_fusion.6.rest_2_), channel_id=1, source_target_pairs={{0,4},{4,0},{8,12},{12,8},{16,20},{20,16},{24,28},{28,24},{1,5},{5... | collective-permute-start | bytes 1572872 | tf_op jit(solution)/shard_map/ppermute | solution.py:132
  93.0 11.4 %collective-permute-start.32 = (f32[8,128,128]{2,1,0:T(8,128)S(1)}, f32[8,128,128]{2,1,0:T(8,128)S(1)}, u32[]{:S(2)}, u32[]{:S(2)}) collective-permute-start(f32[8,128,128]{2,1,0:T(8,128)S(1)} %pad_maximum_fusion.5.rest_0_), channel_id=1, source_target_pairs={{0,1},{1,0},{2,3},{3,2},{4,5},{5,4},{6,7},{7,6},{8,9},{9,8},{10,11... | collective-permute-start | bytes 1572872 | tf_op jit(solution)/shard_map/ppermute | solution.py:134
  93.0 11.4 %collective-permute-start.33 = (f32[8,128,128]{2,1,0:T(8,128)S(1)}, f32[8,128,128]{2,1,0:T(8,128)S(1)}, u32[]{:S(2)}, u32[]{:S(2)}) collective-permute-start(f32[8,128,128]{2,1,0:T(8,128)S(1)} %pad_maximum_fusion.6.rest_2_), channel_id=1, source_target_pairs={{0,1},{1,0},{2,3},{3,2},{4,5},{5,4},{6,7},{7,6},{8,9},{9,8},{10,11... | collective-permute-start | bytes 1572872 | tf_op jit(solution)/shard_map/ppermute | solution.py:134
  121.5 9.7 %collective-permute-start.36 = (f32[16,256,128]{2,1,0:T(8,128)S(1)}, f32[16,256,128]{2,1,0:T(8,128)S(1)}, u32[]{:S(2)}, u32[]{:S(2)}) collective-permute-start(f32[16,256,128]{2,1,0:T(8,128)S(1)} %shard_map.282), channel_id=1, source_target_pairs={{0,1},{1,0},{2,3},{3,2},{4,5},{5,4},{6,7},{7,6},{8,9},{9,8},{10,11... | collective-permute-start | bytes 6291464 | tf_op jit(solution)/shard_map/ppermute | solution.py:134
  124.8 6.4 %collective-permute-start.37 = (f32[16,256,128]{2,1,0:T(8,128)S(1)}, f32[16,256,128]{2,1,0:T(8,128)S(1)}, u32[]{:S(2)}, u32[]{:S(2)}) collective-permute-start(f32[16,256,128]{2,1,0:T(8,128)S(1)} %shard_map.283), channel_id=1, source_target_pairs={{0,1},{1,0},{2,3},{3,2},{4,5},{5,4},{6,7},{7,6},{8,9},{9,8},{10,11... | collective-permute-start | bytes 6291464 | tf_op jit(solution)/shard_map/ppermute | solution.py:134
  131.3 33.0 %collective-permute-start.38 = (f32[8,256,128]{2,1,0:T(8,128)S(1)}, f32[8,256,128]{2,1,0:T(8,128)S(1)}, u32[]{:S(2)}, u32[]{:S(2)}) collective-permute-start(f32[8,256,128]{2,1,0:T(8,128)S(1)} %slice_add_fusion), channel_id=1, source_target_pairs={{0,8},{4,12},{8,0},{12,4},{16,24},{20,28},{24,16},{28,20},{1,9},{5... | collective-permute-start | bytes 3145736 | tf_op jit(solution)/shard_map/ppermute | solution.py:132
  132.6 31.7 %collective-permute-start.39 = (f32[4,256,128]{2,1,0:T(8,128)S(1)}, f32[4,256,128]{2,1,0:T(8,128)S(1)}, u32[]{:S(2)}, u32[]{:S(2)}) collective-permute-start(f32[4,256,128]{2,1,0:T(8,128)S(1)} %get-tuple-element.246), channel_id=1, source_target_pairs={{0,4},{4,0},{8,12},{12,8},{16,20},{20,16},{24,28},{28,24},{1,5},{5... | collective-permute-start | bytes 1572872 | tf_op jit(solution)/shard_map/ppermute | solution.py:132
  133.7 30.6 %collective-permute-start.40 = (f32[4,256,128]{2,1,0:T(8,128)S(1)}, f32[4,256,128]{2,1,0:T(8,128)S(1)}, u32[]{:S(2)}, u32[]{:S(2)}) collective-permute-start(f32[4,256,128]{2,1,0:T(8,128)S(1)} %get-tuple-element.245), channel_id=1, source_target_pairs={{0,2},{1,3},{2,0},{3,1},{4,6},{5,7},{6,4},{7,5},{8,10},{9,11},{10,... | collective-permute-start | bytes 1572872 | tf_op jit(solution)/shard_map/ppermute | solution.py:134
  135.2 29.1 %collective-permute-start.41 = (f32[4,256,128]{2,1,0:T(8,128)S(1)}, f32[4,256,128]{2,1,0:T(8,128)S(1)}, u32[]{:S(2)}, u32[]{:S(2)}) collective-permute-start(f32[4,256,128]{2,1,0:T(8,128)S(1)} %get-tuple-element.244), channel_id=1, source_target_pairs={{0,6},{1,7},{2,4},{3,5},{4,2},{5,3},{6,0},{7,1},{8,14},{9,15},{10,... | collective-permute-start | bytes 1572872 | tf_op jit(solution)/shard_map/ppermute | solution.py:137
  164.3 5.7 %collective-permute-start.42 = (f32[2,2,16,512]{3,2,1,0:T(8,128)S(1)}, f32[2,2,16,512]{3,2,1,0:T(8,128)S(1)}, u32[]{:S(2)}, u32[]{:S(2)}) collective-permute-start(f32[2,2,16,512]{3,2,1,0:T(8,128)S(1)} %get-tuple-element.208), channel_id=1, source_target_pairs={{0,1},{1,0},{2,3},{3,2},{4,5},{5,4},{6,7},{7,6},{8,9},{9,8},{10,11... | collective-permute-start | bytes 393224 | tf_op jit(solution)/shard_map/ppermute | solution.py:1007
  174.9 22.4 %collective-permute-start.45 = (f32[16,192,128]{2,1,0:T(8,128)}, f32[16,192,128]{2,1,0:T(8,128)}, u32[]{:S(2)}, u32[]{:S(2)}) collective-permute-start(f32[16,192,128]{2,1,0:T(8,128)} %get-tuple-element.217), channel_id=1, source_target_pairs={{0,1},{1,0},{2,3},{3,2},{4,5},{5,4},{6,7},{7,6},{8,9},{9,8},{10,11... | collective-permute-start | bytes 4718600 | tf_op jit(solution)/shard_map/ppermute | solution.py:134
  175.1 6.2 %collective-permute-start.46 = (f32[16,64,128]{2,1,0:T(8,128)S(1)}, f32[16,64,128]{2,1,0:T(8,128)S(1)}, u32[]{:S(2)}, u32[]{:S(2)}) collective-permute-start(f32[16,64,128]{2,1,0:T(8,128)S(1)} %get-tuple-element.222), channel_id=1, source_target_pairs={{0,1},{1,0},{2,3},{3,2},{4,5},{5,4},{6,7},{7,6},{8,9},{9,8},{10,11... | collective-permute-start | bytes 1572872 | tf_op jit(solution)/shard_map/ppermute | solution.py:134
  176.5 28.9 %collective-permute-start.54 = (f32[4,256,128]{2,1,0:T(8,128)}, f32[4,256,128]{2,1,0:T(8,128)}, u32[]{:S(2)}, u32[]{:S(2)}) collective-permute-start(f32[4,256,128]{2,1,0:T(8,128)} %fusion), channel_id=1, source_target_pairs={{0,4},{4,0},{8,12},{12,8},{16,20},{20,16},{24,28},{28,24},{1,5},{5... | collective-permute-start | bytes 1572872 | tf_op jit(solution)/shard_map/ppermute | solution.py:132
  182.1 12.3 %collective-permute-start.47 = (f32[4,64,128]{2,1,0:T(8,128)}, f32[4,64,128]{2,1,0:T(8,128)}, u32[]{:S(2)}, u32[]{:S(2)}) collective-permute-start(f32[4,64,128]{2,1,0:T(8,128)} %get-tuple-element.256), channel_id=1, source_target_pairs={{0,4},{4,0},{8,12},{12,8},{16,20},{20,16},{24,28},{28,24},{1,5},{5... | collective-permute-start | bytes 393224 | tf_op jit(solution)/shard_map/ppermute | solution.py:132
  183.1 11.3 %collective-permute-start.48 = (f32[4,64,128]{2,1,0:T(8,128)S(1)}, f32[4,64,128]{2,1,0:T(8,128)}, u32[]{:S(2)}, u32[]{:S(2)}) collective-permute-start(f32[4,64,128]{2,1,0:T(8,128)S(1)} %get-tuple-element.255), channel_id=1, source_target_pairs={{0,2},{1,3},{2,0},{3,1},{4,6},{5,7},{6,4},{7,5},{8,10},{9,11},{10,... | collective-permute-start | bytes 393224 | tf_op jit(solution)/shard_map/ppermute | solution.py:134
  184.4 12.9 %collective-permute-start.49 = (f32[4,64,128]{2,1,0:T(8,128)S(1)}, f32[4,64,128]{2,1,0:T(8,128)}, u32[]{:S(2)}, u32[]{:S(2)}) collective-permute-start(f32[4,64,128]{2,1,0:T(8,128)S(1)} %get-tuple-element.254), channel_id=1, source_target_pairs={{0,6},{1,7},{2,4},{3,5},{4,2},{5,3},{6,0},{7,1},{8,14},{9,15},{10,... | collective-permute-start | bytes 393224 | tf_op jit(solution)/shard_map/ppermute | solution.py:137
  199.6 19.3 %collective-permute-start.51 = (f32[4,208,128]{2,1,0:T(8,128)S(1)}, f32[4,208,128]{2,1,0:T(8,128)S(1)}, u32[]{:S(2)}, u32[]{:S(2)}) collective-permute-start(f32[4,208,128]{2,1,0:T(8,128)S(1)} %get-tuple-element.262), channel_id=1, source_target_pairs={{0,2},{1,3},{2,0},{3,1},{4,6},{5,7},{6,4},{7,5},{8,10},{9,11},{10,... | collective-permute-start | bytes 1277960 | tf_op jit(solution)/shard_map/ppermute | solution.py:134
  200.3 18.7 %collective-permute-start.50 = (f32[4,208,128]{2,1,0:T(8,128)S(1)}, f32[4,208,128]{2,1,0:T(8,128)S(1)}, u32[]{:S(2)}, u32[]{:S(2)}) collective-permute-start(f32[4,208,128]{2,1,0:T(8,128)S(1)} %get-tuple-element.263), channel_id=1, source_target_pairs={{0,4},{4,0},{8,12},{12,8},{16,20},{20,16},{24,28},{28,24},{1,5},{5... | collective-permute-start | bytes 1277960 | tf_op jit(solution)/shard_map/ppermute | solution.py:132
  201.3 19.9 %collective-permute-start.52 = (f32[4,208,128]{2,1,0:T(8,128)S(1)}, f32[4,208,128]{2,1,0:T(8,128)S(1)}, u32[]{:S(2)}, u32[]{:S(2)}) collective-permute-start(f32[4,208,128]{2,1,0:T(8,128)S(1)} %get-tuple-element.261), channel_id=1, source_target_pairs={{0,6},{1,7},{2,4},{3,5},{4,2},{5,3},{6,0},{7,1},{8,14},{9,15},{10,... | collective-permute-start | bytes 1277960 | tf_op jit(solution)/shard_map/ppermute | solution.py:137
  204.4 14.6 %collective-permute-start.53 = (f32[2,320,128]{2,1,0:T(8,128)S(1)}, f32[2,320,128]{2,1,0:T(8,128)S(1)}, u32[]{:S(2)}, u32[]{:S(2)}) collective-permute-start(f32[2,320,128]{2,1,0:T(8,128)S(1)} %fusion.4), channel_id=1, source_target_pairs={{0,8},{4,12},{8,0},{12,4},{16,24},{20,28},{24,16},{28,20},{1,9},{5... | collective-permute-start | bytes 983048 | tf_op jit(solution)/shard_map/ppermute | solution.py:132
  206.6 12.3 %collective-permute-start.55 = (f32[2,256,128]{2,1,0:T(8,128)S(1)}, f32[2,256,128]{2,1,0:T(8,128)S(1)}, u32[]{:S(2)}, u32[]{:S(2)}) collective-permute-start(f32[2,256,128]{2,1,0:T(8,128)S(1)} %fusion.6), channel_id=1, source_target_pairs={{0,16},{4,20},{8,24},{12,28},{16,0},{20,4},{24,8},{28,12},{1,17},{... | collective-permute-start | bytes 786440 | tf_op jit(solution)/shard_map/ppermute | solution.py:132
  221.3 19.3 %collective-permute-start.58 = (f32[1,208,128]{2,1,0:T(8,128)S(1)}, f32[1,208,128]{2,1,0:T(8,128)S(1)}, u32[]{:S(2)}, u32[]{:S(2)}) collective-permute-start(f32[1,208,128]{2,1,0:T(8,128)S(1)} %get-tuple-element.253), channel_id=1, source_target_pairs={{0,24},{4,28},{8,16},{12,20},{16,8},{20,12},{24,0},{28,4},{1,25},{... | collective-permute-start | bytes 319496 | tf_op jit(solution)/shard_map/ppermute | solution.py:132
  224.4 16.2 %collective-permute-start.57 = (f32[1,208,128]{2,1,0:T(8,128)S(1)}, f32[1,208,128]{2,1,0:T(8,128)S(1)}, u32[]{:S(2)}, u32[]{:S(2)}) collective-permute-start(f32[1,208,128]{2,1,0:T(8,128)S(1)} %get-tuple-element.251), channel_id=1, source_target_pairs={{0,16},{4,20},{8,24},{12,28},{16,0},{20,4},{24,8},{28,12},{1,17},{... | collective-permute-start | bytes 319496 | tf_op jit(solution)/shard_map/ppermute | solution.py:132
  224.4 16.2 %collective-permute-start.56 = (f32[1,208,128]{2,1,0:T(8,128)S(1)}, f32[1,208,128]{2,1,0:T(8,128)S(1)}, u32[]{:S(2)}, u32[]{:S(2)}) collective-permute-start(f32[1,208,128]{2,1,0:T(8,128)S(1)} %get-tuple-element.252), channel_id=1, source_target_pairs={{0,8},{4,12},{8,0},{12,4},{16,24},{20,28},{24,16},{28,20},{1,9},{5... | collective-permute-start | bytes 319496 | tf_op jit(solution)/shard_map/ppermute | solution.py:132
  227.3 12.0 %collective-permute-start.60 = (f32[1,320,128]{2,1,0:T(8,128)S(1)}, f32[1,320,128]{2,1,0:T(8,128)S(1)}, u32[]{:S(2)}, u32[]{:S(2)}) collective-permute-start(f32[1,320,128]{2,1,0:T(8,128)S(1)} %fusion.12), channel_id=1, source_target_pairs={{0,16},{4,20},{8,24},{12,28},{16,0},{20,4},{24,8},{28,12},{1,17},{... | collective-permute-start | bytes 491528 | tf_op jit(solution)/shard_map/ppermute | solution.py:132
  (60 other events, 905.3 us)
